TPU v7x, 128 devices: a whole 4x4x4 slice. The times are simulated.
128 devices in a mesh: owner: 32 (over z, y, core), sub: 4 (over x).
Axes of the slice: x: 4, y: 4, z: 4, core: 2. Of those that a mesh axis runs over, the one named last changes fastest.
Arguments:
- velocity: float32 [6, 65536], P(None, 'owner'), may hold values from -6 to 6
- properties: float32 [4, 65536], P(None, 'owner'), may hold values from 0.3 to 3
- first_body: int32 [4194304], P(('owner', 'sub')), may hold values from 0 to 65535, as said below
- second_body: int32 [4194304], P(('owner', 'sub')), may hold values from 0 to 65535, as said below
- geometry: float32 [9, 4194304], P(None, ('owner', 'sub')), may hold values from -2 to 2, as said below
- target_speed: float32 [4194304], P(('owner', 'sub')), may hold values from -1 to 2
- warm_impulse: float32 [4194304], P(('owner', 'sub')), may hold values from 0 to 0.5
- live_pairs: int32 [32768], P(('owner', 'sub')), may hold values from 0 to 128, as said below
Outputs:
- velocity_out: float32 [6, 65536], P(None, 'owner')
- impulse_out: float32 [4194304], P(('owner', 'sub'))
Inputs may be any that keep to these rules, and one draw needn't show every extreme that they name: Pair slots are ordered by device of owner+sub, then by partner owner, then by 8 blocks of 128 slots; a slot on a device of owner o with partner owner q has first_body in [o * 2048, (o+1) * 2048) and second_body in [q * 2048, (q+1) * 2048). `second_body`: see first_body. `live_pairs`: on every device the first block toward its own owner is full; live counts differ strongly between devices and between partner owners. `geometry`: rows 0 to 2 of every column have unit length.
All inputs are finite; a program needn't handle non-finite values.
Results may differ from a plain program's by a relative error of at most 0.0001.
Values sent between devices are 32-bit elements; how exact they have to be, the bound alone decides.
No kernel may reach another device: no remote copies, remote signals or barrier semaphores. Data moves between devices by JAX's collectives and lax.ppermute only.
A program may use at most 128 MiB of HBM per device.

v0:
```python
import math

import jax
import jax.numpy as jnp
from jax import lax
from jax.sharding import PartitionSpec as P

ITERS = 4


relax = 0.1


def from_everyone(shard, axis):
    copies = jnp.broadcast_to(shard, (lax.axis_size(axis), *shard.shape))
    return lax.all_to_all(copies, axis, split_axis=0, concat_axis=0, tiled=True)


def of_everyone(shard, axis):
    return from_everyone(shard, axis).sum(axis=0)


def cross_rows(left, right):
    return jnp.stack(
        [
            left[1] * right[2] - left[2] * right[1],
            left[2] * right[0] - left[0] * right[2],
            left[0] * right[1] - left[1] * right[0],
        ]
    )


def index_tables(index, length):
    width = math.gcd(length, 128)
    height = length // width
    lows = (
        (index % width)[:, :, None] == jnp.arange(width, dtype=jnp.int32)[None, None, :]
    ).astype(jnp.float32)
    highs = (
        (index // width)[:, None, :] == jnp.arange(height, dtype=jnp.int32)[None, :, None]
    ).astype(jnp.float32)
    return (lows, highs)


def pick_columns(table, tables):
    lows, highs = tables
    rows, groups, length = table.shape
    width = lows.shape[2]
    height = highs.shape[1]
    parts = jnp.einsum(
        "cqhw,qsw->cqhs",
        table.reshape(rows, groups, height, width),
        lows,
        precision=lax.Precision.HIGHEST,
    )
    return jnp.sum(parts * highs[None], axis=2)


def place_columns(values, tables):
    lows, highs = tables
    rows, groups, count = values.shape
    width = lows.shape[2]
    height = highs.shape[1]
    weighted = values[:, :, None, :] * highs[None]
    placed = jnp.einsum("cqhs,qsw->cqhw", weighted, lows, precision=lax.Precision.HIGHEST)
    return placed.reshape(rows, groups, height * width)


def on_device(
    velocity, properties, first_body, second_body, geometry, target_speed, warm_impulse, live_pairs
):
    owned = velocity.shape[1]
    groups = lax.axis_size("owner")
    slots_count = first_body.shape[0]
    block_len = slots_count // live_pairs.shape[0]
    local_first = first_body - lax.axis_index("owner") * owned
    first_tables = index_tables(local_first.reshape(1, -1), owned)
    slots = jnp.arange(slots_count, dtype=jnp.int32)
    live = slots % block_len < jnp.repeat(live_pairs, block_len, total_repeat_length=slots_count)
    normal = geometry[0:3]
    arm_first = geometry[3:6]
    arm_second = geometry[6:9]
    cross_first = cross_rows(arm_first, normal)
    cross_second = cross_rows(arm_second, normal)
    props_first = pick_columns(properties[:, None, :], first_tables)[:, 0]
    wanted = lax.all_to_all(
        (second_body % owned).reshape(groups, -1), "owner", split_axis=0, concat_axis=0, tiled=True
    )
    wanted_tables = index_tables(wanted.reshape(1, -1), owned)
    asked_props = pick_columns(properties[:, None, :], wanted_tables)[:, 0].reshape(4, groups, -1)
    props_second = lax.all_to_all(
        asked_props, "owner", split_axis=1, concat_axis=1, tiled=True
    ).reshape(4, slots_count)
    mass_sum = (
        props_first[0]
        + props_second[0]
        + jnp.sum(cross_first * cross_first * props_first[1:4], 0)
        + jnp.sum(cross_second * cross_second * props_second[1:4], 0)
    )
    speeds = velocity
    impulse = warm_impulse
    for iteration in range(ITERS):
        vel_first = pick_columns(speeds[:, None, :], first_tables)[:, 0]
        asked_speeds = pick_columns(speeds[:, None, :], wanted_tables)[:, 0].reshape(6, groups, -1)
        vel_second = lax.all_to_all(
            asked_speeds, "owner", split_axis=1, concat_axis=1, tiled=True
        ).reshape(6, slots_count)
        relative = (
            vel_first[0:3]
            + cross_rows(vel_first[3:6], arm_first)
            - vel_second[0:3]
            - cross_rows(vel_second[3:6], arm_second)
        )
        normal_speed = jnp.sum(normal * relative, 0)
        change = relax * (target_speed - normal_speed) / mass_sum
        fresh = jnp.where(live, jnp.maximum(impulse + change, 0.0), impulse)
        applied = fresh - impulse
        impulse = fresh
        delta_first = jnp.concatenate(
            [props_first[0] * applied * normal, props_first[1:4] * (applied * cross_first)]
        )
        delta_second = -jnp.concatenate(
            [props_second[0] * applied * normal, props_second[1:4] * (applied * cross_second)]
        )
        own_terms = place_columns(delta_first[:, None, :], first_tables)[:, 0]
        returned = lax.all_to_all(
            delta_second.reshape(6, groups, -1), "owner", split_axis=1, concat_axis=1, tiled=True
        )
        arrived = place_columns(returned.reshape(6, 1, -1), wanted_tables)[:, 0]
        summed = of_everyone(own_terms + arrived, "sub")
        speeds = speeds + summed
    return (speeds, impulse)


def solution(mesh):
    return jax.shard_map(
        on_device,
        mesh=mesh,
        in_specs=(
            P(None, "owner"),
            P(None, "owner"),
            P(("owner", "sub")),
            P(("owner", "sub")),
            P(None, ("owner", "sub")),
            P(("owner", "sub")),
            P(("owner", "sub")),
            P(("owner", "sub")),
        ),
        out_specs=(P(None, "owner"), P(("owner", "sub"))),
        check_vma=False,
    )
```

profile of v0, /device:TPU:1, one launch (start us, length us, event | category | flops | bytes accessed | tf_op | source)
XLA Modules:
  0.0 953.5 jit_solution(6998134265429559747)
XLA Ops:
  2.3 9.6 %all-to-all-start = ((s32[32,1,1024]{2,1,0:T(1,128)}), s32[32,1,1024]{2,1,0:T(1,128)S(1)}, u32[]{:S(2)}, u32[]{:S(2)}) async-start(s32[32,1,1024]{2,1,0:T(1,128)} %bitcast.19), calls=%async_computation | async-start | bytes 262144 | tf_op jit(solution)/shard_map/all_to_all | solution.py:86
  13.1 6.8 multiply_subtract_fusion.23
  19.9 15.6 %fusion.82 = f32[6,32768]{1,0:T(8,128)S(1)} fusion(f32[16,32768]{1,0:T(8,128)S(1)} %fusion.112, s32[32768]{0:T(1024)S(1)} %get-tuple-element.86, f32[1,6,16,128]{3,1,2,0:T(8,128)} %bitcast.364), kind=kOutput, calls=%fused_computation.80 | convolution fusion | flops 4842127360 | bytes 3063808 | tf_op jit(solution)/shard_map/cqhw,qsw->cqhs/dot_general | solution.py:50
  36.5 4.0 multiply_subtract_fusion.29
  44.9 14.7 %fusion.106 = f32[4,32768]{1,0:T(4,128)S(1)} fusion(f32[16,32768]{1,0:T(8,128)S(1)} %fusion.112, s32[32768]{0:T(1024)S(1)} %get-tuple-element.86, f32[1,4,16,128]{3,1,2,0:T(4,128)S(1)} %bitcast.369), kind=kOutput, calls=%fused_computation.88 | convolution fusion | flops 3229483008 | bytes 2785280 | tf_op jit(solution)/shard_map/cqhw,qsw->cqhs/dot_general | solution.py:50
  61.4 15.5 %fusion.109 = f32[4,32768]{1,0:T(4,128)} fusion(f32[16,32768]{1,0:T(8,128)S(1)} %fusion.113, s32[32768]{0:T(1024)S(1)} %get-tuple-element.83, f32[1,4,16,128]{3,1,2,0:T(4,128)S(1)} %bitcast.370), kind=kOutput, calls=%fused_computation.89 | convolution fusion | flops 3229483008 | bytes 2785280 | tf_op jit(solution)/shard_map/cqhw,qsw->cqhs/dot_general | solution.py:50
  76.9 7.4 all-to-all-start.2
  84.3 17.3 %fusion.85 = f32[6,32768]{1,0:T(8,128)} fusion(f32[16,32768]{1,0:T(8,128)} %copy-done.2, s32[32768]{0:T(1024)} %copy-done.29, f32[1,6,16,128]{3,1,2,0:T(8,128)} %bitcast.365), kind=kOutput, calls=%fused_computation.81 | convolution fusion | flops 4842127360 | bytes 3063808 | tf_op jit(solution)/shard_map/cqhw,qsw->cqhs/dot_general | solution.py:50
  101.6 7.8 all-to-all-start.1
  110.2 344.7 %gather_fusion = s32[32768]{0:T(1024)} fusion(s32[256]{0:T(256)S(1)} %copy-done, s32[32768]{0:T(1024)} %broadcast_clamp_fusion), kind=kCustom, calls=%fused_computation | custom fusion | bytes 393216 | tf_op jit(solution)/shard_map/jit(_take)/gather | solution.py:79
  455.7 2.6 fusion.209
  458.2 5.4 multiply_subtract_fusion.22
  467.4 3.7 fusion.169
  480.5 5.6 fusion.240
  487.8 7.9 all-to-all-start.3
  495.8 13.8 %fusion.17 = f32[128,6,16]{0,2,1:T(8,128)} fusion(s32[32768]{0:T(1024)} %copy-done.31, f32[6,16,32768]{2,1,0:T(8,128)} %fusion.240), kind=kOutput, calls=%fused_computation.30 | convolution fusion | flops 4836032512 | bytes 12763136 | tf_op jit(solution)/shard_map/cqhs,qsw->cqhw/dot_general | solution.py:65
  509.6 2.9 all-to-all-done.3
  512.5 7.5 fusion.242
  520.0 13.9 %fusion.119 = f32[1,6,16,128]{3,2,1,0:T(8,128)} fusion(f32[128,6,16]{0,2,1:T(8,128)} %fusion.17, s32[32768]{0:T(1024)} %copy-done.29, f32[6,16,32768]{2,1,0:T(8,128)} %fusion.242), kind=kOutput, calls=%fused_computation.95 | convolution fusion | flops 4836044800 | bytes 12812288 | tf_op jit(solution)/shard_map/cqhs,qsw->cqhw/dot_general | solution.py:65
  534.7 9.7 %all_to_all.74 = f32[4,6,2048]{2,1,0:T(8,128)} all-to-all(f32[4,6,2048]{2,1,0:T(8,128)S(1)} %broadcast_in_dim.18), channel_id=1, replica_groups=mesh['owner'=32,'sub'=4] {'sub'}, dimensions={0} | all-to-all | bytes 393216 | tf_op jit(solution)/shard_map/all_to_all | solution.py:16
  546.9 17.1 %fusion.91 = f32[6,32768]{1,0:T(8,128)} fusion(f32[16,32768]{1,0:T(8,128)} %copy-done.2, s32[32768]{0:T(1024)} %copy-done.29, f32[1,6,16,128]{3,1,2,0:T(8,128)S(1)} %bitcast.358), kind=kOutput, calls=%fused_computation.83 | convolution fusion | flops 4842127360 | bytes 3063808 | tf_op jit(solution)/shard_map/cqhw,qsw->cqhs/dot_general | solution.py:50
  564.0 15.6 %fusion.88 = f32[6,32768]{1,0:T(8,128)} fusion(f32[16,32768]{1,0:T(8,128)S(1)} %fusion.112, s32[32768]{0:T(1024)S(1)} %copy-done.32, f32[1,6,16,128]{3,1,2,0:T(8,128)S(1)} %bitcast.359), kind=kOutput, calls=%fused_computation.82 | convolution fusion | flops 4842127360 | bytes 3063808 | tf_op jit(solution)/shard_map/cqhw,qsw->cqhs/dot_general | solution.py:50
  579.6 6.1 all-to-all-start.5
  585.8 4.9 multiply_subtract_fusion.17
  590.6 12.5 %all-to-all-done.5 = f32[6,32,1024]{2,0,1:T(8,128)} async-done(((f32[6,32,1024]{2,0,1:T(8,128)}), f32[6,32,1024]{2,0,1:T(8,128)}, u32[]{:S(2)}, u32[]{:S(2)}) %all-to-all-start.5) | async-done | bytes 786464 | tf_op jit(solution)/shard_map/all_to_all | solution.py:105
  603.1 2.5 fusion.208
  609.2 2.8 fusion.165
  621.3 5.6 fusion.238
  628.6 5.0 all-to-all-start.6
  633.7 13.8 %fusion.15 = f32[128,6,16]{0,2,1:T(8,128)} fusion(s32[32768]{0:T(1024)} %copy-done.31, f32[6,16,32768]{2,1,0:T(8,128)} %fusion.238), kind=kOutput, calls=%fused_computation.29 | convolution fusion | flops 4836032512 | bytes 12763136 | tf_op jit(solution)/shard_map/cqhs,qsw->cqhw/dot_general | solution.py:65
  647.5 3.1 all-to-all-done.6
  650.6 7.5 fusion.244
  658.1 13.9 %fusion.129 = f32[1,6,16,128]{3,2,1,0:T(8,128)} fusion(f32[128,6,16]{0,2,1:T(8,128)} %fusion.15, s32[32768]{0:T(1024)} %copy-done.29, f32[6,16,32768]{2,1,0:T(8,128)} %fusion.244), kind=kOutput, calls=%fused_computation.97 | convolution fusion | flops 4836044800 | bytes 12812288 | tf_op jit(solution)/shard_map/cqhs,qsw->cqhw/dot_general | solution.py:65
  672.9 9.5 all_to_all.75
  684.9 17.1 %fusion.97 = f32[6,32768]{1,0:T(8,128)} fusion(f32[16,32768]{1,0:T(8,128)} %copy-done.2, s32[32768]{0:T(1024)} %copy-done.29, f32[1,6,16,128]{3,1,2,0:T(8,128)S(1)} %bitcast.356), kind=kOutput, calls=%fused_computation.85 | convolution fusion | flops 4842127360 | bytes 3063808 | tf_op jit(solution)/shard_map/cqhw,qsw->cqhs/dot_general | solution.py:50
  701.9 15.6 %fusion.94 = f32[6,32768]{1,0:T(8,128)} fusion(f32[16,32768]{1,0:T(8,128)S(1)} %fusion.112, s32[32768]{0:T(1024)S(1)} %copy-done.33, f32[1,6,16,128]{3,1,2,0:T(8,128)S(1)} %bitcast.357), kind=kOutput, calls=%fused_computation.84 | convolution fusion | flops 4842127360 | bytes 3063808 | tf_op jit(solution)/shard_map/cqhw,qsw->cqhs/dot_general | solution.py:50
  717.6 5.5 all-to-all-start.8
  723.1 4.9 multiply_subtract_fusion.11
  727.9 12.5 %all-to-all-done.8 = f32[6,32,1024]{2,0,1:T(8,128)} async-done(((f32[6,32,1024]{2,0,1:T(8,128)}), f32[6,32,1024]{2,0,1:T(8,128)}, u32[]{:S(2)}, u32[]{:S(2)}) %all-to-all-start.8) | async-done | bytes 786464 | tf_op jit(solution)/shard_map/all_to_all | solution.py:105
  740.4 2.5 fusion.207
  746.5 2.8 fusion.161
  751.2 2.3 multiply_multiply_fusion.3
  758.6 5.6 fusion.236
  765.9 5.0 all-to-all-start.9
  771.0 13.8 %fusion.13 = f32[128,6,16]{0,2,1:T(8,128)} fusion(s32[32768]{0:T(1024)} %copy-done.31, f32[6,16,32768]{2,1,0:T(8,128)} %fusion.236), kind=kOutput, calls=%fused_computation.28 | convolution fusion | flops 4836032512 | bytes 12763136 | tf_op jit(solution)/shard_map/cqhs,qsw->cqhw/dot_general | solution.py:65
  784.8 3.1 all-to-all-done.9
  787.9 7.5 fusion.246
  795.4 13.9 %fusion.139 = f32[1,6,16,128]{3,2,1,0:T(8,128)} fusion(f32[128,6,16]{0,2,1:T(8,128)} %fusion.13, s32[32768]{0:T(1024)} %copy-done.29, f32[6,16,32768]{2,1,0:T(8,128)} %fusion.246), kind=kOutput, calls=%fused_computation.99 | convolution fusion | flops 4836044800 | bytes 12812288 | tf_op jit(solution)/shard_map/cqhs,qsw->cqhw/dot_general | solution.py:65
  810.2 9.5 all_to_all.76
  822.2 17.1 %fusion.103 = f32[6,32768]{1,0:T(8,128)} fusion(f32[16,32768]{1,0:T(8,128)} %copy-done.2, s32[32768]{0:T(1024)} %copy-done.29, f32[1,6,16,128]{3,1,2,0:T(8,128)S(1)} %bitcast.354), kind=kOutput, calls=%fused_computation.87 | convolution fusion | flops 4842127360 | bytes 3063808 | tf_op jit(solution)/shard_map/cqhw,qsw->cqhs/dot_general | solution.py:50
  839.2 15.6 %fusion.100 = f32[6,32768]{1,0:T(8,128)} fusion(f32[16,32768]{1,0:T(8,128)S(1)} %fusion.112, s32[32768]{0:T(1024)S(1)} %copy-done.34, f32[1,6,16,128]{3,1,2,0:T(8,128)S(1)} %bitcast.355), kind=kOutput, calls=%fused_computation.86 | convolution fusion | flops 4842127360 | bytes 3063808 | tf_op jit(solution)/shard_map/cqhw,qsw->cqhs/dot_general | solution.py:50
  854.9 5.5 all-to-all-start.11
  860.3 4.9 multiply_subtract_fusion.5
  865.2 12.5 %all-to-all-done.11 = f32[6,32,1024]{2,0,1:T(8,128)} async-done(((f32[6,32,1024]{2,0,1:T(8,128)}), f32[6,32,1024]{2,0,1:T(8,128)}, u32[]{:S(2)}, u32[]{:S(2)}) %all-to-all-start.11) | async-done | bytes 786464 | tf_op jit(solution)/shard_map/all_to_all | solution.py:105
  877.7 2.5 fusion.206
  883.8 2.8 fusion.157
  888.5 2.3 multiply_multiply_fusion.1
  894.6 5.6 fusion.234
  903.0 4.3 all-to-all-start.12
  907.4 13.2 %fusion.11 = f32[128,6,16]{0,2,1:T(8,128)S(1)} fusion(s32[32768]{0:T(1024)S(1)} %copy-done.35, f32[6,16,32768]{2,1,0:T(8,128)} %fusion.234), kind=kOutput, calls=%fused_computation.27 | convolution fusion | flops 4836032512 | bytes 12763136 | tf_op jit(solution)/shard_map/cqhs,qsw->cqhw/dot_general | solution.py:65
  920.6 3.9 all-to-all-done.12
  924.4 5.6 fusion.248
  930.1 13.4 %fusion.149 = f32[1,6,16,128]{3,2,1,0:T(8,128)S(1)} fusion(f32[128,6,16]{0,2,1:T(8,128)S(1)} %fusion.11, s32[32768]{0:T(1024)S(1)} %copy-done.30, f32[6,16,32768]{2,1,0:T(8,128)} %fusion.248), kind=kOutput, calls=%fused_computation.101 | convolution fusion | flops 4836044800 | bytes 12812288 | tf_op jit(solution)/shard_map/cqhs,qsw->cqhw/dot_general | solution.py:65
  943.6 8.8 all_to_all.77
  (160 shorter events, 75.9 us)
Async XLA Ops:
  0.6 109.5 %copy-start = (s32[256]{0:T(256)S(1)}, s32[256]{0:T(256)}, u32[]{:S(2)}) copy-start(s32[256]{0:T(256)} %param.17) | copy-start | bytes 3076
  2.3 57.5 %all-to-all-start = ((s32[32,1,1024]{2,1,0:T(1,128)}), s32[32,1,1024]{2,1,0:T(1,128)S(1)}, u32[]{:S(2)}, u32[]{:S(2)}) async-start(s32[32,1,1024]{2,1,0:T(1,128)} %bitcast.19), calls=%async_computation | async-start | bytes 262144 | tf_op jit(solution)/shard_map/all_to_all | solution.py:86
  12.9 32.0 %copy-start.31 = (s32[32768]{0:T(1024)}, s32[32768]{0:T(1024)S(1)}, u32[]{:S(2)}) copy-start(s32[32768]{0:T(1024)S(1)} %get-tuple-element.86) | copy-start | bytes 393220
  19.9 20.6 %copy-start.36 = (s32[2,128]{1,0:T(2,128)S(1)}, s32[2,128]{1,0:T(2,128)}, u32[]{:S(2)}) copy-start(s32[2,128]{1,0:T(2,128)} %constant.141.clone.1) | copy-start | bytes 3076
  19.9 25.0 %copy-start.37 = (f32[4,2048]{1,0:T(4,128)S(1)}, f32[4,2048]{1,0:T(4,128)}, u32[]{:S(2)}) copy-start(f32[4,2048]{1,0:T(4,128)} %param.11) | copy-start | bytes 98308
  35.5 1.0 copy-start.20
  44.0 0.9 copy-start.18
  44.1 0.8 copy-start.19
  59.9 17.0 %copy-start.29 = (s32[32768]{0:T(1024)}, s32[32768]{0:T(1024)S(1)}, u32[]{:S(2)}) copy-start(s32[32768]{0:T(1024)S(1)} %get-tuple-element.83) | copy-start | bytes 393220
  60.1 1.3 copy-start.2
  76.9 24.7 %all-to-all-start.2 = ((f32[4,32,1024]{2,0,1:T(4,128)}), f32[4,32,1024]{2,0,1:T(4,128)S(1)}, u32[]{:S(2)}, u32[]{:S(2)}) async-start(f32[4,32,1024]{2,0,1:T(4,128)} %bitcast.339), calls=%async_computation.2 | async-start | bytes 1048576 | tf_op jit(solution)/shard_map/all_to_all | solution.py:91
  84.3 25.2 %copy-start.21 = (s32[32768,1]{0,1:T(1,128)S(1)}, s32[32768,1]{0,1:T(1,128)}, u32[]{:S(2)}) copy-start(s32[32768,1]{0,1:T(1,128)} %compare_select_fusion) | copy-start | bytes 393220
  101.6 354.0 %all-to-all-start.1 = ((f32[6,32,1024]{2,0,1:T(8,128)}), f32[6,32,1024]{2,0,1:T(8,128)}, u32[]{:S(2)}, u32[]{:S(2)}) async-start(f32[6,32,1024]{2,0,1:T(8,128)} %bitcast.332), calls=%async_computation.1 | async-start | bytes 2097152 | tf_op jit(solution)/shard_map/all_to_all | solution.py:105
  463.6 0.7 copy-start.4
  473.1 2.3 copy-start.14
  477.7 8.4 copy-start.5
  477.7 8.4 copy-start.8
  477.7 8.4 copy-start.11
  477.7 8.4 copy-start.22
  487.8 24.7 %all-to-all-start.3 = ((f32[6,32,1024]{2,0,1:T(8,128)}), f32[6,32,1024]{2,0,1:T(8,128)}, u32[]{:S(2)}, u32[]{:S(2)}) async-start(f32[6,32,1024]{2,0,1:T(8,128)} %maximum_negate_fusion), calls=%async_computation.3 | async-start | bytes 2097152 | tf_op jit(solution)/shard_map/all_to_all | solution.py:126
  546.9 17.1 %copy-start.28 = (f32[6,2048]{1,0:T(8,128)}, f32[6,2048]{1,0:T(8,128)S(1)}, u32[]{:S(2)}) copy-start(f32[6,2048]{1,0:T(8,128)S(1)} %add.210) | copy-start | bytes 147460
  546.9 17.1 %copy-start.32 = (s32[32768]{0:T(1024)S(1)}, s32[32768]{0:T(1024)}, u32[]{:S(2)}) copy-start(s32[32768]{0:T(1024)} %copy-done.31) | copy-start | bytes 393220
  579.6 23.4 %all-to-all-start.5 = ((f32[6,32,1024]{2,0,1:T(8,128)}), f32[6,32,1024]{2,0,1:T(8,128)}, u32[]{:S(2)}, u32[]{:S(2)}) async-start(f32[6,32,1024]{2,0,1:T(8,128)} %bitcast.333), calls=%async_computation.5 | async-start | bytes 2097152 | tf_op jit(solution)/shard_map/all_to_all | solution.py:105
  613.9 2.3 copy-start.16
  618.5 8.4 copy-start.6
  618.5 8.4 copy-start.9
  618.5 8.4 copy-start.12
  618.5 8.4 copy-start.23
  628.6 22.0 %all-to-all-start.6 = ((f32[6,32,1024]{2,0,1:T(8,128)}), f32[6,32,1024]{2,0,1:T(8,128)}, u32[]{:S(2)}, u32[]{:S(2)}) async-start(f32[6,32,1024]{2,0,1:T(8,128)} %maximum_negate_fusion.1), calls=%async_computation.6 | async-start | bytes 2097152 | tf_op jit(solution)/shard_map/all_to_all | solution.py:126
  684.8 17.1 %copy-start.27 = (f32[6,2048]{1,0:T(8,128)}, f32[6,2048]{1,0:T(8,128)S(1)}, u32[]{:S(2)}) copy-start(f32[6,2048]{1,0:T(8,128)S(1)} %add.217) | copy-start | bytes 147460
  684.9 17.1 %copy-start.33 = (s32[32768]{0:T(1024)S(1)}, s32[32768]{0:T(1024)}, u32[]{:S(2)}) copy-start(s32[32768]{0:T(1024)} %copy-done.31) | copy-start | bytes 393220
  717.6 22.8 %all-to-all-start.8 = ((f32[6,32,1024]{2,0,1:T(8,128)}), f32[6,32,1024]{2,0,1:T(8,128)}, u32[]{:S(2)}, u32[]{:S(2)}) async-start(f32[6,32,1024]{2,0,1:T(8,128)} %bitcast.334), calls=%async_computation.8 | async-start | bytes 2097152 | tf_op jit(solution)/shard_map/all_to_all | solution.py:105
  751.2 2.3 copy-start.17
  755.8 8.4 copy-start.7
  755.8 8.4 copy-start.10
  755.8 8.4 copy-start.13
  755.8 8.4 copy-start.24
  765.9 22.0 %all-to-all-start.9 = ((f32[6,32,1024]{2,0,1:T(8,128)}), f32[6,32,1024]{2,0,1:T(8,128)}, u32[]{:S(2)}, u32[]{:S(2)}) async-start(f32[6,32,1024]{2,0,1:T(8,128)} %maximum_negate_fusion.2), calls=%async_computation.9 | async-start | bytes 2097152 | tf_op jit(solution)/shard_map/all_to_all | solution.py:126
  822.1 17.1 %copy-start.25 = (f32[6,2048]{1,0:T(8,128)}, f32[6,2048]{1,0:T(8,128)S(1)}, u32[]{:S(2)}) copy-start(f32[6,2048]{1,0:T(8,128)S(1)} %add.224) | copy-start | bytes 147460
  822.1 17.1 %copy-start.34 = (s32[32768]{0:T(1024)S(1)}, s32[32768]{0:T(1024)}, u32[]{:S(2)}) copy-start(s32[32768]{0:T(1024)} %copy-done.31) | copy-start | bytes 393220
  854.9 22.8 %all-to-all-start.11 = ((f32[6,32,1024]{2,0,1:T(8,128)}), f32[6,32,1024]{2,0,1:T(8,128)}, u32[]{:S(2)}, u32[]{:S(2)}) async-start(f32[6,32,1024]{2,0,1:T(8,128)} %bitcast.335), calls=%async_computation.11 | async-start | bytes 2097152 | tf_op jit(solution)/shard_map/all_to_all | solution.py:105
  888.5 2.3 copy-start.15
  891.7 15.6 %copy-start.35 = (s32[32768]{0:T(1024)S(1)}, s32[32768]{0:T(1024)}, u32[]{:S(2)}) copy-start(s32[32768]{0:T(1024)} %copy-done.31) | copy-start | bytes 393220
  903.0 21.4 %copy-start.3 = (f32[16,32768]{1,0:T(8,128)S(1)}, f32[16,32768]{1,0:T(8,128)}, u32[]{:S(2)}) copy-start(f32[16,32768]{1,0:T(8,128)} %copy-done.2) | copy-start | bytes 6291460
  903.0 21.4 %all-to-all-start.12 = ((f32[6,32,1024]{2,0,1:T(8,128)}), f32[6,32,1024]{2,0,1:T(8,128)S(1)}, u32[]{:S(2)}, u32[]{:S(2)}) async-start(f32[6,32,1024]{2,0,1:T(8,128)} %maximum_negate_fusion.3), calls=%async_computation.12 | async-start | bytes 2097152 | tf_op jit(solution)/shard_map/all_to_all | solution.py:126
  920.5 9.5 copy-start.30
  924.4 28.6 %copy-start.1 = (s32[256]{0:T(256)S(1)}, s32[256]{0:T(256)}, u32[]{:S(2)}) copy-start(s32[256]{0:T(256)} %param.17) | copy-start | bytes 3076
  930.1 22.3 %copy-start.26 = (f32[6,2048]{1,0:T(8,128)S(1)}, f32[6,2048]{1,0:T(8,128)}, u32[]{:S(2)}) copy-start(f32[6,2048]{1,0:T(8,128)} %copy-done.25) | copy-start | bytes 147460
where the time goes:
time: 964 us; the launch traced here: 953 us
  local copies, waits for them, and re-layouts  373 us (39%)
  matrix products  271 us (28%)
  other arithmetic  156 us (16%)
  starting transfers between devices  64.2 us (7%)
  waiting for transfers between devices  50.5 us (5%)
  blocking collectives  37.4 us (4%)
    gather x1, local copies, waits for them, and re-layouts, on_device(): jnp.repeat(live_pairs, block_len, total_repeat_length=slots_count)  345 us
    dot_general x10, matrix products, pick_columns(): jnp.einsum('cqhw,qsw->cqhs', table.reshape(rows, groups, height, width),...  161 us
    dot_general x8, matrix products, place_columns(): jnp.einsum('cqhs,qsw->cqhw', weighted, lows, precision=lax.Precision.HIGH...  110 us
    dot_general x8, other arithmetic, place_columns(): jnp.einsum('cqhs,qsw->cqhw', weighted, lows, precision=lax.Precision.HIGH...  50.5 us
    all_to_all x4, blocking collectives, from_everyone(): return lax.all_to_all(copies, axis, split_axis=0, concat_axis=0, tiled=True)  37.4 us
    all_to_all x4, waiting for transfers between devices, on_device(): lax.all_to_all(asked_speeds, 'owner', split_axis=1, concat_axis=1, tiled=...  37.4 us
    sub x8, other arithmetic, cross_rows(): left[1] * right[2] - left[2] * right[1]  32.4 us
    all_to_all x4, starting transfers between devices, on_device(): lax.all_to_all(asked_speeds, 'owner', split_axis=1, concat_axis=1, tiled=...  24.9 us
  transfers between devices with their start and end apart: 10, of which 7 were waited for; matrix products, arithmetic and copies ran while one was open for 50% of the time, Pallas kernels for 0%

commit v1 on v0

v1 whole, which is shorter than its diff:
```python
import functools

import jax
import jax.numpy as jnp
from jax import lax
from jax.experimental import pallas as pl
from jax.experimental.pallas import tpu as pltpu
from jax.sharding import PartitionSpec as P

ITERS = 4
relax = 0.1
F32 = jnp.float32
BF16 = jnp.bfloat16
LANES = 128
BLK = 8
PEERS = 32
HIGH = 16
ROWS = PEERS * BLK
STREAM = ROWS + BLK
PARAMS = pltpu.CompilerParams(vmem_limit_bytes=40 << 20)
VMEM = pl.BlockSpec(memory_space=pltpu.VMEM)
SMEM = pl.BlockSpec(memory_space=pltpu.SMEM)


def lane_iota():
    return lax.broadcasted_iota(jnp.int32, (8, LANES), 1)


def row_iota():
    return lax.broadcasted_iota(jnp.int32, (8, LANES), 0)


def pack_kernel(live, geom, first, second, target, warm, send, local, mixed, packed0, packed1):
    lanes = lane_iota()
    subs = row_iota()
    dead = jnp.where(subs == 4, -1.0, 0.0).astype(F32)

    def one_partner(q, _):
        rows = pl.ds(pl.multiple_of(q * BLK, BLK), BLK)
        mixed[pl.ds(4, 8, stride=8), :] = (second[rows, :] & (HIGH * LANES - 1)).astype(F32)
        mixed[pl.ds(5, 8, stride=8), :] = warm[rows, :]
        mixed[pl.ds(6, 8, stride=8), :] = target[rows, :]
        mixed[pl.ds(7, 8, stride=8), :] = (first[rows, :] & (HIGH * LANES - 1)).astype(F32)
        cols = [pl.ds(pl.multiple_of(q * BLK * LANES + b * LANES, LANES), LANES) for b in range(BLK)]
        for b in range(BLK):
            mixed[pl.ds(8 * b + 3, 1), :] = geom[8:9, cols[b]]
        offset = jnp.int32(0)
        cur0 = jnp.zeros((8, LANES), F32)
        cur1 = cur0
        for b in range(BLK):
            geo = geom[0:8, cols[b]]
            mix = mixed[8 * b : 8 * b + 8, :]
            shift = offset & (LANES - 1)
            row = offset >> 7
            rolled0 = pltpu.roll(jnp.where((subs >= 3) & (subs < 6), mix, geo), shift, 1)
            rolled1 = pltpu.roll(jnp.where(subs >= 6, mix, geo), shift, 1)
            keep = lanes < shift
            cur0 = jnp.where(keep, cur0, rolled0)
            cur1 = jnp.where(keep, cur1, rolled1)
            packed0[row] = cur0
            packed1[row] = cur1
            offset = offset + live[q * BLK + b]
            spill = jnp.broadcast_to((offset >> 7) > row, (8, LANES))
            cur0 = jnp.where(spill, rolled0, cur0)
            cur1 = jnp.where(spill, rolled1, cur1)
        packed0[offset >> 7] = cur0
        packed1[offset >> 7] = cur1
        for r in range(BLK):
            alive = lanes + r * LANES < offset
            send[q, 8 * r : 8 * r + 8, :] = jnp.where(alive, packed0[r], dead)
            local[q, 8 * r : 8 * r + 8, :] = jnp.where(alive, packed1[r], 0.0)
        return 0

    lax.fori_loop(0, PEERS, one_partner, 0)


def gather_rows(tables, index, count):
    lows = [i & (LANES - 1) for i in index]
    highs = [i >> 7 for i in index]
    found = [[None] * count for _ in index]
    for h in range(HIGH):
        masks = [hi == h for hi in highs]
        for c in range(count):
            ref, start = tables[c]
            line = jnp.broadcast_to(ref[start + h : start + h + 1, :], (8, LANES))
            for k in range(len(index)):
                got = jnp.take_along_axis(line, lows[k], axis=1, mode="promise_in_bounds")
                found[k][c] = got if h == 0 else jnp.where(masks[k], got, found[k][c])
    return found


def group_rows(g):
    return pl.ds(pl.multiple_of(g * 8, 8), 8)


def prepare(first, meta, d0, d1, vel, prop, x_out, idx_out, imp_out, u_out, m_out):
    total = meta[PEERS]

    def one_group(g, _):
        base = g * 64

        def get(ref, k):
            return ref[pl.ds(base + k, 8, stride=8), :]

        flag = get(d0, 4)
        alive = (flag >= 0.0) & (row_iota() + g * 8 < total)
        if first:
            normal = [get(d1, k) for k in (0, 1, 2)]
            arm = [get(d1, k) for k in (3, 4, 5)]
            index = get(d1, 7)
            sign = 1.0
        else:
            normal = [get(d0, k) for k in (0, 1, 2)]
            arm = [get(d0, k) for k in (6, 7, 3)]
            index = flag
            sign = -1.0
        cross = [
            arm[1] * normal[2] - arm[2] * normal[1],
            arm[2] * normal[0] - arm[0] * normal[2],
            arm[0] * normal[1] - arm[1] * normal[0],
        ]
        index = jnp.where(alive, index, 0.0).astype(jnp.int32)
        tables = [(vel, 16 * c) for c in range(6)] + [(prop, 16 * c) for c in range(4)]
        got = gather_rows(tables, [index], 10)[0]
        terms = [jnp.where(alive, sign * t, 0.0) for t in normal + cross]
        mass = got[6]
        for k in range(3):
            mass = mass + cross[k] * cross[k] * got[7 + k]
        u = terms[0] * got[0]
        for c in range(1, 6):
            u = u + terms[c] * got[c]
        for c in range(6):
            x_out[g, c] = terms[c]
        if first:
            off = jnp.where(alive, get(d1, 6), 0.0)
            x_out[g, 6] = off
            u = u - off
        rows = group_rows(g)
        idx_out[rows, :] = index
        imp_out[rows, :] = jnp.where(alive, get(d0, 5), 0.0)
        u_out[rows, :] = u
        m_out[rows, :] = jnp.where(alive, mass, -1.0)
        return 0

    lax.fori_loop(0, (total + 7) >> 3, one_group, 0)


def first_kernel(
    live, send, local, velocity, properties,
    x_out, idx_out, imp_out, u_out, m_out, meta, share, vel, prop, d0, d1,
):
    for c in range(6):
        for h in range(HIGH):
            vel[c * HIGH + h : c * HIGH + h + 1, :] = velocity[c : c + 1, h * LANES : (h + 1) * LANES]
    for c in range(4):
        for h in range(HIGH):
            prop[c * HIGH + h : c * HIGH + h + 1, :] = properties[c : c + 1, h * LANES : (h + 1) * LANES]

    def one_partner(q, base):
        count = live[q * BLK]
        for b in range(1, BLK):
            count = count + live[q * BLK + b]
        meta[q] = base
        rows = pl.ds(pl.multiple_of(base * 8, 8), 64)
        d0[rows, :] = send[q]
        d1[rows, :] = local[q]
        return base + ((count + LANES - 1) >> 7)

    meta[PEERS] = lax.fori_loop(0, PEERS, one_partner, jnp.int32(0))
    prepare(True, meta, d0, d1, vel, prop, x_out, idx_out, imp_out, u_out, m_out)

    def one_share(q, _):
        rows = pl.ds(meta[q], 8)
        share[q, 0] = u_out[rows, :]
        share[q, 1] = m_out[rows, :]
        return 0

    lax.fori_loop(0, PEERS, one_share, 0)


def second_kernel(
    received, share_first, vel, prop,
    x_out, idx_out, imp_out, u_out, m_out, meta, share, d0,
):
    def one_partner(q, base):
        meta[q] = base
        block = received[q]
        d0[pl.ds(pl.multiple_of(base * 8, 8), 64), :] = block
        flags = received[q, pl.ds(4, 8, stride=8), :]
        used = jnp.max(jnp.where(flags >= 0.0, row_iota() + 1, 0))
        return base + used

    meta[PEERS] = lax.fori_loop(0, PEERS, one_partner, jnp.int32(0))
    prepare(False, meta, d0, None, vel, prop, x_out, idx_out, imp_out, u_out, m_out)

    def one_share(q, _):
        rows = pl.ds(meta[q], 8)
        share[q, 0] = share_first[q, 0]
        share[q, 1] = share_first[q, 1]
        share[q, 2] = u_out[rows, :]
        share[q, 3] = m_out[rows, :]
        return 0

    lax.fori_loop(0, PEERS, one_share, 0)


def apply_kernel(start, *refs):
    (meta_a, meta_b, x_a, x_b, idx_a, idx_b, imp_a, imp_b, u_a, u_b, w_a, w_b, received) = refs[:13]
    outs = refs[13:]
    if start:
        j_out, new_a, new_b, weight_a, weight_b, other_a, other_b, mass_a, mass_b, total = outs
    else:
        j_out, new_a, new_b, other_a, other_b, total = outs
        weight_a, weight_b, mass_a, mass_b = w_a, w_b, None, None

    step = 2 if start else 1

    def one_partner(p, _):
        rows_a = pl.ds(meta_a[p], 8)
        rows_b = pl.ds(meta_b[p], 8)
        other_a[rows_a, :] = received[p, step]
        other_b[rows_b, :] = received[p, 0]
        if start:
            mass_a[rows_a, :] = received[p, 3]
            mass_b[rows_b, :] = received[p, 1]
        return 0

    lax.fori_loop(0, PEERS, one_partner, 0)
    total[...] = jnp.zeros_like(total)
    iota_high = lax.broadcasted_iota(jnp.int32, (HIGH, LANES), 0)
    iota_low = lax.broadcasted_iota(jnp.int32, (LANES, LANES), 0)

    def side(x, idx, imp, u, other, mass, own_mass, weight, new):
        def one_group(g, _):
            rows = group_rows(g)
            if mass is not None:
                mine = own_mass[rows, :]
                alive = mine > 0.0
                scale = jnp.where(alive, relax / (mine + mass[rows, :]), 0.0)
                weight[rows, :] = scale
            else:
                scale = weight[rows, :]
                alive = scale > 0.0
            before = imp[rows, :]
            fresh = jnp.maximum(before - (u[rows, :] + other[rows, :]) * scale, 0.0)
            fresh = jnp.where(alive, fresh, before)
            applied = fresh - before
            new[rows, :] = fresh
            values = [applied * x[g, c] for c in range(6)]
            tops = [v.astype(BF16).astype(F32) for v in values]
            pieces = tops + [v - t for v, t in zip(values, tops)]
            index = idx[rows, :]
            low = index & (LANES - 1)
            high = index >> 7
            lefts = []
            rights = []
            for b in range(8):
                mask = jnp.broadcast_to(high[b : b + 1], (HIGH, LANES)) == iota_high
                lefts.append(
                    jnp.concatenate(
                        [
                            jnp.where(mask, jnp.broadcast_to(v[b : b + 1], (HIGH, LANES)), 0.0).astype(BF16)
                            for v in pieces
                        ],
                        axis=0,
                    )
                )
                hit = jnp.broadcast_to(low[b : b + 1], (LANES, LANES)) == iota_low
                rights.append(jnp.where(hit, 1.0, 0.0).astype(BF16))
            total[...] += lax.dot_general(
                jnp.concatenate(lefts, axis=1),
                jnp.concatenate(rights, axis=1),
                (((1,), (1,)), ((), ())),
                preferred_element_type=F32,
            )
            return 0

        return one_group

    lax.fori_loop(
        0, (meta_a[PEERS] + 7) >> 3,
        side(x_a, idx_a, imp_a, u_a, other_a, mass_a, w_a, weight_a, new_a), 0,
    )
    lax.fori_loop(
        0, (meta_b[PEERS] + 7) >> 3,
        side(x_b, idx_b, imp_b, u_b, other_b, mass_b, w_b, weight_b, new_b), 0,
    )
    j_out[...] = total[0:96] + total[96:192]


def moved(vel, prop, j0, j1, j2, j3, c):
    rows = slice(c * HIGH, (c + 1) * HIGH)
    k = max(c - 2, 0)
    gain = (j0[rows, :] + j2[rows, :]) + (j1[rows, :] + j3[rows, :])
    return vel[rows, :] + prop[k * HIGH : (k + 1) * HIGH, :] * gain


def gather_kernel(
    meta_a, meta_b, vel, prop, j0, j1, j2, j3, x_a, x_b, idx_a, idx_b,
    vel_out, u_a, u_b, share,
):
    for c in range(6):
        vel_out[c * HIGH : (c + 1) * HIGH, :] = moved(vel, prop, j0, j1, j2, j3, c)
    tables = [(vel_out, HIGH * c) for c in range(6)]

    def side(x, idx, u_out, offset):
        def two_groups(pair, _):
            groups = [pair * 2, pair * 2 + 1]
            got = gather_rows(tables, [idx[group_rows(g), :] for g in groups], 6)
            for k, g in enumerate(groups):
                u = x[g, 0] * got[k][0]
                for c in range(1, 6):
                    u = u + x[g, c] * got[k][c]
                if offset:
                    u = u - x[g, 6]
                u_out[group_rows(g), :] = u
            return 0

        return two_groups

    lax.fori_loop(0, (meta_a[PEERS] + 15) >> 4, side(x_a, idx_a, u_a, True), 0)
    lax.fori_loop(0, (meta_b[PEERS] + 15) >> 4, side(x_b, idx_b, u_b, False), 0)

    def one_share(q, _):
        share[q, 0] = u_a[pl.ds(meta_a[q], 8), :]
        share[q, 1] = u_b[pl.ds(meta_b[q], 8), :]
        return 0

    lax.fori_loop(0, PEERS, one_share, 0)


def final_kernel(vel, prop, j0, j1, j2, j3, out):
    for c in range(6):
        rows = moved(vel, prop, j0, j1, j2, j3, c)
        for h in range(HIGH):
            out[c : c + 1, h * LANES : (h + 1) * LANES] = rows[h : h + 1]


def unpack_kernel(live, meta, imp, warm, out):
    lanes = lax.broadcasted_iota(jnp.int32, (1, LANES), 1)

    def one_partner(q, _):
        offset = jnp.int32(0)
        for b in range(BLK):
            count = live[q * BLK + b]
            shift = offset & (LANES - 1)
            row = meta[q] + (offset >> 7)
            here = imp[pl.ds(row, 1), :]
            after = imp[pl.ds(row + 1, 1), :]
            both = jnp.where(lanes >= shift, here, after)
            back = pltpu.roll(both, (LANES - shift) & (LANES - 1), 1)
            slot = pl.ds(q * BLK + b, 1)
            out[slot, :] = jnp.where(lanes < count, back, warm[slot, :])
            offset = offset + count
        return 0

    lax.fori_loop(0, PEERS, one_partner, 0)


def shape(*dims, dtype=F32):
    return jax.ShapeDtypeStruct(dims, dtype)


def call(kernel, ins, outs, scratch=(), flops=10_000_000, bytes_accessed=4_000_000, name=None):
    return pl.pallas_call(
        kernel,
        in_specs=list(ins),
        out_specs=tuple(SMEM if o.dtype == jnp.int32 and len(o.shape) == 1 else VMEM for o in outs),
        out_shape=tuple(outs),
        scratch_shapes=list(scratch),
        compiler_params=PARAMS,
        cost_estimate=pl.CostEstimate(
            flops=flops, bytes_accessed=bytes_accessed, transcendentals=0
        ),
        name=name,
    )


def on_device(
    velocity, properties, first_body, second_body, geometry, target_speed, warm_impulse, live_pairs
):
    table = lambda array: array.reshape(ROWS, LANES)
    warm = table(warm_impulse)
    stream = shape(STREAM, LANES)
    meta_shape = shape(PEERS + 1, dtype=jnp.int32)
    send, local = call(
        pack_kernel,
        [SMEM] + [VMEM] * 5,
        [shape(PEERS, 64, LANES)] * 2,
        [pltpu.VMEM((64, LANES), F32)] + [pltpu.VMEM((16, 8, LANES), F32)] * 2,
        name="pack",
    )(live_pairs, geometry, table(first_body), table(second_body), table(target_speed), warm)
    received = lax.all_to_all(send, "owner", split_axis=0, concat_axis=0, tiled=True)
    x_a, idx_a, imp_a, u_a, m_a, meta_a, share_a, vel, prop = call(
        first_kernel,
        [SMEM] + [VMEM] * 4,
        [
            shape(ROWS // 8, 7, 8, LANES), shape(STREAM, LANES, dtype=jnp.int32), stream, stream,
            stream, meta_shape, shape(PEERS, 2, 8, LANES), shape(96, LANES), shape(64, LANES),
        ],
        [pltpu.VMEM((STREAM * 8, LANES), F32)] * 2,
        name="first",
    )(live_pairs, send, local, velocity, properties)
    x_b, idx_b, imp_b, u_b, m_b, meta_b, share = call(
        second_kernel,
        [VMEM] * 4,
        [
            shape(ROWS // 8, 6, 8, LANES), shape(STREAM, LANES, dtype=jnp.int32), stream, stream,
            stream, meta_shape, shape(PEERS, 4, 8, LANES),
        ],
        [pltpu.VMEM((STREAM * 8, LANES), F32)],
        name="second",
    )(received, share_a, vel, prop)
    w_a, w_b = m_a, m_b
    n_sub = lax.axis_size("sub")
    for iteration in range(ITERS):
        start = iteration == 0
        told = lax.all_to_all(share, "owner", split_axis=0, concat_axis=0, tiled=True)
        outs = call(
            functools.partial(apply_kernel, start),
            [SMEM, SMEM] + [VMEM] * 11,
            [shape(96, LANES), stream, stream] + ([stream, stream] if start else []),
            [pltpu.VMEM((STREAM, LANES), F32)] * (4 if start else 2)
            + [pltpu.VMEM((192, LANES), F32)],
            name="apply",
        )(meta_a, meta_b, x_a, x_b, idx_a, idx_b, imp_a, imp_b, u_a, u_b, w_a, w_b, told)
        if start:
            own, imp_a, imp_b, w_a, w_b = outs
        else:
            own, imp_a, imp_b = outs
        gains = [own] + [
            lax.ppermute(own, "sub", [(i, (i + d) % n_sub) for i in range(n_sub)])
            for d in (1, 2, 3)
        ]
        if iteration < ITERS - 1:
            vel, u_a, u_b, share = call(
                gather_kernel,
                [SMEM, SMEM] + [VMEM] * 10,
                [shape(96, LANES), stream, stream, shape(PEERS, 2, 8, LANES)],
                name="gather",
            )(meta_a, meta_b, vel, prop, *gains, x_a, x_b, idx_a, idx_b)
    (impulse,) = call(
        unpack_kernel, [SMEM, SMEM, VMEM, VMEM], [shape(ROWS, LANES)], name="unpack"
    )(live_pairs, meta_a, imp_a, warm)
    (out,) = call(final_kernel, [VMEM] * 6, [shape(6, HIGH * LANES)], name="final")(
        vel, prop, *gains
    )
    return (out, impulse.reshape(-1))


def solution(mesh):
    return jax.shard_map(
        on_device,
        mesh=mesh,
        in_specs=(
            P(None, "owner"),
            P(None, "owner"),
            P(("owner", "sub")),
            P(("owner", "sub")),
            P(None, ("owner", "sub")),
            P(("owner", "sub")),
            P(("owner", "sub")),
            P(("owner", "sub")),
        ),
        out_specs=(P(None, "owner"), P(("owner", "sub"))),
        check_vma=False,
    )
```

time: 964 us -> 173 us (0.18); the launches traced: 953 us -> 173 us
  local copies, waits for them, and re-layouts: 373 us -> 8.69 us
  matrix products: 271 us -> 0 us
  other arithmetic: 156 us -> 0 us
  Pallas kernels: 0 us -> 66.3 us
  starting transfers between devices: 64.2 us -> 26.8 us
  waiting for transfers between devices: 50.5 us -> 13.7 us
  blocking collectives: 37.4 us -> 56.6 us
    gather x1 -> x0, local copies, waits for them, and re-layouts: 345 us -> none  [on_device(): jnp.repeat(live_pairs, block_len, total_repeat_length=slots_count)]
    dot_general x18 -> x0, matrix products: 271 us -> none  [the longest x10 161 us: pick_columns(): jnp.einsum('cqhw,qsw->cqhs', table.reshape(rows, groups, height, width),...]
    pallas_call x0 -> x12, Pallas kernels: none -> 66.3 us  [the longest x4 28.6 us: on_device(): call(functools.partial(apply_kernel, start), [SMEM, SMEM] + [VMEM] * 11,...]
    all_to_all x10 -> x1, starting transfers between devices: 64.2 us -> 9.6 us  [on_device(): lax.all_to_all(send, 'owner', split_axis=0, concat_axis=0, tiled=True)]
    dot_general x8 -> x0, other arithmetic: 50.5 us -> none  [place_columns(): jnp.einsum('cqhs,qsw->cqhw', weighted, lows, precision=lax.Precision.HIGH...]
    all_to_all x10 -> x1, waiting for transfers between devices: 50.5 us -> 8.8 us  [on_device(): lax.all_to_all(send, 'owner', split_axis=0, concat_axis=0, tiled=True)]
    sub x10 -> x0, other arithmetic: 37.8 us -> none  [the longest x8 32.4 us: cross_rows(): left[1] * right[2] - left[2] * right[1]]
    mul x20 -> x0, other arithmetic: 28.3 us -> none  [the longest x8 13.9 us: on_device(): props_second[0] * applied * normal]
  transfers between devices with their start and end apart: 10 -> 13, of which waited for: 7 -> 7; matrix products, arithmetic and copies ran while one was open for 50% -> 0% of each run, Pallas kernels for 0% -> 6%
where the time goes in v1:
time: 173 us
  Pallas kernels  66.3 us (38%)
  blocking collectives  56.6 us (33%)
  starting transfers between devices  26.8 us (15%)
  waiting for transfers between devices  13.7 us (8%)
  local copies, waits for them, and re-layouts  8.69 us (5%)
    all_to_all x4, blocking collectives, on_device(): lax.all_to_all(share, 'owner', split_axis=0, concat_axis=0, tiled=True)  56.6 us
    pallas_call x4, Pallas kernels, on_device(): call(functools.partial(apply_kernel, start), [SMEM, SMEM] + [VMEM] * 11,...  28.6 us
    ppermute x12, starting transfers between devices, on_device(): lax.ppermute(own, 'sub', [(i, (i + d) % n_sub) for i in range(n_sub)])  17.2 us
    pallas_call x3, Pallas kernels, on_device(): call(gather_kernel, [SMEM, SMEM] + [VMEM] * 10, [shape(96, LANES), stream...  12.7 us
    pallas_call x1, Pallas kernels, on_device(): call(second_kernel, [VMEM] * 4, [shape(ROWS // 8, 6, 8, LANES), shape(STR...  9.94 us
    all_to_all x1, starting transfers between devices, on_device(): lax.all_to_all(send, 'owner', split_axis=0, concat_axis=0, tiled=True)  9.6 us
    all_to_all x1, waiting for transfers between devices, on_device(): lax.all_to_all(send, 'owner', split_axis=0, concat_axis=0, tiled=True)  8.8 us
    unnamed x32, local copies, waits for them, and re-layouts  8.69 us
  transfers between devices with their start and end apart: 13, of which 7 were waited for; matrix products, arithmetic and copies ran while one was open for 0% of the time, Pallas kernels for 6%

profile of v1, /device:TPU:1, one launch (start us, length us, event | category | flops | bytes accessed | tf_op | source)
XLA Modules:
  0.0 172.9 jit_solution(14845827891634512267)
XLA Ops:
  0.6 0.0 copy-start
  0.6 1.6 copy-done
  2.2 0.0 copy-start.1
  2.2 0.9 copy-done.1
  3.1 0.0 copy-start.9
  3.1 0.9 copy-done.9
  4.0 0.9 copy-done.10
  4.9 0.9 copy-done.11
  5.8 0.7 copy-done.14
  6.5 5.0 %pack.1 = (f32[32,64,128]{2,1,0:T(8,128)}, f32[32,64,128]{2,1,0:T(8,128)S(1)}) custom-call(s32[256]{0:T(256)S(1)} %copy-done.14, f32[9,32768]{1,0:T(8,128)S(1)} %copy-done, s32[256,128]{1,0:T(8,128)S(1)} %bitcast.7, s32[256,128]{1,0:T(8,128)S(1)} %bitcast.8, f32[256,128]{1,0:T(8,128)S(1)} %bitcast.9, f32[256,128]{1,0:T(8,128)S(1)} %bitcast.5), custom_call_target="tpu_custom_call" | custom-call | flops 10000000 | bytes 4000000 | tf_op jit(solution)/shard_map/pack/pallas_call | solution.py:386
  11.5 9.6 %all-to-all-start = ((f32[32,64,128]{2,1,0:T(8,128)}), f32[32,64,128]{2,1,0:T(8,128)S(1)}, u32[]{:S(2)}, u32[]{:S(2)}) async-start(f32[32,64,128]{2,1,0:T(8,128)} %get-tuple-element.45.send), calls=%async_computation | async-start | bytes 2097152 | tf_op jit(solution)/shard_map/all_to_all | solution.py:393
  21.1 0.0 copy-done.13
  21.1 0.0 copy-done.15
  21.1 0.0 copy-start.12
  21.1 0.8 copy-done.12
  22.0 5.5 %first.1 = (f32[32,7,8,128]{3,2,1,0:T(8,128)S(1)}, s32[264,128]{1,0:T(8,128)S(1)}, f32[264,128]{1,0:T(8,128)S(1)}, f32[264,128]{1,0:T(8,128)S(1)}, f32[264,128]{...) custom-call(s32[256]{0:T(256)S(1)} %copy-done.15, ...), custom_call_target="tpu_custom_call" | custom-call | flops 10000000 | bytes 4000000 | tf_op jit(solution)/shard_map/first/pallas_call | solution.py:394
  27.5 0.0 copy-start.3
  27.5 0.7 copy-done.3
  28.2 0.6 copy-done.5
  28.8 0.6 copy-done.7
  29.5 8.8 %all-to-all-done.received = f32[32,64,128]{2,1,0:T(8,128)S(1)} async-done(((f32[32,64,128]{2,1,0:T(8,128)}), f32[32,64,128]{2,1,0:T(8,128)S(1)}, u32[]{:S(2)}, u32[]{:S(2)}) %all-to-all-start) | async-done | bytes 1048608 | tf_op jit(solution)/shard_map/all_to_all | solution.py:393
  38.3 9.9 %second.1 = (f32[32,6,8,128]{3,2,1,0:T(8,128)S(1)}, s32[264,128]{1,0:T(8,128)S(1)}, f32[264,128]{1,0:T(8,128)S(1)}, f32[264,128]{1,0:T(8,128)S(1)}, f32[264,128]...) custom-call(f32[32,64,128]{2,1,0:T(8,128)S(1)} %all-to-all-done.received, ...), custom_call_target="tpu_custom_call" | custom-call | flops 10000000 | bytes 4000000 | tf_op jit(solution)/shard_map/second/pallas_call | solution.py:404
  48.2 14.8 %all_to_all.25.refs_12_ = f32[32,4,8,128]{3,2,1,0:T(8,128)S(1)} all-to-all(f32[32,4,8,128]{3,2,1,0:T(8,128)S(1)} %get-tuple-element.62), channel_id=1, replica_groups=mesh['owner'=32,'sub'=4] {'owner'}, dimensions={0} | all-to-all | bytes 1048576 | tf_op jit(solution)/shard_map/all_to_all | solution.py:418
  63.1 0.0 copy-done.4
  63.1 0.0 copy-done.6
  63.1 0.0 copy-done.8
  63.1 7.0 %apply.4 = (f32[96,128]{1,0:T(8,128)S(1)}, f32[264,128]{1,0:T(8,128)S(1)}, f32[264,128]{1,0:T(8,128)S(1)}, f32[264,128]{1,0:T(8,128)S(1)}, f32[264,128]{1,0:T(8,128)S(1)}) custom-call(s32[33]{0:T(128)S(1)} %get-tuple-element.47.refs_0_.meta_a.meta, s32[33]{0:T(128)S(1)} %get-tuple-element.51.refs_1_.meta_b, ...), custom_call_target="tpu_custom_call" | custom-call | flops 10000000 | bytes 4000000 | tf_op jit(solution)/shard_map/apply/pallas_call | solution.py:419
  70.1 1.3 collective-permute-start
  71.3 2.2 %collective-permute-start.1 = (f32[96,128]{1,0:T(8,128)S(1)}, f32[96,128]{1,0:T(8,128)S(1)}, u32[]{:S(2)}, u32[]{:S(2)}) collective-permute-start(f32[96,128]{1,0:T(8,128)S(1)} %get-tuple-element.63.j0), channel_id=1, source_target_pairs={{0,2},{1,3},{2,0},{3,1},{4,6},{5,7},{6,4},{7,5},{8,10},{9,11},{10,... | collective-permute-start | bytes 147464 | tf_op jit(solution)/shard_map/ppermute | solution.py:432
  73.5 2.0 %collective-permute-start.2 = (f32[96,128]{1,0:T(8,128)S(1)}, f32[96,128]{1,0:T(8,128)S(1)}, u32[]{:S(2)}, u32[]{:S(2)}) collective-permute-start(f32[96,128]{1,0:T(8,128)S(1)} %get-tuple-element.63.j0), channel_id=1, source_target_pairs={{0,3},{1,0},{2,1},{3,2},{4,7},{5,4},{6,5},{7,6},{8,11},{9,8},{10,9... | collective-permute-start | bytes 147464 | tf_op jit(solution)/shard_map/ppermute | solution.py:432
  75.5 0.0 collective-permute-done.j1
  75.5 0.7 collective-permute-done.1.j2
  76.2 0.5 collective-permute-done.2.j3
  76.6 4.2 %gather.3 = (f32[96,128]{1,0:T(8,128)S(1)}, f32[264,128]{1,0:T(8,128)S(1)}, f32[264,128]{1,0:T(8,128)S(1)}, f32[32,2,8,128]{3,2,1,0:T(8,128)S(1)}) custom-call(s32[33]{0:T(128)S(1)} %get-tuple-element.47.refs_0_.meta_a.meta, s32[33]{0:T(128)S(1)} %get-tuple-element.51.refs_1_.meta_b, f32[96,128]{1,0:T(8,128)S(1)} %get-tuple-element.49.vel, ...), custom_call_target="tpu_custom_call" | custom-call | flops 10000000 | bytes 4000000 | tf_op jit(solution)/shard_map/gather/pallas_call | solution.py:436
  80.9 13.7 %all_to_all.26.refs_12_ = f32[32,2,8,128]{3,2,1,0:T(8,128)S(1)} all-to-all(f32[32,2,8,128]{3,2,1,0:T(8,128)S(1)} %get-tuple-element.71), channel_id=1, replica_groups=mesh['owner'=32,'sub'=4] {'owner'}, dimensions={0} | all-to-all | bytes 524288 | tf_op jit(solution)/shard_map/all_to_all | solution.py:418
  94.6 7.0 %apply.5 = (f32[96,128]{1,0:T(8,128)S(1)}, f32[264,128]{1,0:T(8,128)S(1)}, f32[264,128]{1,0:T(8,128)S(1)}) custom-call(s32[33]{0:T(128)S(1)} %get-tuple-element.47.refs_0_.meta_a.meta, s32[33]{0:T(128)S(1)} %get-tuple-element.51.refs_1_.meta_b, f32[32,7,8,128]{3,2,1,0:T(8,128)S(1)} %get-tuple-element.52.refs_2_.x_a, ...), custom_call_target="tpu_custom_call" | custom-call | flops 10000000 | bytes 4000000 | tf_op jit(solution)/shard_map/apply/pallas_call | solution.py:419
  101.5 0.7 collective-permute-start.3
  102.2 2.3 %collective-permute-start.4 = (f32[96,128]{1,0:T(8,128)S(1)}, f32[96,128]{1,0:T(8,128)S(1)}, u32[]{:S(2)}, u32[]{:S(2)}) collective-permute-start(f32[96,128]{1,0:T(8,128)S(1)} %get-tuple-element.72.j0), channel_id=1, source_target_pairs={{0,2},{1,3},{2,0},{3,1},{4,6},{5,7},{6,4},{7,5},{8,10},{9,11},{10,... | collective-permute-start | bytes 147464 | tf_op jit(solution)/shard_map/ppermute | solution.py:432
  104.5 1.7 collective-permute-start.5
  106.1 0.7 collective-permute-done.3.j1
  106.8 0.0 collective-permute-done.4.j2
  106.8 0.9 collective-permute-done.5.j3
  107.7 4.2 %gather.4 = (f32[96,128]{1,0:T(8,128)S(1)}, f32[264,128]{1,0:T(8,128)S(1)}, f32[264,128]{1,0:T(8,128)S(1)}, f32[32,2,8,128]{3,2,1,0:T(8,128)S(1)}) custom-call(s32[33]{0:T(128)S(1)} %get-tuple-element.47.refs_0_.meta_a.meta, s32[33]{0:T(128)S(1)} %get-tuple-element.51.refs_1_.meta_b, f32[96,128]{1,0:T(8,128)S(1)} %get-tuple-element.64.vel, ...), custom_call_target="tpu_custom_call" | custom-call | flops 10000000 | bytes 4000000 | tf_op jit(solution)/shard_map/gather/pallas_call | solution.py:436
  112.0 14.4 %all_to_all.27.refs_12_ = f32[32,2,8,128]{3,2,1,0:T(8,128)S(1)} all-to-all(f32[32,2,8,128]{3,2,1,0:T(8,128)S(1)} %get-tuple-element.78), channel_id=1, replica_groups=mesh['owner'=32,'sub'=4] {'owner'}, dimensions={0} | all-to-all | bytes 524288 | tf_op jit(solution)/shard_map/all_to_all | solution.py:418
  126.3 7.0 %apply.6 = (f32[96,128]{1,0:T(8,128)S(1)}, f32[264,128]{1,0:T(8,128)S(1)}, f32[264,128]{1,0:T(8,128)S(1)}) custom-call(s32[33]{0:T(128)S(1)} %get-tuple-element.47.refs_0_.meta_a.meta, s32[33]{0:T(128)S(1)} %get-tuple-element.51.refs_1_.meta_b, f32[32,7,8,128]{3,2,1,0:T(8,128)S(1)} %get-tuple-element.52.refs_2_.x_a, ...), custom_call_target="tpu_custom_call" | custom-call | flops 10000000 | bytes 4000000 | tf_op jit(solution)/shard_map/apply/pallas_call | solution.py:419
  133.3 0.1 collective-permute-start.6
  133.4 1.9 %collective-permute-start.7 = (f32[96,128]{1,0:T(8,128)S(1)}, f32[96,128]{1,0:T(8,128)S(1)}, u32[]{:S(2)}, u32[]{:S(2)}) collective-permute-start(f32[96,128]{1,0:T(8,128)S(1)} %get-tuple-element.79.j0), channel_id=1, source_target_pairs={{0,2},{1,3},{2,0},{3,1},{4,6},{5,7},{6,4},{7,5},{8,10},{9,11},{10,... | collective-permute-start | bytes 147464 | tf_op jit(solution)/shard_map/ppermute | solution.py:432
  135.3 1.8 %collective-permute-start.8 = (f32[96,128]{1,0:T(8,128)S(1)}, f32[96,128]{1,0:T(8,128)S(1)}, u32[]{:S(2)}, u32[]{:S(2)}) collective-permute-start(f32[96,128]{1,0:T(8,128)S(1)} %get-tuple-element.79.j0), channel_id=1, source_target_pairs={{0,3},{1,0},{2,1},{3,2},{4,7},{5,4},{6,5},{7,6},{8,11},{9,8},{10,9... | collective-permute-start | bytes 147464 | tf_op jit(solution)/shard_map/ppermute | solution.py:432
  137.1 1.7 collective-permute-done.6.j1
  138.8 0.0 collective-permute-done.7.j2
  138.8 0.5 collective-permute-done.8.j3
  139.3 4.2 %gather.5 = (f32[96,128]{1,0:T(8,128)S(1)}, f32[264,128]{1,0:T(8,128)S(1)}, f32[264,128]{1,0:T(8,128)S(1)}, f32[32,2,8,128]{3,2,1,0:T(8,128)S(1)}) custom-call(s32[33]{0:T(128)S(1)} %get-tuple-element.47.refs_0_.meta_a.meta, s32[33]{0:T(128)S(1)} %get-tuple-element.51.refs_1_.meta_b, f32[96,128]{1,0:T(8,128)S(1)} %get-tuple-element.73.vel, ...), custom_call_target="tpu_custom_call" | custom-call | flops 10000000 | bytes 4000000 | tf_op jit(solution)/shard_map/gather/pallas_call | solution.py:436
  143.5 0.0 copy-start.2
  143.5 13.7 %all_to_all.28.refs_12_ = f32[32,2,8,128]{3,2,1,0:T(8,128)S(1)} all-to-all(f32[32,2,8,128]{3,2,1,0:T(8,128)S(1)} %get-tuple-element.85), channel_id=1, replica_groups=mesh['owner'=32,'sub'=4] {'owner'}, dimensions={0} | all-to-all | bytes 524288 | tf_op jit(solution)/shard_map/all_to_all | solution.py:418
  157.2 7.6 %apply.7 = (f32[96,128]{1,0:T(8,128)S(1)}, f32[264,128]{1,0:T(8,128)S(1)}, f32[264,128]{1,0:T(8,128)}) custom-call(s32[33]{0:T(128)S(1)} %get-tuple-element.47.refs_0_.meta_a.meta, s32[33]{0:T(128)S(1)} %get-tuple-element.51.refs_1_.meta_b, f32[32,7,8,128]{3,2,1,0:T(8,128)S(1)} %get-tuple-element.52.refs_2_.x_a, ...), custom_call_target="tpu_custom_call" | custom-call | flops 10000000 | bytes 4000000 | tf_op jit(solution)/shard_map/apply/pallas_call | solution.py:419
  164.9 1.9 %collective-permute-start.10 = (f32[96,128]{1,0:T(8,128)S(1)}, f32[96,128]{1,0:T(8,128)S(1)}, u32[]{:S(2)}, u32[]{:S(2)}) collective-permute-start(f32[96,128]{1,0:T(8,128)S(1)} %get-tuple-element.86.j0), channel_id=1, source_target_pairs={{0,2},{1,3},{2,0},{3,1},{4,6},{5,7},{6,4},{7,5},{8,10},{9,11},{10,... | collective-permute-start | bytes 147464 | tf_op jit(solution)/shard_map/ppermute | solution.py:432
  166.7 0.7 collective-permute-start.11
  167.5 0.7 collective-permute-start.9
  168.2 0.0 copy-done.2
  168.2 4.0 %unpack.1 = f32[256,128]{1,0:T(8,128)} custom-call(s32[256]{0:T(256)S(1)} %copy-done.15, s32[33]{0:T(128)S(1)} %get-tuple-element.47.refs_0_.meta_a.meta, f32[264,128]{1,0:T(8,128)S(1)} %get-tuple-element.87.imp, f32[256,128]{1,0:T(8,128)S(1)} %bitcast.6), custom_call_target="tpu_custom_call" | custom-call | flops 10000000 | bytes 4000000 | tf_op jit(solution)/shard_map/unpack/pallas_call | solution.py:442
  172.2 0.0 collective-permute-done.10.j2
  172.2 0.0 collective-permute-done.11.j3
  172.2 0.0 collective-permute-done.9.j1
  172.2 0.7 final.1
  (10 shorter events, 0.0 us)
Async XLA Ops:
  0.6 1.6 copy-start
  2.2 0.9 copy-start.1
  3.1 0.9 copy-start.9
  4.0 0.9 copy-start.10
  4.9 0.9 copy-start.11
  5.8 0.7 copy-start.14
  6.5 14.6 %copy-start.13 = (f32[4,2048]{1,0:T(4,128)S(1)}, f32[4,2048]{1,0:T(4,128)}, u32[]{:S(2)}) copy-start(f32[4,2048]{1,0:T(4,128)} %properties.1) | copy-start | bytes 98308
  6.5 14.6 %copy-start.15 = (s32[256]{0:T(256)S(1)}, s32[256]{0:T(256)}, u32[]{:S(2)}) copy-start(s32[256]{0:T(256)} %live.5) | copy-start | bytes 3076
  11.5 26.8 %all-to-all-start = ((f32[32,64,128]{2,1,0:T(8,128)}), f32[32,64,128]{2,1,0:T(8,128)S(1)}, u32[]{:S(2)}, u32[]{:S(2)}) async-start(f32[32,64,128]{2,1,0:T(8,128)} %get-tuple-element.45.send), calls=%async_computation | async-start | bytes 2097152 | tf_op jit(solution)/shard_map/all_to_all | solution.py:393
  21.1 0.8 copy-start.12
  27.5 0.7 copy-start.3
  28.2 0.6 copy-start.5
  28.8 0.6 copy-start.7
  38.3 24.8 %copy-start.4 = (f32[264,128]{1,0:T(8,128)S(1)}, f32[264,128]{1,0:T(8,128)}, u32[]{:S(2)}) copy-start(f32[264,128]{1,0:T(8,128)} %copy-done.3) | copy-start | bytes 405508
  38.3 24.8 %copy-start.6 = (f32[264,128]{1,0:T(8,128)S(1)}, f32[264,128]{1,0:T(8,128)}, u32[]{:S(2)}) copy-start(f32[264,128]{1,0:T(8,128)} %copy-done.5) | copy-start | bytes 405508
  38.3 24.8 %copy-start.8 = (f32[264,128]{1,0:T(8,128)S(1)}, f32[264,128]{1,0:T(8,128)}, u32[]{:S(2)}) copy-start(f32[264,128]{1,0:T(8,128)} %copy-done.7) | copy-start | bytes 405508
  70.1 5.4 %collective-permute-start = (f32[96,128]{1,0:T(8,128)S(1)}, f32[96,128]{1,0:T(8,128)S(1)}, u32[]{:S(2)}, u32[]{:S(2)}) collective-permute-start(f32[96,128]{1,0:T(8,128)S(1)} %get-tuple-element.63.j0), channel_id=1, source_target_pairs={{0,1},{1,2},{2,3},{3,0},{4,5},{5,6},{6,7},{7,4},{8,9},{9,10},{10,1... | collective-permute-start | bytes 147464 | tf_op jit(solution)/shard_map/ppermute | solution.py:432
  71.3 4.8 %collective-permute-start.1 = (f32[96,128]{1,0:T(8,128)S(1)}, f32[96,128]{1,0:T(8,128)S(1)}, u32[]{:S(2)}, u32[]{:S(2)}) collective-permute-start(f32[96,128]{1,0:T(8,128)S(1)} %get-tuple-element.63.j0), channel_id=1, source_target_pairs={{0,2},{1,3},{2,0},{3,1},{4,6},{5,7},{6,4},{7,5},{8,10},{9,11},{10,... | collective-permute-start | bytes 147464 | tf_op jit(solution)/shard_map/ppermute | solution.py:432
  73.5 3.2 %collective-permute-start.2 = (f32[96,128]{1,0:T(8,128)S(1)}, f32[96,128]{1,0:T(8,128)S(1)}, u32[]{:S(2)}, u32[]{:S(2)}) collective-permute-start(f32[96,128]{1,0:T(8,128)S(1)} %get-tuple-element.63.j0), channel_id=1, source_target_pairs={{0,3},{1,0},{2,1},{3,2},{4,7},{5,4},{6,5},{7,6},{8,11},{9,8},{10,9... | collective-permute-start | bytes 147464 | tf_op jit(solution)/shard_map/ppermute | solution.py:432
  101.5 5.2 %collective-permute-start.3 = (f32[96,128]{1,0:T(8,128)S(1)}, f32[96,128]{1,0:T(8,128)S(1)}, u32[]{:S(2)}, u32[]{:S(2)}) collective-permute-start(f32[96,128]{1,0:T(8,128)S(1)} %get-tuple-element.72.j0), channel_id=1, source_target_pairs={{0,1},{1,2},{2,3},{3,0},{4,5},{5,6},{6,7},{7,4},{8,9},{9,10},{10,1... | collective-permute-start | bytes 147464 | tf_op jit(solution)/shard_map/ppermute | solution.py:432
  102.2 4.6 %collective-permute-start.4 = (f32[96,128]{1,0:T(8,128)S(1)}, f32[96,128]{1,0:T(8,128)S(1)}, u32[]{:S(2)}, u32[]{:S(2)}) collective-permute-start(f32[96,128]{1,0:T(8,128)S(1)} %get-tuple-element.72.j0), channel_id=1, source_target_pairs={{0,2},{1,3},{2,0},{3,1},{4,6},{5,7},{6,4},{7,5},{8,10},{9,11},{10,... | collective-permute-start | bytes 147464 | tf_op jit(solution)/shard_map/ppermute | solution.py:432
  104.5 3.2 %collective-permute-start.5 = (f32[96,128]{1,0:T(8,128)S(1)}, f32[96,128]{1,0:T(8,128)S(1)}, u32[]{:S(2)}, u32[]{:S(2)}) collective-permute-start(f32[96,128]{1,0:T(8,128)S(1)} %get-tuple-element.72.j0), channel_id=1, source_target_pairs={{0,3},{1,0},{2,1},{3,2},{4,7},{5,4},{6,5},{7,6},{8,11},{9,8},{10,9... | collective-permute-start | bytes 147464 | tf_op jit(solution)/shard_map/ppermute | solution.py:432
  133.3 5.5 %collective-permute-start.6 = (f32[96,128]{1,0:T(8,128)S(1)}, f32[96,128]{1,0:T(8,128)S(1)}, u32[]{:S(2)}, u32[]{:S(2)}) collective-permute-start(f32[96,128]{1,0:T(8,128)S(1)} %get-tuple-element.79.j0), channel_id=1, source_target_pairs={{0,1},{1,2},{2,3},{3,0},{4,5},{5,6},{6,7},{7,4},{8,9},{9,10},{10,1... | collective-permute-start | bytes 147464 | tf_op jit(solution)/shard_map/ppermute | solution.py:432
  133.4 5.4 %collective-permute-start.7 = (f32[96,128]{1,0:T(8,128)S(1)}, f32[96,128]{1,0:T(8,128)S(1)}, u32[]{:S(2)}, u32[]{:S(2)}) collective-permute-start(f32[96,128]{1,0:T(8,128)S(1)} %get-tuple-element.79.j0), channel_id=1, source_target_pairs={{0,2},{1,3},{2,0},{3,1},{4,6},{5,7},{6,4},{7,5},{8,10},{9,11},{10,... | collective-permute-start | bytes 147464 | tf_op jit(solution)/shard_map/ppermute | solution.py:432
  135.3 4.0 %collective-permute-start.8 = (f32[96,128]{1,0:T(8,128)S(1)}, f32[96,128]{1,0:T(8,128)S(1)}, u32[]{:S(2)}, u32[]{:S(2)}) collective-permute-start(f32[96,128]{1,0:T(8,128)S(1)} %get-tuple-element.79.j0), channel_id=1, source_target_pairs={{0,3},{1,0},{2,1},{3,2},{4,7},{5,4},{6,5},{7,6},{8,11},{9,8},{10,9... | collective-permute-start | bytes 147464 | tf_op jit(solution)/shard_map/ppermute | solution.py:432
  143.5 24.7 %copy-start.2 = (f32[32768]{0:T(1024)S(1)}, f32[32768]{0:T(1024)}, u32[]{:S(2)}) copy-start(f32[32768]{0:T(1024)} %param.14) | copy-start | bytes 393220
  164.9 7.3 %collective-permute-start.10 = (f32[96,128]{1,0:T(8,128)S(1)}, f32[96,128]{1,0:T(8,128)S(1)}, u32[]{:S(2)}, u32[]{:S(2)}) collective-permute-start(f32[96,128]{1,0:T(8,128)S(1)} %get-tuple-element.86.j0), channel_id=1, source_target_pairs={{0,2},{1,3},{2,0},{3,1},{4,6},{5,7},{6,4},{7,5},{8,10},{9,11},{10,... | collective-permute-start | bytes 147464 | tf_op jit(solution)/shard_map/ppermute | solution.py:432
  166.7 5.5 %collective-permute-start.11 = (f32[96,128]{1,0:T(8,128)S(1)}, f32[96,128]{1,0:T(8,128)S(1)}, u32[]{:S(2)}, u32[]{:S(2)}) collective-permute-start(f32[96,128]{1,0:T(8,128)S(1)} %get-tuple-element.86.j0), channel_id=1, source_target_pairs={{0,3},{1,0},{2,1},{3,2},{4,7},{5,4},{6,5},{7,6},{8,11},{9,8},{10,9... | collective-permute-start | bytes 147464 | tf_op jit(solution)/shard_map/ppermute | solution.py:432
  167.5 4.7 %collective-permute-start.9 = (f32[96,128]{1,0:T(8,128)S(1)}, f32[96,128]{1,0:T(8,128)S(1)}, u32[]{:S(2)}, u32[]{:S(2)}) collective-permute-start(f32[96,128]{1,0:T(8,128)S(1)} %get-tuple-element.86.j0), channel_id=1, source_target_pairs={{0,1},{1,2},{2,3},{3,0},{4,5},{5,6},{6,7},{7,4},{8,9},{9,10},{10,1... | collective-permute-start | bytes 147464 | tf_op jit(solution)/shard_map/ppermute | solution.py:432

commit v2 on v1

v2 whole, which is shorter than its diff:
```python
import functools

import jax
import jax.numpy as jnp
from jax import lax
from jax.experimental import pallas as pl
from jax.experimental.pallas import tpu as pltpu
from jax.sharding import PartitionSpec as P

ITERS = 4
relax = 0.1
F32 = jnp.float32
BF16 = jnp.bfloat16
LANES = 128
BLK = 8
PEERS = 32
HIGH = 16
ROWS = PEERS * BLK
STAGE = ROWS + 2 * BLK
CHUNK = 4
GROUPS = 2 * ROWS // 8 + CHUNK
STREAM = GROUPS * 8
COUNT = 2 * PEERS
PART = 4
VMEM = pl.BlockSpec(memory_space=pltpu.VMEM)
SMEM = pl.BlockSpec(memory_space=pltpu.SMEM)


def lane_iota():
    return lax.broadcasted_iota(jnp.int32, (8, LANES), 1)


def row_iota():
    return lax.broadcasted_iota(jnp.int32, (8, LANES), 0)


def pack_kernel(live, geom, first, second, target, warm, send, local, mixed, packed0, packed1):
    start = pl.program_id(0) * PART
    lanes = lane_iota()
    subs = row_iota()
    dead = jnp.where(subs == 4, -1.0, 0.0).astype(F32)

    def one_partner(q, _):
        rows = pl.ds(pl.multiple_of(q * BLK, BLK), BLK)
        mixed[pl.ds(4, 8, stride=8), :] = (second[rows, :] & (HIGH * LANES - 1)).astype(F32)
        mixed[pl.ds(5, 8, stride=8), :] = warm[rows, :]
        mixed[pl.ds(6, 8, stride=8), :] = target[rows, :]
        mixed[pl.ds(7, 8, stride=8), :] = (first[rows, :] & (HIGH * LANES - 1)).astype(F32)
        cols = [pl.ds(pl.multiple_of(q * BLK * LANES + b * LANES, LANES), LANES) for b in range(BLK)]
        for b in range(BLK):
            mixed[pl.ds(8 * b + 3, 1), :] = geom[8:9, cols[b]]
        offset = jnp.int32(0)
        cur0 = jnp.zeros((8, LANES), F32)
        cur1 = cur0
        for b in range(BLK):
            geo = geom[0:8, cols[b]]
            mix = mixed[8 * b : 8 * b + 8, :]
            shift = offset & (LANES - 1)
            row = offset >> 7
            rolled0 = pltpu.roll(jnp.where((subs >= 3) & (subs < 6), mix, geo), shift, 1)
            rolled1 = pltpu.roll(jnp.where(subs >= 6, mix, geo), shift, 1)
            keep = lanes < shift
            cur0 = jnp.where(keep, cur0, rolled0)
            cur1 = jnp.where(keep, cur1, rolled1)
            packed0[row] = cur0
            packed1[row] = cur1
            offset = offset + live[(start + q) * BLK + b]
            spill = jnp.broadcast_to((offset >> 7) > row, (8, LANES))
            cur0 = jnp.where(spill, rolled0, cur0)
            cur1 = jnp.where(spill, rolled1, cur1)
        packed0[offset >> 7] = cur0
        packed1[offset >> 7] = cur1
        for r in range(BLK):
            alive = lanes + r * LANES < offset
            send[q, 8 * r : 8 * r + 8, :] = jnp.where(alive, packed0[r], dead)
            local[q, 8 * r : 8 * r + 8, :] = jnp.where(alive, packed1[r], 0.0)
        return 0

    lax.fori_loop(0, PART, one_partner, 0)


def gather_rows(tables, index, count):
    lows = [i & (LANES - 1) for i in index]
    highs = [i >> 7 for i in index]
    found = [[None] * count for _ in index]
    for h in range(HIGH):
        masks = [hi == h for hi in highs]
        for c in range(count):
            ref, start = tables[c]
            line = jnp.broadcast_to(ref[start + h : start + h + 1, :], (8, LANES))
            for k in range(len(index)):
                got = jnp.take_along_axis(line, lows[k], axis=1, mode="promise_in_bounds")
                found[k][c] = got if h == 0 else jnp.where(masks[k], got, found[k][c])
    return found


def group_rows(g):
    return pl.ds(pl.multiple_of(g * 8, 8), 8)


def prepare(first, shift, total, d0, d1, vel, prop, x_out, idx_out, imp_out, u_out, m_out):
    def load(g):
        base = g * 64

        def get(ref, k):
            return ref[pl.ds(base + k, 8, stride=8), :]

        flag = get(d0, 4)
        alive = (flag >= 0.0) & (row_iota() + g * 8 < total)
        source, arms, index = (d1, (3, 4, 5), get(d1, 7)) if first else (d0, (6, 7, 3), flag)
        normal = [get(source, k) for k in (0, 1, 2)]
        arm = [get(source, k) for k in arms]
        cross = [
            arm[1] * normal[2] - arm[2] * normal[1],
            arm[2] * normal[0] - arm[0] * normal[2],
            arm[0] * normal[1] - arm[1] * normal[0],
        ]
        return get, alive, jnp.where(alive, index, 0.0).astype(jnp.int32), normal, cross

    def two_groups(pair, _):
        groups = [pair * 2, pair * 2 + 1]
        indices = [load(g)[2] for g in groups]
        masses = gather_rows([(prop, HIGH * c) for c in range(4)], indices, 4)
        for k, g in enumerate(groups):
            get, alive, index, normal, cross = load(g)
            mass = masses[k][0]
            for c in range(3):
                mass = mass + cross[c] * cross[c] * masses[k][1 + c]
            rows = group_rows(g + shift)
            m_out[rows, :] = jnp.where(alive, mass, -1.0)
            idx_out[rows, :] = index
            imp_out[rows, :] = jnp.where(alive, get(d0, 5), 0.0)
            sign = 1.0 if first else -1.0
            for c, term in enumerate(normal + cross):
                x_out[g + shift, c] = jnp.where(alive, sign * term, 0.0)
            x_out[g + shift, 6] = (
                jnp.where(alive, get(d1, 6), 0.0) if first else jnp.zeros((8, LANES), F32)
            )
        project(groups, shift, vel, x_out, idx_out, u_out)
        return 0

    lax.fori_loop(0, (total + 15) >> 4, two_groups, 0)


def project(groups, shift, vel, x, idx, u_out):
    rows = [group_rows(g + shift) for g in groups]
    got = gather_rows([(vel, HIGH * c) for c in range(6)], [idx[r, :] for r in rows], 6)
    for k, g in enumerate(groups):
        u = x[g + shift, 0] * got[k][0]
        for c in range(1, 6):
            u = u + x[g + shift, c] * got[k][c]
        u_out[rows[k], :] = u - x[g + shift, 6]


def first_kernel(
    live, send, local, velocity, properties,
    x_out, idx_out, imp_out, u_out, m_out, meta, share, vel, prop, d0, d1,
):
    for c in range(6):
        for h in range(HIGH):
            vel[c * HIGH + h : c * HIGH + h + 1, :] = velocity[c : c + 1, h * LANES : (h + 1) * LANES]
    for c in range(4):
        for h in range(HIGH):
            prop[c * HIGH + h : c * HIGH + h + 1, :] = properties[c : c + 1, h * LANES : (h + 1) * LANES]

    def one_partner(q, base):
        count = live[q * BLK]
        for b in range(1, BLK):
            count = count + live[q * BLK + b]
        meta[q] = base
        rows = pl.ds(pl.multiple_of(base * 8, 8), 64)
        d0[rows, :] = send[q]
        d1[rows, :] = local[q]
        return base + ((count + LANES - 1) >> 7)

    total = lax.fori_loop(0, PEERS, one_partner, jnp.int32(0))
    meta[PEERS] = total
    prepare(True, 0, total, d0, d1, vel, prop, x_out, idx_out, imp_out, u_out, m_out)

    def one_share(q, _):
        rows = pl.ds(meta[q], 8)
        share[q, 0] = u_out[rows, :]
        share[q, 1] = m_out[rows, :]
        return 0

    lax.fori_loop(0, PEERS, one_share, 0)


def second_kernel(
    received, share_first, vel, prop, meta_first, x_in, idx_in, imp_in, u_in, m_in,
    x_out, idx_out, imp_out, u_out, m_out, meta, share, d0, used,
):
    def count_rows(q, _):
        flags = received[q, pl.ds(4, 8, stride=8), :]
        used[q] = jnp.max(jnp.where(flags >= 0.0, row_iota() + 1, 0))
        return 0

    lax.fori_loop(0, PEERS, count_rows, 0, unroll=8)
    shift = (meta_first[PEERS] + 7) >> 3

    def one_partner(q, base):
        meta[q] = meta_first[q]
        meta[PEERS + q] = base + shift * 8
        d0[pl.ds(pl.multiple_of(base * 8, 8), 64), :] = received[q]
        return base + used[q]

    total = lax.fori_loop(0, PEERS, one_partner, jnp.int32(0))
    groups = shift + ((total + 7) >> 3)
    meta[COUNT] = groups
    prepare(False, shift, total, d0, None, vel, prop, x_out, idx_out, imp_out, u_out, m_out)
    zero = jnp.zeros((8, LANES), F32)
    for k in range(CHUNK):
        rows = group_rows(groups + k)
        for c in range(7):
            x_out[groups + k, c] = zero
        idx_out[rows, :] = zero.astype(jnp.int32)
        imp_out[rows, :] = zero
        u_out[rows, :] = zero
        m_out[rows, :] = zero - 1.0

    def one_share(q, _):
        rows = pl.ds(meta[PEERS + q], 8)
        share[q, 0] = share_first[q, 0]
        share[q, 1] = share_first[q, 1]
        share[q, 2] = u_out[rows, :]
        share[q, 3] = m_out[rows, :]
        return 0

    lax.fori_loop(0, PEERS, one_share, 0)


def apply_kernel(start, meta, x, idx, imp, u, w, received, *refs):
    if start:
        j_out, new, weight, other, mass = refs
    else:
        j_out, new, other = refs
        weight = w
    step = 2 if start else 1

    def one_partner(p, _):
        other[pl.ds(meta[p], 8), :] = received[p, step]
        if start:
            mass[pl.ds(meta[p], 8), :] = received[p, 3]
        return 0

    def second_partner(p, _):
        other[pl.ds(meta[PEERS + p], 8), :] = received[p, 0]
        if start:
            mass[pl.ds(meta[PEERS + p], 8), :] = received[p, 1]
        return 0

    lax.fori_loop(0, PEERS, one_partner, 0)
    lax.fori_loop(0, PEERS, second_partner, 0)
    iota_high = lax.broadcasted_iota(jnp.int32, (HIGH, LANES), 0)
    iota_low = lax.broadcasted_iota(jnp.int32, (LANES, LANES), 0)

    def one_chunk(i, total):
        lefts = []
        rights = []
        for j in range(CHUNK):
            g = i * CHUNK + j
            rows = group_rows(g)
            if start:
                mine = w[rows, :]
                alive = mine > 0.0
                scale = jnp.where(alive, relax / (mine + mass[rows, :]), 0.0)
                weight[rows, :] = scale
            else:
                scale = weight[rows, :]
                alive = scale > 0.0
            before = imp[rows, :]
            fresh = jnp.maximum(before - (u[rows, :] + other[rows, :]) * scale, 0.0)
            fresh = jnp.where(alive, fresh, before)
            applied = fresh - before
            new[rows, :] = fresh
            values = [applied * x[g, c] for c in range(6)]
            tops = [v.astype(BF16).astype(F32) for v in values]
            pieces = tops + [v - t for v, t in zip(values, tops)]
            index = idx[rows, :]
            low = index & (LANES - 1)
            high = index >> 7
            for b in range(8):
                mask = jnp.broadcast_to(high[b : b + 1], (HIGH, LANES)) == iota_high
                lefts.append(
                    jnp.concatenate(
                        [
                            jnp.where(mask, jnp.broadcast_to(v[b : b + 1], (HIGH, LANES)), 0.0).astype(BF16)
                            for v in pieces
                        ],
                        axis=0,
                    )
                )
                hit = jnp.broadcast_to(low[b : b + 1], (LANES, LANES)) == iota_low
                rights.append(jnp.where(hit, 1.0, 0.0).astype(BF16))
        return total + lax.dot_general(
            jnp.concatenate(lefts, axis=1),
            jnp.concatenate(rights, axis=1),
            (((1,), (1,)), ((), ())),
            preferred_element_type=F32,
        )

    chunks = (meta[COUNT] + CHUNK - 1) // CHUNK
    total = lax.fori_loop(0, chunks, one_chunk, jnp.zeros((12 * HIGH, LANES), F32))
    j_out[...] = total[0:96] + total[96:192]


def moved(vel, prop, j0, j1, j2, j3, c):
    rows = slice(c * HIGH, (c + 1) * HIGH)
    k = max(c - 2, 0)
    gain = (j0[rows, :] + j2[rows, :]) + (j1[rows, :] + j3[rows, :])
    return vel[rows, :] + prop[k * HIGH : (k + 1) * HIGH, :] * gain


def gather_kernel(meta, vel, prop, j0, j1, j2, j3, x, idx, vel_out, u_out, share):
    for c in range(6):
        vel_out[c * HIGH : (c + 1) * HIGH, :] = moved(vel, prop, j0, j1, j2, j3, c)

    def two_groups(pair, _):
        project([pair * 2, pair * 2 + 1], 0, vel_out, x, idx, u_out)
        return 0

    lax.fori_loop(0, (meta[COUNT] + 1) >> 1, two_groups, 0)

    def one_share(q, _):
        share[q, 0] = u_out[pl.ds(meta[q], 8), :]
        share[q, 1] = u_out[pl.ds(meta[PEERS + q], 8), :]
        return 0

    lax.fori_loop(0, PEERS, one_share, 0)


def final_kernel(vel, prop, j0, j1, j2, j3, out):
    for c in range(6):
        rows = moved(vel, prop, j0, j1, j2, j3, c)
        for h in range(HIGH):
            out[c : c + 1, h * LANES : (h + 1) * LANES] = rows[h : h + 1]


def unpack_kernel(live, meta, imp, warm, out):
    lanes = lax.broadcasted_iota(jnp.int32, (1, LANES), 1)

    def one_partner(q, _):
        offset = jnp.int32(0)
        for b in range(BLK):
            count = live[q * BLK + b]
            shift = offset & (LANES - 1)
            row = meta[q] + (offset >> 7)
            here = imp[pl.ds(row, 1), :]
            after = imp[pl.ds(row + 1, 1), :]
            both = jnp.where(lanes >= shift, here, after)
            back = pltpu.roll(both, (LANES - shift) & (LANES - 1), 1)
            slot = pl.ds(q * BLK + b, 1)
            out[slot, :] = jnp.where(lanes < count, back, warm[slot, :])
            offset = offset + count
        return 0

    lax.fori_loop(0, PEERS, one_partner, 0, unroll=2)


def shape(*dims, dtype=F32):
    return jax.ShapeDtypeStruct(dims, dtype)


def call(kernel, ins, outs, scratch=(), aliases=None, name=None):
    return pl.pallas_call(
        kernel,
        in_specs=list(ins),
        out_specs=tuple(SMEM if o.dtype == jnp.int32 and len(o.shape) == 1 else VMEM for o in outs),
        out_shape=tuple(outs),
        scratch_shapes=list(scratch),
        input_output_aliases=aliases or {},
        compiler_params=pltpu.CompilerParams(vmem_limit_bytes=16 << 20),
        cost_estimate=pl.CostEstimate(
            flops=10_000_000, bytes_accessed=4_000_000, transcendentals=0
        ),
        name=name,
    )


def pack(live, geometry, first, second, target, warm):
    rows = pl.BlockSpec((PART * BLK, LANES), lambda i: (i, 0))
    out = pl.BlockSpec((PART, 64, LANES), lambda i: (i, 0, 0))
    return pl.pallas_call(
        pack_kernel,
        grid=(PEERS // PART,),
        in_specs=[SMEM, pl.BlockSpec((9, PART * BLK * LANES), lambda i: (0, i))] + [rows] * 4,
        out_specs=(out, out),
        out_shape=(shape(PEERS, 64, LANES),) * 2,
        scratch_shapes=[pltpu.VMEM((64, LANES), F32)] + [pltpu.VMEM((16, 8, LANES), F32)] * 2,
        compiler_params=pltpu.CompilerParams(
            dimension_semantics=("arbitrary",), vmem_limit_bytes=60 << 20
        ),
        name="pack",
    )(live, geometry, first, second, target, warm)


def on_device(
    velocity, properties, first_body, second_body, geometry, target_speed, warm_impulse, live_pairs
):
    table = lambda array: array.reshape(ROWS, LANES)
    warm = table(warm_impulse)
    stream = shape(STREAM, LANES)
    streams = [
        shape(GROUPS, 7, 8, LANES), shape(STREAM, LANES, dtype=jnp.int32), stream, stream, stream
    ]
    send, local = pack(
        live_pairs, geometry, table(first_body), table(second_body), table(target_speed), warm
    )
    received = lax.all_to_all(send, "owner", split_axis=0, concat_axis=0, tiled=True)
    x, idx, imp, u, m, meta_first, share, vel, prop = call(
        first_kernel,
        [SMEM] + [VMEM] * 4,
        streams
        + [
            shape(PEERS + 1, dtype=jnp.int32), shape(PEERS, 2, 8, LANES),
            shape(96, LANES), shape(64, LANES),
        ],
        [pltpu.VMEM((STAGE * 8, LANES), F32)] * 2,
        name="first",
    )(live_pairs, send, local, velocity, properties)
    x, idx, imp, u, m, meta, share = call(
        second_kernel,
        [VMEM] * 4 + [SMEM] + [VMEM] * 5,
        streams + [shape(COUNT + 1, dtype=jnp.int32), shape(PEERS, 4, 8, LANES)],
        [pltpu.VMEM((STAGE * 8, LANES), F32), pltpu.SMEM((PEERS,), jnp.int32)],
        aliases={5 + k: k for k in range(5)},
        name="second",
    )(received, share, vel, prop, meta_first, x, idx, imp, u, m)
    weight = m
    n_sub = lax.axis_size("sub")
    for iteration in range(ITERS):
        start = iteration == 0
        told = lax.all_to_all(share, "owner", split_axis=0, concat_axis=0, tiled=True)
        outs = call(
            functools.partial(apply_kernel, start),
            [SMEM] + [VMEM] * 6,
            [shape(96, LANES), stream] + ([stream] if start else []),
            [pltpu.VMEM((STREAM, LANES), F32)] * (2 if start else 1),
            name="apply",
        )(meta, x, idx, imp, u, weight, told)
        own, imp = outs[:2]
        if start:
            weight = outs[2]
        gains = [own] + [
            lax.ppermute(own, "sub", [(i, (i + d) % n_sub) for i in range(n_sub)])
            for d in (1, 2, 3)
        ]
        if iteration < ITERS - 1:
            vel, u, share = call(
                gather_kernel,
                [SMEM] + [VMEM] * 8,
                [shape(96, LANES), stream, shape(PEERS, 2, 8, LANES)],
                name="gather",
            )(meta, vel, prop, *gains, x, idx)
    (impulse,) = call(
        unpack_kernel, [SMEM, SMEM, VMEM, VMEM], [shape(ROWS, LANES)], name="unpack"
    )(live_pairs, meta, imp, warm)
    (out,) = call(final_kernel, [VMEM] * 6, [shape(6, HIGH * LANES)], name="final")(
        vel, prop, *gains
    )
    return (out, impulse.reshape(-1))


def solution(mesh):
    return jax.shard_map(
        on_device,
        mesh=mesh,
        in_specs=(
            P(None, "owner"),
            P(None, "owner"),
            P(("owner", "sub")),
            P(("owner", "sub")),
            P(None, ("owner", "sub")),
            P(("owner", "sub")),
            P(("owner", "sub")),
            P(("owner", "sub")),
        ),
        out_specs=(P(None, "owner"), P(("owner", "sub"))),
        check_vma=False,
    )
```

time: 173 us -> 162 us (0.936)
  Pallas kernels: 66.3 us -> 51.8 us
  starting transfers between devices: 26.8 us -> 18.5 us
  waiting for transfers between devices: 13.7 us -> 19 us
  local copies, waits for them, and re-layouts: 8.69 us -> 13.8 us
    pallas_call x10, Pallas kernels: 61.7 us -> 48.3 us  [the longest x4 18 us: on_device(): call(functools.partial(apply_kernel, start), [SMEM] + [VMEM] * 6, [shape(...]
    ppermute x12, waiting for transfers between devices: 4.92 us -> 16.2 us  [on_device(): lax.ppermute(own, 'sub', [(i, (i + d) % n_sub) for i in range(n_sub)])]
    ppermute x12, starting transfers between devices: 17.2 us -> 8.88 us  [on_device(): lax.ppermute(own, 'sub', [(i, (i + d) % n_sub) for i in range(n_sub)])]
    all_to_all x1, waiting for transfers between devices: 8.8 us -> 2.84 us  [on_device(): lax.all_to_all(send, 'owner', split_axis=0, concat_axis=0, tiled=True)]
    unnamed x32 -> x42, local copies, waits for them, and re-layouts: 8.69 us -> 13.8 us
  transfers between devices with their start and end apart: 13 -> 13, of which waited for: 7 -> 12; matrix products, arithmetic and copies ran while one was open for 0% -> 0% of each run, Pallas kernels for 6% -> 5%
where the time goes in v2:
time: 162 us; the launch traced here: 160 us
  blocking collectives  56.4 us (35%)
  Pallas kernels  51.8 us (32%)
  waiting for transfers between devices  19 us (12%)
  starting transfers between devices  18.5 us (11%)
  local copies, waits for them, and re-layouts  13.8 us (9%)
    all_to_all x4, blocking collectives, on_device(): lax.all_to_all(share, 'owner', split_axis=0, concat_axis=0, tiled=True)  56.4 us
    pallas_call x4, Pallas kernels, on_device(): call(functools.partial(apply_kernel, start), [SMEM] + [VMEM] * 6, [shape(...  18 us
    ppermute x12, waiting for transfers between devices, on_device(): lax.ppermute(own, 'sub', [(i, (i + d) % n_sub) for i in range(n_sub)])  16.2 us
    unnamed x42, local copies, waits for them, and re-layouts  13.8 us
    pallas_call x3, Pallas kernels, on_device(): call(gather_kernel, [SMEM] + [VMEM] * 8, [shape(96, LANES), stream, shape...  11.6 us
    all_to_all x1, starting transfers between devices, on_device(): lax.all_to_all(send, 'owner', split_axis=0, concat_axis=0, tiled=True)  9.6 us
    ppermute x12, starting transfers between devices, on_device(): lax.ppermute(own, 'sub', [(i, (i + d) % n_sub) for i in range(n_sub)])  8.88 us
    pallas_call x1, Pallas kernels, pack(): pl.pallas_call(pack_kernel, grid=(PEERS // PART,), in_specs=[SMEM, pl.Blo...  7.45 us
  transfers between devices with their start and end apart: 13, of which 12 were waited for; matrix products, arithmetic and copies ran while one was open for 0% of the time, Pallas kernels for 5%

profile of v2, /device:TPU:1, one launch (start us, length us, event | category | flops | bytes accessed | tf_op | source)
XLA Modules:
  0.0 160.2 jit_solution(1073726967782693437)
XLA Ops:
  0.6 7.5 %pack.1 = (f32[32,64,128]{2,1,0:T(8,128)}, f32[32,64,128]{2,1,0:T(8,128)}) custom-call(s32[256]{0:T(256)} %live.5, f32[9,32768]{1,0:T(8,128)} %geom.1, s32[256,128]{1,0:T(8,128)} %bitcast.7, s32[256,128]{1,0:T(8,128)} %bitcast.8, f32[256,128]{1,0:T(8,128)} %bitcast.9, f32[256,128]{1,0:T(8,128)} %bitcast.5), custom_call_target="tpu_custom_call" | custom-call | tf_op jit(solution)/shard_map/pack/pallas_call | solution.py:383
  8.1 9.6 %all-to-all-start = ((f32[32,64,128]{2,1,0:T(8,128)}), f32[32,64,128]{2,1,0:T(8,128)S(1)}, u32[]{:S(2)}, u32[]{:S(2)}) async-start(f32[32,64,128]{2,1,0:T(8,128)} %get-tuple-element.38.send), calls=%async_computation | async-start | bytes 2097152 | tf_op jit(solution)/shard_map/all_to_all | solution.py:409
  17.7 0.0 copy-start
  17.7 1.2 copy-done
  18.9 1.2 copy-done.5
  20.2 0.8 copy-done.15
  21.0 0.8 copy-done.16
  21.8 0.7 copy-done.17
  22.5 5.6 %first.1 = (f32[68,7,8,128]{3,2,1,0:T(8,128)S(1)}, s32[544,128]{1,0:T(8,128)S(1)}, f32[544,128]{1,0:T(8,128)S(1)}, f32[544,128]{1,0:T(8,128)S(1)}, f32[544,128]{...) custom-call(s32[256]{0:T(256)S(1)} %copy-done.17, ...), custom_call_target="tpu_custom_call" | custom-call | flops 10000000 | bytes 4000000 | tf_op jit(solution)/shard_map/first/pallas_call | solution.py:410
  28.0 0.0 copy-start.1
  28.1 0.7 copy-done.1
  28.8 0.7 copy-done.3
  29.5 0.6 copy-done.6
  30.1 0.7 copy-done.10
  30.8 0.6 copy-done.12
  31.4 0.6 copy-done.19
  32.0 2.8 %all-to-all-done.received = f32[32,64,128]{2,1,0:T(8,128)S(1)} async-done(((f32[32,64,128]{2,1,0:T(8,128)}), f32[32,64,128]{2,1,0:T(8,128)S(1)}, u32[]{:S(2)}, u32[]{:S(2)}) %all-to-all-start) | async-done | bytes 1048608 | tf_op jit(solution)/shard_map/all_to_all | solution.py:409
  34.9 1.0 copy-done.2
  35.8 1.0 copy-done.4
  36.8 0.8 copy-done.7
  37.5 0.9 copy-done.11
  38.5 0.8 copy-done.13
  39.3 0.7 copy-done.20
  40.0 5.6 %second.1 = (f32[68,7,8,128]{3,2,1,0:T(8,128)S(1)}, s32[544,128]{1,0:T(8,128)S(1)}, f32[544,128]{1,0:T(8,128)S(1)}, f32[544,128]{1,0:T(8,128)S(1)}, f32[544,128]...) custom-call(f32[32,64,128]{2,1,0:T(8,128)S(1)} %all-to-all-done.rece, ...), custom_call_target="tpu_custom_call", output_to_operand_aliasing={{0}: (5, {}), {1}: (6, {}), {2}: (7, {}), {3}: (8, {}), {4}... | custom-call | flops 10000000 | bytes 4000000 | tf_op jit(solution)/shard_map/second/pallas_call | solution.py:421
  45.6 16.3 %all_to_all.25.received = f32[32,4,8,128]{3,2,1,0:T(8,128)S(1)} all-to-all(f32[32,4,8,128]{3,2,1,0:T(8,128)S(1)} %get-tuple-element.55), channel_id=1, replica_groups=mesh['owner'=32,'sub'=4] {'owner'}, dimensions={0} | all-to-all | bytes 1048576 | tf_op jit(solution)/shard_map/all_to_all | solution.py:433
  61.9 4.5 %apply.4 = (f32[96,128]{1,0:T(8,128)S(1)}, f32[544,128]{1,0:T(8,128)S(1)}, f32[544,128]{1,0:T(8,128)S(1)}) custom-call(s32[65]{0:T(128)S(1)} %get-tuple-element.49.meta, f32[68,7,8,128]{3,2,1,0:T(8,128)S(1)} %get-tuple-element.50.x, s32[544,128]{1,0:T(8,128)S(1)} %get-tuple-element.51.idx, f32[544,128]{1,0:T(8,128)S(1)} %get-tuple-element.52.imp, ...), custom_call_target="tpu_custom_call" | custom-call | flops 10000000 | bytes 4000000 | tf_op jit(solution)/shard_map/apply/pallas_call | solution.py:434
  66.4 2.9 %collective-permute-start.2 = (f32[96,128]{1,0:T(8,128)S(1)}, f32[96,128]{1,0:T(8,128)S(1)}, u32[]{:S(2)}, u32[]{:S(2)}) collective-permute-start(f32[96,128]{1,0:T(8,128)S(1)} %get-tuple-element.56.j0), channel_id=1, source_target_pairs={{0,3},{1,0},{2,1},{3,2},{4,7},{5,4},{6,5},{7,6},{8,11},{9,8},{10,9... | collective-permute-start | bytes 147464 | tf_op jit(solution)/shard_map/ppermute | solution.py:445
  69.3 0.0 collective-permute-start.1
  69.3 0.7 collective-permute-start
  70.0 0.5 collective-permute-done.2.j3
  70.5 3.4 %collective-permute-done.1.j2 = f32[96,128]{1,0:T(8,128)S(1)} collective-permute-done((f32[96,128]{1,0:T(8,128)S(1)}, f32[96,128]{1,0:T(8,128)S(1)}, u32[]{:S(2)}, u32[]{:S(2)}) %collective-permute-start.1) | collective-permute-done | bytes 49184 | tf_op jit(solution)/shard_map/ppermute | solution.py:445
  73.9 0.1 collective-permute-done.j1
  74.0 3.9 %gather.3 = (f32[96,128]{1,0:T(8,128)S(1)}, f32[544,128]{1,0:T(8,128)S(1)}, f32[32,2,8,128]{3,2,1,0:T(8,128)S(1)}) custom-call(s32[65]{0:T(128)S(1)} %get-tuple-element.49.meta, f32[96,128]{1,0:T(8,128)S(1)} %copy-done.14, f32[64,128]{1,0:T(8,128)S(1)} %copy-done.8, f32[96,128]{1,0:T(8,128)S(1)} %get-tuple-element.56.j0, ...), custom_call_target="tpu_custom_call" | custom-call | flops 10000000 | bytes 4000000 | tf_op jit(solution)/shard_map/gather/pallas_call | solution.py:449
  77.9 14.2 %all_to_all.26.received = f32[32,2,8,128]{3,2,1,0:T(8,128)S(1)} all-to-all(f32[32,2,8,128]{3,2,1,0:T(8,128)S(1)} %get-tuple-element.61), channel_id=1, replica_groups=mesh['owner'=32,'sub'=4] {'owner'}, dimensions={0} | all-to-all | bytes 524288 | tf_op jit(solution)/shard_map/all_to_all | solution.py:433
  92.0 4.5 %apply.5 = (f32[96,128]{1,0:T(8,128)S(1)}, f32[544,128]{1,0:T(8,128)S(1)}) custom-call(s32[65]{0:T(128)S(1)} %get-tuple-element.49.meta, f32[68,7,8,128]{3,2,1,0:T(8,128)S(1)} %get-tuple-element.50.x, s32[544,128]{1,0:T(8,128)S(1)} %get-tuple-element.51.idx, f32[544,128]{1,0:T(8,128)S(1)} %get-tuple-element.58.imp, f32[544,128]{1,0:T(8,128)S(1)} %get-tuple-element.59.u, ...), custom_call_target="tpu_custom_call" | custom-call | flops 10000000 | bytes 4000000 | tf_op jit(solution)/shard_map/apply/pallas_call | solution.py:434
  96.5 0.5 collective-permute-start.5
  97.0 0.9 collective-permute-start.4
  97.9 0.3 collective-permute-start.3
  98.2 1.3 collective-permute-done.5.j3
  99.5 1.9 %collective-permute-done.4.j2 = f32[96,128]{1,0:T(8,128)S(1)} collective-permute-done((f32[96,128]{1,0:T(8,128)S(1)}, f32[96,128]{1,0:T(8,128)S(1)}, u32[]{:S(2)}, u32[]{:S(2)}) %collective-permute-start.4) | collective-permute-done | bytes 49184 | tf_op jit(solution)/shard_map/ppermute | solution.py:445
  101.5 1.5 collective-permute-done.3.j1
  102.9 3.9 %gather.4 = (f32[96,128]{1,0:T(8,128)S(1)}, f32[544,128]{1,0:T(8,128)S(1)}, f32[32,2,8,128]{3,2,1,0:T(8,128)S(1)}) custom-call(s32[65]{0:T(128)S(1)} %get-tuple-element.49.meta, f32[96,128]{1,0:T(8,128)S(1)} %get-tuple-element.57.vel, f32[64,128]{1,0:T(8,128)S(1)} %copy-done.8, f32[96,128]{1,0:T(8,128)S(1)} %get-tuple-element.62.j0, ...), custom_call_target="tpu_custom_call" | custom-call | flops 10000000 | bytes 4000000 | tf_op jit(solution)/shard_map/gather/pallas_call | solution.py:449
  106.8 13.2 %all_to_all.27.received = f32[32,2,8,128]{3,2,1,0:T(8,128)S(1)} all-to-all(f32[32,2,8,128]{3,2,1,0:T(8,128)S(1)} %get-tuple-element.66), channel_id=1, replica_groups=mesh['owner'=32,'sub'=4] {'owner'}, dimensions={0} | all-to-all | bytes 524288 | tf_op jit(solution)/shard_map/all_to_all | solution.py:433
  120.0 4.5 %apply.6 = (f32[96,128]{1,0:T(8,128)S(1)}, f32[544,128]{1,0:T(8,128)S(1)}) custom-call(s32[65]{0:T(128)S(1)} %get-tuple-element.49.meta, f32[68,7,8,128]{3,2,1,0:T(8,128)S(1)} %get-tuple-element.50.x, s32[544,128]{1,0:T(8,128)S(1)} %get-tuple-element.51.idx, f32[544,128]{1,0:T(8,128)S(1)} %get-tuple-element.64.imp, f32[544,128]{1,0:T(8,128)S(1)} %get-tuple-element.65.u, ...), custom_call_target="tpu_custom_call" | custom-call | flops 10000000 | bytes 4000000 | tf_op jit(solution)/shard_map/apply/pallas_call | solution.py:434
  124.5 1.3 collective-permute-start.8
  125.7 0.3 collective-permute-start.7
  126.1 0.3 collective-permute-start.6
  126.4 1.1 collective-permute-done.8.j3
  127.5 2.7 %collective-permute-done.7.j2 = f32[96,128]{1,0:T(8,128)S(1)} collective-permute-done((f32[96,128]{1,0:T(8,128)S(1)}, f32[96,128]{1,0:T(8,128)S(1)}, u32[]{:S(2)}, u32[]{:S(2)}) %collective-permute-start.7) | collective-permute-done | bytes 49184 | tf_op jit(solution)/shard_map/ppermute | solution.py:445
  130.2 1.5 collective-permute-done.6.j1
  131.7 3.9 %gather.5 = (f32[96,128]{1,0:T(8,128)S(1)}, f32[544,128]{1,0:T(8,128)S(1)}, f32[32,2,8,128]{3,2,1,0:T(8,128)S(1)}) custom-call(s32[65]{0:T(128)S(1)} %get-tuple-element.49.meta, f32[96,128]{1,0:T(8,128)S(1)} %get-tuple-element.63.vel, f32[64,128]{1,0:T(8,128)S(1)} %copy-done.8, f32[96,128]{1,0:T(8,128)S(1)} %get-tuple-element.67.j0, ...), custom_call_target="tpu_custom_call" | custom-call | flops 10000000 | bytes 4000000 | tf_op jit(solution)/shard_map/gather/pallas_call | solution.py:449
  135.6 0.0 copy-start.9
  135.6 0.0 copy-start.18
  135.6 12.8 %all_to_all.28.received = f32[32,2,8,128]{3,2,1,0:T(8,128)S(1)} all-to-all(f32[32,2,8,128]{3,2,1,0:T(8,128)S(1)} %get-tuple-element.71), channel_id=1, replica_groups=mesh['owner'=32,'sub'=4] {'owner'}, dimensions={0} | all-to-all | bytes 524288 | tf_op jit(solution)/shard_map/all_to_all | solution.py:433
  148.4 4.5 %apply.7 = (f32[96,128]{1,0:T(8,128)S(1)}, f32[544,128]{1,0:T(8,128)S(1)}) custom-call(s32[65]{0:T(128)S(1)} %get-tuple-element.49.meta, f32[68,7,8,128]{3,2,1,0:T(8,128)S(1)} %get-tuple-element.50.x, s32[544,128]{1,0:T(8,128)S(1)} %get-tuple-element.51.idx, f32[544,128]{1,0:T(8,128)S(1)} %get-tuple-element.69.imp, f32[544,128]{1,0:T(8,128)S(1)} %get-tuple-element.70.u, ...), custom_call_target="tpu_custom_call" | custom-call | flops 10000000 | bytes 4000000 | tf_op jit(solution)/shard_map/apply/pallas_call | solution.py:434
  152.9 0.9 collective-permute-start.11
  153.8 0.2 collective-permute-start.10
  154.1 0.5 collective-permute-start.9
  154.6 0.0 copy-done.18
  154.6 2.9 %unpack.1 = f32[256,128]{1,0:T(8,128)} custom-call(s32[256]{0:T(256)S(1)} %copy-done.18, s32[65]{0:T(128)S(1)} %get-tuple-element.49.meta, f32[544,128]{1,0:T(8,128)S(1)} %get-tuple-element.73.imp, f32[256,128]{1,0:T(8,128)S(1)} %bitcast.6), custom_call_target="tpu_custom_call" | custom-call | flops 10000000 | bytes 4000000 | tf_op jit(solution)/shard_map/unpack/pallas_call | solution.py:455
  157.5 0.0 collective-permute-done.11.j3
  157.5 0.8 collective-permute-done.10.j2
  158.3 1.2 collective-permute-done.9.j1
  159.5 0.7 final.1
  (20 shorter events, 0.0 us)
Async XLA Ops:
  8.1 26.8 %all-to-all-start = ((f32[32,64,128]{2,1,0:T(8,128)}), f32[32,64,128]{2,1,0:T(8,128)S(1)}, u32[]{:S(2)}, u32[]{:S(2)}) async-start(f32[32,64,128]{2,1,0:T(8,128)} %get-tuple-element.38.send), calls=%async_computation | async-start | bytes 2097152 | tf_op jit(solution)/shard_map/all_to_all | solution.py:409
  17.7 1.3 copy-start
  18.9 1.2 copy-start.5
  20.2 0.8 copy-start.15
  21.0 0.8 copy-start.16
  21.8 0.7 copy-start.17
  28.0 0.7 copy-start.1
  28.8 0.7 copy-start.3
  29.5 0.6 copy-start.6
  30.1 0.7 copy-start.10
  30.8 0.6 copy-start.12
  31.4 0.6 copy-start.19
  34.9 1.0 copy-start.2
  35.8 1.0 copy-start.4
  36.8 0.8 copy-start.7
  37.5 0.9 copy-start.11
  38.5 0.8 copy-start.13
  39.3 0.7 copy-start.20
  61.8 12.1 %copy-start.8 = (f32[64,128]{1,0:T(8,128)S(1)}, f32[64,128]{1,0:T(8,128)}, u32[]{:S(2)}) copy-start(f32[64,128]{1,0:T(8,128)} %copy-done.6) | copy-start | bytes 98308
  61.8 12.2 %copy-start.14 = (f32[96,128]{1,0:T(8,128)S(1)}, f32[96,128]{1,0:T(8,128)}, u32[]{:S(2)}) copy-start(f32[96,128]{1,0:T(8,128)} %copy-done.12) | copy-start | bytes 147460
  66.4 4.1 %collective-permute-start.2 = (f32[96,128]{1,0:T(8,128)S(1)}, f32[96,128]{1,0:T(8,128)S(1)}, u32[]{:S(2)}, u32[]{:S(2)}) collective-permute-start(f32[96,128]{1,0:T(8,128)S(1)} %get-tuple-element.56.j0), channel_id=1, source_target_pairs={{0,3},{1,0},{2,1},{3,2},{4,7},{5,4},{6,5},{7,6},{8,11},{9,8},{10,9... | collective-permute-start | bytes 147464 | tf_op jit(solution)/shard_map/ppermute | solution.py:445
  69.3 4.5 %collective-permute-start.1 = (f32[96,128]{1,0:T(8,128)S(1)}, f32[96,128]{1,0:T(8,128)S(1)}, u32[]{:S(2)}, u32[]{:S(2)}) collective-permute-start(f32[96,128]{1,0:T(8,128)S(1)} %get-tuple-element.56.j0), channel_id=1, source_target_pairs={{0,2},{1,3},{2,0},{3,1},{4,6},{5,7},{6,4},{7,5},{8,10},{9,11},{10,... | collective-permute-start | bytes 147464 | tf_op jit(solution)/shard_map/ppermute | solution.py:445
  69.3 4.7 %collective-permute-start = (f32[96,128]{1,0:T(8,128)S(1)}, f32[96,128]{1,0:T(8,128)S(1)}, u32[]{:S(2)}, u32[]{:S(2)}) collective-permute-start(f32[96,128]{1,0:T(8,128)S(1)} %get-tuple-element.56.j0), channel_id=1, source_target_pairs={{0,1},{1,2},{2,3},{3,0},{4,5},{5,6},{6,7},{7,4},{8,9},{9,10},{10,1... | collective-permute-start | bytes 147464 | tf_op jit(solution)/shard_map/ppermute | solution.py:445
  96.5 3.0 %collective-permute-start.5 = (f32[96,128]{1,0:T(8,128)S(1)}, f32[96,128]{1,0:T(8,128)S(1)}, u32[]{:S(2)}, u32[]{:S(2)}) collective-permute-start(f32[96,128]{1,0:T(8,128)S(1)} %get-tuple-element.62.j0), channel_id=1, source_target_pairs={{0,3},{1,0},{2,1},{3,2},{4,7},{5,4},{6,5},{7,6},{8,11},{9,8},{10,9... | collective-permute-start | bytes 147464 | tf_op jit(solution)/shard_map/ppermute | solution.py:445
  97.0 4.4 %collective-permute-start.4 = (f32[96,128]{1,0:T(8,128)S(1)}, f32[96,128]{1,0:T(8,128)S(1)}, u32[]{:S(2)}, u32[]{:S(2)}) collective-permute-start(f32[96,128]{1,0:T(8,128)S(1)} %get-tuple-element.62.j0), channel_id=1, source_target_pairs={{0,2},{1,3},{2,0},{3,1},{4,6},{5,7},{6,4},{7,5},{8,10},{9,11},{10,... | collective-permute-start | bytes 147464 | tf_op jit(solution)/shard_map/ppermute | solution.py:445
  97.9 5.0 %collective-permute-start.3 = (f32[96,128]{1,0:T(8,128)S(1)}, f32[96,128]{1,0:T(8,128)S(1)}, u32[]{:S(2)}, u32[]{:S(2)}) collective-permute-start(f32[96,128]{1,0:T(8,128)S(1)} %get-tuple-element.62.j0), channel_id=1, source_target_pairs={{0,1},{1,2},{2,3},{3,0},{4,5},{5,6},{6,7},{7,4},{8,9},{9,10},{10,1... | collective-permute-start | bytes 147464 | tf_op jit(solution)/shard_map/ppermute | solution.py:445
  124.5 3.0 %collective-permute-start.8 = (f32[96,128]{1,0:T(8,128)S(1)}, f32[96,128]{1,0:T(8,128)S(1)}, u32[]{:S(2)}, u32[]{:S(2)}) collective-permute-start(f32[96,128]{1,0:T(8,128)S(1)} %get-tuple-element.67.j0), channel_id=1, source_target_pairs={{0,3},{1,0},{2,1},{3,2},{4,7},{5,4},{6,5},{7,6},{8,11},{9,8},{10,9... | collective-permute-start | bytes 147464 | tf_op jit(solution)/shard_map/ppermute | solution.py:445
  125.7 4.5 %collective-permute-start.7 = (f32[96,128]{1,0:T(8,128)S(1)}, f32[96,128]{1,0:T(8,128)S(1)}, u32[]{:S(2)}, u32[]{:S(2)}) collective-permute-start(f32[96,128]{1,0:T(8,128)S(1)} %get-tuple-element.67.j0), channel_id=1, source_target_pairs={{0,2},{1,3},{2,0},{3,1},{4,6},{5,7},{6,4},{7,5},{8,10},{9,11},{10,... | collective-permute-start | bytes 147464 | tf_op jit(solution)/shard_map/ppermute | solution.py:445
  126.1 5.7 %collective-permute-start.6 = (f32[96,128]{1,0:T(8,128)S(1)}, f32[96,128]{1,0:T(8,128)S(1)}, u32[]{:S(2)}, u32[]{:S(2)}) collective-permute-start(f32[96,128]{1,0:T(8,128)S(1)} %get-tuple-element.67.j0), channel_id=1, source_target_pairs={{0,1},{1,2},{2,3},{3,0},{4,5},{5,6},{6,7},{7,4},{8,9},{9,10},{10,1... | collective-permute-start | bytes 147464 | tf_op jit(solution)/shard_map/ppermute | solution.py:445
  135.6 19.0 %copy-start.9 = (f32[32768]{0:T(1024)S(1)}, f32[32768]{0:T(1024)}, u32[]{:S(2)}) copy-start(f32[32768]{0:T(1024)} %param.14) | copy-start | bytes 393220
  135.6 19.0 %copy-start.18 = (s32[256]{0:T(256)S(1)}, s32[256]{0:T(256)}, u32[]{:S(2)}) copy-start(s32[256]{0:T(256)} %live.5) | copy-start | bytes 3076
  152.9 4.6 %collective-permute-start.11 = (f32[96,128]{1,0:T(8,128)S(1)}, f32[96,128]{1,0:T(8,128)S(1)}, u32[]{:S(2)}, u32[]{:S(2)}) collective-permute-start(f32[96,128]{1,0:T(8,128)S(1)} %get-tuple-element.72.j0), channel_id=1, source_target_pairs={{0,3},{1,0},{2,1},{3,2},{4,7},{5,4},{6,5},{7,6},{8,11},{9,8},{10,9... | collective-permute-start | bytes 147464 | tf_op jit(solution)/shard_map/ppermute | solution.py:445
  153.8 4.5 %collective-permute-start.10 = (f32[96,128]{1,0:T(8,128)S(1)}, f32[96,128]{1,0:T(8,128)S(1)}, u32[]{:S(2)}, u32[]{:S(2)}) collective-permute-start(f32[96,128]{1,0:T(8,128)S(1)} %get-tuple-element.72.j0), channel_id=1, source_target_pairs={{0,2},{1,3},{2,0},{3,1},{4,6},{5,7},{6,4},{7,5},{8,10},{9,11},{10,... | collective-permute-start | bytes 147464 | tf_op jit(solution)/shard_map/ppermute | solution.py:445
  154.1 5.5 %collective-permute-start.9 = (f32[96,128]{1,0:T(8,128)S(1)}, f32[96,128]{1,0:T(8,128)S(1)}, u32[]{:S(2)}, u32[]{:S(2)}) collective-permute-start(f32[96,128]{1,0:T(8,128)S(1)} %get-tuple-element.72.j0), channel_id=1, source_target_pairs={{0,1},{1,2},{2,3},{3,0},{4,5},{5,6},{6,7},{7,4},{8,9},{9,10},{10,1... | collective-permute-start | bytes 147464 | tf_op jit(solution)/shard_map/ppermute | solution.py:445

commit v3 on v2

--- a/solution.py
+++ b/solution.py
@@ -17,11 +17,12 @@
 HIGH = 16
 ROWS = PEERS * BLK
 STAGE = ROWS + 2 * BLK
-CHUNK = 4
+HALF = float(1 << 20)
+CHUNK = 6
 GROUPS = 2 * ROWS // 8 + CHUNK
 STREAM = GROUPS * 8
 COUNT = 2 * PEERS
-PART = 4
+PART = 8
 VMEM = pl.BlockSpec(memory_space=pltpu.VMEM)
 SMEM = pl.BlockSpec(memory_space=pltpu.SMEM)
 
@@ -34,13 +35,13 @@
     return lax.broadcasted_iota(jnp.int32, (8, LANES), 0)
 
 
-def pack_kernel(live, geom, first, second, target, warm, send, local, mixed, packed0, packed1):
+def pack_kernel(live, geom, first, second, target, warm, send, local, *scratch):
     start = pl.program_id(0) * PART
     lanes = lane_iota()
     subs = row_iota()
     dead = jnp.where(subs == 4, -1.0, 0.0).astype(F32)
 
-    def one_partner(q, _):
+    def one_partner(q, mixed, packed0, packed1):
         rows = pl.ds(pl.multiple_of(q * BLK, BLK), BLK)
         mixed[pl.ds(4, 8, stride=8), :] = (second[rows, :] & (HIGH * LANES - 1)).astype(F32)
         mixed[pl.ds(5, 8, stride=8), :] = warm[rows, :]
@@ -74,9 +75,13 @@
             alive = lanes + r * LANES < offset
             send[q, 8 * r : 8 * r + 8, :] = jnp.where(alive, packed0[r], dead)
             local[q, 8 * r : 8 * r + 8, :] = jnp.where(alive, packed1[r], 0.0)
-        return 0
-
-    lax.fori_loop(0, PART, one_partner, 0)
+
+    def two_partners(pair, _):
+        one_partner(pair * 2, *scratch[0::2])
+        one_partner(pair * 2 + 1, *scratch[1::2])
+        return 0
+
+    lax.fori_loop(0, PART // 2, two_partners, 0)
 
 
 def gather_rows(tables, index, count):
@@ -98,7 +103,38 @@
     return pl.ds(pl.multiple_of(g * 8, 8), 8)
 
 
-def prepare(first, shift, total, d0, d1, vel, prop, x_out, idx_out, imp_out, u_out, m_out):
+def fixed_words(rows, words):
+    most = jnp.abs(rows[0])
+    for part in rows[1:]:
+        most = jnp.maximum(most, jnp.abs(part))
+    most = jnp.max(jnp.max(most, axis=0, keepdims=True), axis=1, keepdims=True)
+    most = jnp.maximum(jnp.broadcast_to(most, (HIGH, LANES)), 1e-30)
+    scale = (HALF - 2.0) / most
+    whole = [(part * scale + (HALF + 0.5)).astype(jnp.int32) for part in rows]
+    for k in range(4):
+        extra = whole[4 + k // 2]
+        extra = extra >> 11 if k % 2 else extra & 2047
+        words[k * HIGH : (k + 1) * HIGH, :] = whole[k] | (extra << 21)
+    return most[0:8] * (1.0 / (HALF - 2.0))
+
+
+def project(groups, words, unit, x, idx, u_out, offset):
+    rows = [group_rows(g) for g in groups]
+    got = gather_rows([(words, HIGH * k) for k in range(4)], [idx[r, :] for r in rows], 4)
+    for k, g in enumerate(groups):
+        tops = [lax.shift_right_logical(w, 21) for w in got[k]]
+        whole = [w & ((1 << 21) - 1) for w in got[k]]
+        whole += [tops[0] | (tops[1] << 11), tops[2] | (tops[3] << 11)]
+        u = jnp.zeros((8, LANES), F32)
+        for c in range(6):
+            u = u + x[g, c] * (whole[c] - (1 << 20)).astype(F32)
+        u = u * unit
+        u_out[rows[k], :] = u - x[g, 6] if offset else u
+
+
+def prepare(first, total, d0, d1, vel, prop, words, x_out, idx_out, imp_out, u_out, m_out):
+    unit = fixed_words([vel[c * HIGH : (c + 1) * HIGH, :] for c in range(6)], words)
+
     def load(g):
         base = g * 64
 
@@ -126,35 +162,24 @@
             mass = masses[k][0]
             for c in range(3):
                 mass = mass + cross[c] * cross[c] * masses[k][1 + c]
-            rows = group_rows(g + shift)
+            rows = group_rows(g)
             m_out[rows, :] = jnp.where(alive, mass, -1.0)
             idx_out[rows, :] = index
             imp_out[rows, :] = jnp.where(alive, get(d0, 5), 0.0)
             sign = 1.0 if first else -1.0
             for c, term in enumerate(normal + cross):
-                x_out[g + shift, c] = jnp.where(alive, sign * term, 0.0)
-            x_out[g + shift, 6] = (
-                jnp.where(alive, get(d1, 6), 0.0) if first else jnp.zeros((8, LANES), F32)
-            )
-        project(groups, shift, vel, x_out, idx_out, u_out)
+                x_out[g, c] = jnp.where(alive, sign * term, 0.0)
+            if first:
+                x_out[g, 6] = jnp.where(alive, get(d1, 6), 0.0)
+        project(groups, words, unit, x_out, idx_out, u_out, first)
         return 0
 
     lax.fori_loop(0, (total + 15) >> 4, two_groups, 0)
-
-
-def project(groups, shift, vel, x, idx, u_out):
-    rows = [group_rows(g + shift) for g in groups]
-    got = gather_rows([(vel, HIGH * c) for c in range(6)], [idx[r, :] for r in rows], 6)
-    for k, g in enumerate(groups):
-        u = x[g + shift, 0] * got[k][0]
-        for c in range(1, 6):
-            u = u + x[g + shift, c] * got[k][c]
-        u_out[rows[k], :] = u - x[g + shift, 6]
 
 
 def first_kernel(
     live, send, local, velocity, properties,
-    x_out, idx_out, imp_out, u_out, m_out, meta, share, vel, prop, d0, d1,
+    x_out, idx_out, imp_out, u_out, m_out, meta, share, vel, prop, d0, d1, words,
 ):
     for c in range(6):
         for h in range(HIGH):
@@ -175,7 +200,7 @@
 
     total = lax.fori_loop(0, PEERS, one_partner, jnp.int32(0))
     meta[PEERS] = total
-    prepare(True, 0, total, d0, d1, vel, prop, x_out, idx_out, imp_out, u_out, m_out)
+    prepare(True, total, d0, d1, vel, prop, words, x_out, idx_out, imp_out, u_out, m_out)
 
     def one_share(q, _):
         rows = pl.ds(meta[q], 8)
@@ -187,8 +212,8 @@
 
 
 def second_kernel(
-    received, share_first, vel, prop, meta_first, x_in, idx_in, imp_in, u_in, m_in,
-    x_out, idx_out, imp_out, u_out, m_out, meta, share, d0, used,
+    received, share_first, vel, prop,
+    x_out, idx_out, imp_out, u_out, m_out, meta, share, d0, words, used,
 ):
     def count_rows(q, _):
         flags = received[q, pl.ds(4, 8, stride=8), :]
@@ -196,30 +221,18 @@
         return 0
 
     lax.fori_loop(0, PEERS, count_rows, 0, unroll=8)
-    shift = (meta_first[PEERS] + 7) >> 3
 
     def one_partner(q, base):
-        meta[q] = meta_first[q]
-        meta[PEERS + q] = base + shift * 8
+        meta[q] = base
         d0[pl.ds(pl.multiple_of(base * 8, 8), 64), :] = received[q]
         return base + used[q]
 
     total = lax.fori_loop(0, PEERS, one_partner, jnp.int32(0))
-    groups = shift + ((total + 7) >> 3)
-    meta[COUNT] = groups
-    prepare(False, shift, total, d0, None, vel, prop, x_out, idx_out, imp_out, u_out, m_out)
-    zero = jnp.zeros((8, LANES), F32)
-    for k in range(CHUNK):
-        rows = group_rows(groups + k)
-        for c in range(7):
-            x_out[groups + k, c] = zero
-        idx_out[rows, :] = zero.astype(jnp.int32)
-        imp_out[rows, :] = zero
-        u_out[rows, :] = zero
-        m_out[rows, :] = zero - 1.0
+    meta[PEERS] = total
+    prepare(False, total, d0, None, vel, prop, words, x_out, idx_out, imp_out, u_out, m_out)
 
     def one_share(q, _):
-        rows = pl.ds(meta[PEERS + q], 8)
+        rows = pl.ds(meta[q], 8)
         share[q, 0] = share_first[q, 0]
         share[q, 1] = share_first[q, 1]
         share[q, 2] = u_out[rows, :]
@@ -229,24 +242,54 @@
     lax.fori_loop(0, PEERS, one_share, 0)
 
 
-def apply_kernel(start, meta, x, idx, imp, u, w, received, *refs):
+def merge(side, shift, meta_in, ins, outs):
+    terms = 6 if side else 7
+
+    def one_group(g, _):
+        for c in range(7):
+            outs[0][g + shift, c] = ins[0][g, c] if c < terms else jnp.zeros((8, LANES), F32)
+        for k in range(1, 5):
+            outs[k][group_rows(g + shift), :] = ins[k][group_rows(g), :]
+        return 0
+
+    count = (meta_in[PEERS] + 7) >> 3
+    lax.fori_loop(0, count, one_group, 0)
+    return shift + count
+
+
+def apply_kernel(start, *refs):
     if start:
-        j_out, new, weight, other, mass = refs
+        meta_a, meta_b = refs[:2]
+        sides = refs[2:7], refs[7:12]
+        received, j_out, new, weight, x, idx, meta, imp, u, w, other, mass = refs[12:]
+        shift = merge(0, 0, meta_a, sides[0], (x, idx, imp, u, w))
+        groups = merge(1, shift, meta_b, sides[1], (x, idx, imp, u, w))
+        meta[COUNT] = groups
+        zero = jnp.zeros((8, LANES), F32)
+        for k in range(CHUNK):
+            rows = group_rows(groups + k)
+            for c in range(7):
+                x[groups + k, c] = zero
+            idx[rows, :] = zero.astype(jnp.int32)
+            imp[rows, :] = zero
+            u[rows, :] = zero
+            w[rows, :] = zero - 1.0
     else:
-        j_out, new, other = refs
-        weight = w
+        meta, x, idx, imp, u, weight, received, j_out, new, other = refs
     step = 2 if start else 1
 
     def one_partner(p, _):
+        if start:
+            meta[p] = meta_a[p]
+            mass[pl.ds(meta[p], 8), :] = received[p, 3]
         other[pl.ds(meta[p], 8), :] = received[p, step]
+        return 0
+
+    def second_partner(p, _):
         if start:
-            mass[pl.ds(meta[p], 8), :] = received[p, 3]
-        return 0
-
-    def second_partner(p, _):
+            meta[PEERS + p] = meta_b[p] + shift * 8
+            mass[pl.ds(meta[PEERS + p], 8), :] = received[p, 1]
         other[pl.ds(meta[PEERS + p], 8), :] = received[p, 0]
-        if start:
-            mass[pl.ds(meta[PEERS + p], 8), :] = received[p, 1]
         return 0
 
     lax.fori_loop(0, PEERS, one_partner, 0)
@@ -311,12 +354,14 @@
     return vel[rows, :] + prop[k * HIGH : (k + 1) * HIGH, :] * gain
 
 
-def gather_kernel(meta, vel, prop, j0, j1, j2, j3, x, idx, vel_out, u_out, share):
+def gather_kernel(meta, vel, prop, j0, j1, j2, j3, x, idx, vel_out, u_out, share, words):
+    rows = [moved(vel, prop, j0, j1, j2, j3, c) for c in range(6)]
     for c in range(6):
-        vel_out[c * HIGH : (c + 1) * HIGH, :] = moved(vel, prop, j0, j1, j2, j3, c)
+        vel_out[c * HIGH : (c + 1) * HIGH, :] = rows[c]
+    unit = fixed_words(rows, words)
 
     def two_groups(pair, _):
-        project([pair * 2, pair * 2 + 1], 0, vel_out, x, idx, u_out)
+        project([pair * 2, pair * 2 + 1], words, unit, x, idx, u_out, True)
         return 0
 
     lax.fori_loop(0, (meta[COUNT] + 1) >> 1, two_groups, 0)
@@ -361,14 +406,13 @@
     return jax.ShapeDtypeStruct(dims, dtype)
 
 
-def call(kernel, ins, outs, scratch=(), aliases=None, name=None):
+def call(kernel, ins, outs, scratch=(), name=None):
     return pl.pallas_call(
         kernel,
         in_specs=list(ins),
         out_specs=tuple(SMEM if o.dtype == jnp.int32 and len(o.shape) == 1 else VMEM for o in outs),
         out_shape=tuple(outs),
         scratch_shapes=list(scratch),
-        input_output_aliases=aliases or {},
         compiler_params=pltpu.CompilerParams(vmem_limit_bytes=16 << 20),
         cost_estimate=pl.CostEstimate(
             flops=10_000_000, bytes_accessed=4_000_000, transcendentals=0
@@ -386,7 +430,7 @@
         in_specs=[SMEM, pl.BlockSpec((9, PART * BLK * LANES), lambda i: (0, i))] + [rows] * 4,
         out_specs=(out, out),
         out_shape=(shape(PEERS, 64, LANES),) * 2,
-        scratch_shapes=[pltpu.VMEM((64, LANES), F32)] + [pltpu.VMEM((16, 8, LANES), F32)] * 2,
+        scratch_shapes=[pltpu.VMEM((64, LANES), F32)] * 2 + [pltpu.VMEM((16, 8, LANES), F32)] * 4,
         compiler_params=pltpu.CompilerParams(
             dimension_semantics=("arbitrary",), vmem_limit_bytes=60 << 20
         ),
@@ -399,48 +443,60 @@
 ):
     table = lambda array: array.reshape(ROWS, LANES)
     warm = table(warm_impulse)
-    stream = shape(STREAM, LANES)
-    streams = [
-        shape(GROUPS, 7, 8, LANES), shape(STREAM, LANES, dtype=jnp.int32), stream, stream, stream
-    ]
+    words = pltpu.VMEM((64, LANES), jnp.int32)
+
+    def streams(groups, terms, length):
+        stream = shape(length, LANES)
+        return [
+            shape(groups, terms, 8, LANES), shape(length, LANES, dtype=jnp.int32), stream, stream, stream
+        ]
+
     send, local = pack(
         live_pairs, geometry, table(first_body), table(second_body), table(target_speed), warm
     )
     received = lax.all_to_all(send, "owner", split_axis=0, concat_axis=0, tiled=True)
-    x, idx, imp, u, m, meta_first, share, vel, prop = call(
+    *side_a, meta_a, share, vel, prop = call(
         first_kernel,
         [SMEM] + [VMEM] * 4,
-        streams
+        streams(ROWS // 8, 7, STAGE)
         + [
             shape(PEERS + 1, dtype=jnp.int32), shape(PEERS, 2, 8, LANES),
             shape(96, LANES), shape(64, LANES),
         ],
-        [pltpu.VMEM((STAGE * 8, LANES), F32)] * 2,
+        [pltpu.VMEM((STAGE * 8, LANES), F32)] * 2 + [words],
         name="first",
     )(live_pairs, send, local, velocity, properties)
-    x, idx, imp, u, m, meta, share = call(
+    *side_b, meta_b, share = call(
         second_kernel,
-        [VMEM] * 4 + [SMEM] + [VMEM] * 5,
-        streams + [shape(COUNT + 1, dtype=jnp.int32), shape(PEERS, 4, 8, LANES)],
-        [pltpu.VMEM((STAGE * 8, LANES), F32), pltpu.SMEM((PEERS,), jnp.int32)],
-        aliases={5 + k: k for k in range(5)},
+        [VMEM] * 4,
+        streams(ROWS // 8, 6, STAGE)
+        + [shape(PEERS + 1, dtype=jnp.int32), shape(PEERS, 4, 8, LANES)],
+        [pltpu.VMEM((STAGE * 8, LANES), F32), words, pltpu.SMEM((PEERS,), jnp.int32)],
         name="second",
-    )(received, share, vel, prop, meta_first, x, idx, imp, u, m)
-    weight = m
+    )(received, share, vel, prop)
     n_sub = lax.axis_size("sub")
+    stream = shape(STREAM, LANES)
+    scratch = pltpu.VMEM((STREAM, LANES), F32)
     for iteration in range(ITERS):
-        start = iteration == 0
         told = lax.all_to_all(share, "owner", split_axis=0, concat_axis=0, tiled=True)
-        outs = call(
-            functools.partial(apply_kernel, start),
-            [SMEM] + [VMEM] * 6,
-            [shape(96, LANES), stream] + ([stream] if start else []),
-            [pltpu.VMEM((STREAM, LANES), F32)] * (2 if start else 1),
-            name="apply",
-        )(meta, x, idx, imp, u, weight, told)
-        own, imp = outs[:2]
-        if start:
-            weight = outs[2]
+        if iteration == 0:
+            own, imp, weight, x, idx, meta = call(
+                functools.partial(apply_kernel, True),
+                [SMEM] * 2 + [VMEM] * 11,
+                [shape(96, LANES), stream, stream]
+                + streams(GROUPS, 7, STREAM)[:2]
+                + [shape(COUNT + 1, dtype=jnp.int32)],
+                [scratch] * 5,
+                name="apply",
+            )(meta_a, meta_b, *side_a, *side_b, told)
+        else:
+            own, imp = call(
+                functools.partial(apply_kernel, False),
+                [SMEM] + [VMEM] * 6,
+                [shape(96, LANES), stream],
+                [scratch],
+                name="apply",
+            )(meta, x, idx, imp, u, weight, told)
         gains = [own] + [
             lax.ppermute(own, "sub", [(i, (i + d) % n_sub) for i in range(n_sub)])
             for d in (1, 2, 3)
@@ -450,6 +506,7 @@
                 gather_kernel,
                 [SMEM] + [VMEM] * 8,
                 [shape(96, LANES), stream, shape(PEERS, 2, 8, LANES)],
+                [words],
                 name="gather",
             )(meta, vel, prop, *gains, x, idx)
     (impulse,) = call(

time: 162 us -> 150 us (0.926)
  Pallas kernels: 51.8 us -> 39.8 us
  local copies, waits for them, and re-layouts: 13.8 us -> 5.32 us
  starting transfers between devices: 18.5 us -> 22.3 us
  waiting for transfers between devices: 19 us -> 22.3 us
  blocking collectives: 56.4 us -> 58.7 us
    unnamed x42 -> x36, local copies, waits for them, and re-layouts: 13.8 us -> 5.32 us
    pallas_call x6, Pallas kernels: 29.2 us -> 22.8 us  [the longest x3 10.1 us: on_device(): call(functools.partial(apply_kernel, False), [SMEM] + [VMEM] * 6, [shape(...]
    all_to_all x1, waiting for transfers between devices: 2.84 us -> 8.92 us  [on_device(): lax.all_to_all(send, 'owner', split_axis=0, concat_axis=0, tiled=True)]
    ppermute x12, starting transfers between devices: 8.88 us -> 12.5 us  [on_device(): lax.ppermute(own, 'sub', [(i, (i + d) % n_sub) for i in range(n_sub)])]
    pallas_call x3, Pallas kernels: 11.6 us -> 8.55 us  [on_device(): call(gather_kernel, [SMEM] + [VMEM] * 8, [shape(96, LANES), stream, shape...]
    ppermute x12, waiting for transfers between devices: 16.2 us -> 13.4 us  [on_device(): lax.ppermute(own, 'sub', [(i, (i + d) % n_sub) for i in range(n_sub)])]
    pallas_call x1, Pallas kernels: 7.45 us -> 4.94 us  [pack(): pl.pallas_call(pack_kernel, grid=(PEERS // PART,), in_specs=[SMEM, pl.Blo...]
    all_to_all x4, blocking collectives: 56.4 us -> 58.7 us  [on_device(): lax.all_to_all(share, 'owner', split_axis=0, concat_axis=0, tiled=True)]
where the time goes in v3:
time: 150 us; the launch traced here: 149 us
  blocking collectives  58.7 us (39%)
  Pallas kernels  39.8 us (27%)
  starting transfers between devices  22.3 us (15%)
  waiting for transfers between devices  22.3 us (15%)
  local copies, waits for them, and re-layouts  5.32 us (4%)
    all_to_all x4, blocking collectives, on_device(): lax.all_to_all(share, 'owner', split_axis=0, concat_axis=0, tiled=True)  58.7 us
    ppermute x12, waiting for transfers between devices, on_device(): lax.ppermute(own, 'sub', [(i, (i + d) % n_sub) for i in range(n_sub)])  13.4 us
    ppermute x12, starting transfers between devices, on_device(): lax.ppermute(own, 'sub', [(i, (i + d) % n_sub) for i in range(n_sub)])  12.5 us
    pallas_call x3, Pallas kernels, on_device(): call(functools.partial(apply_kernel, False), [SMEM] + [VMEM] * 6, [shape(...  10.1 us
    all_to_all x1, starting transfers between devices, on_device(): lax.all_to_all(send, 'owner', split_axis=0, concat_axis=0, tiled=True)  9.75 us
    all_to_all x1, waiting for transfers between devices, on_device(): lax.all_to_all(send, 'owner', split_axis=0, concat_axis=0, tiled=True)  8.92 us
    pallas_call x3, Pallas kernels, on_device(): call(gather_kernel, [SMEM] + [VMEM] * 8, [shape(96, LANES), stream, shape...  8.55 us
    unnamed x36, local copies, waits for them, and re-layouts  5.32 us
  transfers between devices with their start and end apart: 13, of which 12 were waited for; matrix products, arithmetic and copies ran while one was open for 0% of the time, Pallas kernels for 5%

profile of v3, /device:TPU:1, one launch (start us, length us, event | category | flops | bytes accessed | tf_op | source)
XLA Modules:
  0.0 149.3 jit_solution(6882937353330448352)
XLA Ops:
  0.6 0.0 copy-start.15
  0.6 0.0 copy-start.16
  0.7 0.0 copy-start.17
  0.7 4.9 %pack.1 = (f32[32,64,128]{2,1,0:T(8,128)}, f32[32,64,128]{2,1,0:T(8,128)}) custom-call(s32[256]{0:T(256)} %live.5, f32[9,32768]{1,0:T(8,128)} %geom.1, s32[256,128]{1,0:T(8,128)} %bitcast.7, s32[256,128]{1,0:T(8,128)} %bitcast.8, f32[256,128]{1,0:T(8,128)} %bitcast.9, f32[256,128]{1,0:T(8,128)} %bitcast.5), custom_call_target="tpu_custom_call" | custom-call | tf_op jit(solution)/shard_map/pack/pallas_call | solution.py:427
  5.6 9.7 %all-to-all-start = ((f32[32,64,128]{2,1,0:T(8,128)}), f32[32,64,128]{2,1,0:T(8,128)S(1)}, u32[]{:S(2)}, u32[]{:S(2)}) async-start(f32[32,64,128]{2,1,0:T(8,128)} %get-tuple-element.41.send), calls=%async_computation | async-start | bytes 2097152 | tf_op jit(solution)/shard_map/all_to_all | solution.py:457
  15.4 0.0 copy-done.15
  15.4 0.0 copy-done.16
  15.4 0.0 copy-done.17
  15.4 0.0 copy-done
  15.4 0.0 copy-done.1
  15.4 3.9 %first.1 = (f32[32,7,8,128]{3,2,1,0:T(8,128)S(1)}, s32[272,128]{1,0:T(8,128)S(1)}, f32[272,128]{1,0:T(8,128)S(1)}, f32[272,128]{1,0:T(8,128)S(1)}, f32[272,128]{...) custom-call(s32[256]{0:T(256)S(1)} %copy-done.17, ...), custom_call_target="tpu_custom_call" | custom-call | flops 10000000 | bytes 4000000 | tf_op jit(solution)/shard_map/first/pallas_call | solution.py:458
  19.4 0.0 copy-start.2
  19.4 0.9 copy-done.2
  20.3 0.7 copy-done.5
  21.0 0.6 copy-done.7
  21.7 0.7 copy-done.9
  22.3 0.6 copy-done.11
  23.0 0.7 copy-done.13
  23.6 8.9 %all-to-all-done.received = f32[32,64,128]{2,1,0:T(8,128)S(1)} async-done(((f32[32,64,128]{2,1,0:T(8,128)}), f32[32,64,128]{2,1,0:T(8,128)S(1)}, u32[]{:S(2)}, u32[]{:S(2)}) %all-to-all-start) | async-done | bytes 1048608 | tf_op jit(solution)/shard_map/all_to_all | solution.py:457
  32.5 1.0 copy-done.6
  33.6 4.4 %second.1 = (f32[32,6,8,128]{3,2,1,0:T(8,128)S(1)}, s32[272,128]{1,0:T(8,128)S(1)}, f32[272,128]{1,0:T(8,128)S(1)}, f32[272,128]{1,0:T(8,128)S(1)}, f32[272,128]...) custom-call(f32[32,64,128]{2,1,0:T(8,128)S(1)} %all-to-all-done.received, ...), custom_call_target="tpu_custom_call" | custom-call | flops 10000000 | bytes 4000000 | tf_op jit(solution)/shard_map/second/pallas_call | solution.py:469
  38.0 15.3 %all_to_all.25.refs_12_ = f32[32,4,8,128]{3,2,1,0:T(8,128)S(1)} all-to-all(f32[32,4,8,128]{3,2,1,0:T(8,128)S(1)} %get-tuple-element.58), channel_id=1, replica_groups=mesh['owner'=32,'sub'=4] {'owner'}, dimensions={0} | all-to-all | bytes 1048576 | tf_op jit(solution)/shard_map/all_to_all | solution.py:481
  53.3 0.0 copy-done.3
  53.3 0.0 copy-done.10
  53.3 0.0 copy-done.12
  53.3 0.0 copy-done.14
  53.4 4.3 %apply.4 = (f32[96,128]{1,0:T(8,128)S(1)}, f32[560,128]{1,0:T(8,128)S(1)}, f32[560,128]{1,0:T(8,128)S(1)}, f32[70,7,8,128]{3,2,1,0:T(8,128)S(1)}, s32[560,128]{1,0:T(8,128)S(1)}, /*index=5*/s32[65]{0:T(128)S(1)}) custom-call(s32[33]{0:T(128)S(1)} %get-tuple-element.43.refs_0_, s32[33]{0:T(128)S(1)} %get-tuple-element.47.refs_1_, ...), custom_call_target="tpu_custom_call" | custom-call | flops 10000000 | bytes 4000000 | tf_op jit(solution)/shard_map/apply/pallas_call | solution.py:483
  57.7 3.3 %collective-permute-start.2 = (f32[96,128]{1,0:T(8,128)S(1)}, f32[96,128]{1,0:T(8,128)S(1)}, u32[]{:S(2)}, u32[]{:S(2)}) collective-permute-start(f32[96,128]{1,0:T(8,128)S(1)} %get-tuple-element.60.j0), channel_id=1, source_target_pairs={{0,3},{1,0},{2,1},{3,2},{4,7},{5,4},{6,5},{7,6},{8,11},{9,8},{10,9... | collective-permute-start | bytes 147464 | tf_op jit(solution)/shard_map/ppermute | solution.py:501
  61.0 0.6 collective-permute-start.1
  61.6 0.4 collective-permute-start
  62.0 0.1 collective-permute-done.2.j3
  62.1 3.3 %collective-permute-done.1.j2 = f32[96,128]{1,0:T(8,128)S(1)} collective-permute-done((f32[96,128]{1,0:T(8,128)S(1)}, f32[96,128]{1,0:T(8,128)S(1)}, u32[]{:S(2)}, u32[]{:S(2)}) %collective-permute-start.1) | collective-permute-done | bytes 49184 | tf_op jit(solution)/shard_map/ppermute | solution.py:501
  65.4 0.5 collective-permute-done.j1
  65.9 2.8 %gather.3 = (f32[96,128]{1,0:T(8,128)S(1)}, f32[560,128]{1,0:T(8,128)S(1)}, f32[32,2,8,128]{3,2,1,0:T(8,128)S(1)}) custom-call(s32[65]{0:T(128)S(1)} %get-tuple-element.59.meta.refs_0_, f32[96,128]{1,0:T(8,128)S(1)} %get-tuple-element.45.vel, f32[64,128]{1,0:T(8,128)S(1)} %get-tuple-element.46.prop, f32[96,128]{1,0:T(8,128)S(1)} %get-tuple-element.60.j0, ...), custom_call_target="tpu_custom_call" | custom-call | flops 10000000 | bytes 4000000 | tf_op jit(solution)/shard_map/gather/pallas_call | solution.py:505
  68.8 14.7 %all_to_all.26.refs_6_ = f32[32,2,8,128]{3,2,1,0:T(8,128)S(1)} all-to-all(f32[32,2,8,128]{3,2,1,0:T(8,128)S(1)} %get-tuple-element.67), channel_id=1, replica_groups=mesh['owner'=32,'sub'=4] {'owner'}, dimensions={0} | all-to-all | bytes 524288 | tf_op jit(solution)/shard_map/all_to_all | solution.py:481
  83.5 3.4 %apply.5 = (f32[96,128]{1,0:T(8,128)S(1)}, f32[560,128]{1,0:T(8,128)S(1)}) custom-call(s32[65]{0:T(128)S(1)} %get-tuple-element.59.meta.refs_0_, f32[70,7,8,128]{3,2,1,0:T(8,128)S(1)} %get-tuple-element.61.x.refs_1_, s32[560,128]{1,0:T(8,128)S(1)} %get-tuple-element.62.idx.refs_2_, f32[560,128]{1,0:T(8,128)S(1)} %get-tuple-element.64.refs_3_, ...), custom_call_target="tpu_custom_call" | custom-call | flops 10000000 | bytes 4000000 | tf_op jit(solution)/shard_map/apply/pallas_call | solution.py:493
  86.8 1.1 collective-permute-start.5
  88.0 0.8 collective-permute-start.4
  88.8 0.8 collective-permute-start.3
  89.5 0.3 collective-permute-done.5.j3
  89.8 2.6 %collective-permute-done.4.j2 = f32[96,128]{1,0:T(8,128)S(1)} collective-permute-done((f32[96,128]{1,0:T(8,128)S(1)}, f32[96,128]{1,0:T(8,128)S(1)}, u32[]{:S(2)}, u32[]{:S(2)}) %collective-permute-start.4) | collective-permute-done | bytes 49184 | tf_op jit(solution)/shard_map/ppermute | solution.py:501
  92.4 0.8 collective-permute-done.3.j1
  93.2 2.8 %gather.4 = (f32[96,128]{1,0:T(8,128)S(1)}, f32[560,128]{1,0:T(8,128)S(1)}, f32[32,2,8,128]{3,2,1,0:T(8,128)S(1)}) custom-call(s32[65]{0:T(128)S(1)} %get-tuple-element.59.meta.refs_0_, f32[96,128]{1,0:T(8,128)S(1)} %get-tuple-element.63.vel, f32[64,128]{1,0:T(8,128)S(1)} %get-tuple-element.46.prop, f32[96,128]{1,0:T(8,128)S(1)} %get-tuple-element.68.j0, ...), custom_call_target="tpu_custom_call" | custom-call | flops 10000000 | bytes 4000000 | tf_op jit(solution)/shard_map/gather/pallas_call | solution.py:505
  96.1 14.4 %all_to_all.27.refs_6_ = f32[32,2,8,128]{3,2,1,0:T(8,128)S(1)} all-to-all(f32[32,2,8,128]{3,2,1,0:T(8,128)S(1)} %get-tuple-element.72), channel_id=1, replica_groups=mesh['owner'=32,'sub'=4] {'owner'}, dimensions={0} | all-to-all | bytes 524288 | tf_op jit(solution)/shard_map/all_to_all | solution.py:481
  110.5 3.4 %apply.6 = (f32[96,128]{1,0:T(8,128)S(1)}, f32[560,128]{1,0:T(8,128)S(1)}) custom-call(s32[65]{0:T(128)S(1)} %get-tuple-element.59.meta.refs_0_, f32[70,7,8,128]{3,2,1,0:T(8,128)S(1)} %get-tuple-element.61.x.refs_1_, s32[560,128]{1,0:T(8,128)S(1)} %get-tuple-element.62.idx.refs_2_, f32[560,128]{1,0:T(8,128)S(1)} %get-tuple-element.70.refs_3_, ...), custom_call_target="tpu_custom_call" | custom-call | flops 10000000 | bytes 4000000 | tf_op jit(solution)/shard_map/apply/pallas_call | solution.py:493
  113.8 2.2 %collective-permute-start.8 = (f32[96,128]{1,0:T(8,128)S(1)}, f32[96,128]{1,0:T(8,128)S(1)}, u32[]{:S(2)}, u32[]{:S(2)}) collective-permute-start(f32[96,128]{1,0:T(8,128)S(1)} %get-tuple-element.73.j0), channel_id=1, source_target_pairs={{0,3},{1,0},{2,1},{3,2},{4,7},{5,4},{6,5},{7,6},{8,11},{9,8},{10,9... | collective-permute-start | bytes 147464 | tf_op jit(solution)/shard_map/ppermute | solution.py:501
  116.1 0.6 collective-permute-start.7
  116.7 0.0 collective-permute-start.6
  116.7 0.5 collective-permute-done.8.j3
  117.2 3.3 %collective-permute-done.7.j2 = f32[96,128]{1,0:T(8,128)S(1)} collective-permute-done((f32[96,128]{1,0:T(8,128)S(1)}, f32[96,128]{1,0:T(8,128)S(1)}, u32[]{:S(2)}, u32[]{:S(2)}) %collective-permute-start.7) | collective-permute-done | bytes 49184 | tf_op jit(solution)/shard_map/ppermute | solution.py:501
  120.5 0.9 collective-permute-done.6.j1
  121.4 2.9 %gather.5 = (f32[96,128]{1,0:T(8,128)S(1)}, f32[560,128]{1,0:T(8,128)S(1)}, f32[32,2,8,128]{3,2,1,0:T(8,128)S(1)}) custom-call(s32[65]{0:T(128)S(1)} %get-tuple-element.59.meta.refs_0_, f32[96,128]{1,0:T(8,128)S(1)} %get-tuple-element.69.vel, f32[64,128]{1,0:T(8,128)S(1)} %get-tuple-element.46.prop, f32[96,128]{1,0:T(8,128)S(1)} %get-tuple-element.73.j0, ...), custom_call_target="tpu_custom_call" | custom-call | flops 10000000 | bytes 4000000 | tf_op jit(solution)/shard_map/gather/pallas_call | solution.py:505
  124.3 0.0 copy-start.4
  124.3 14.4 %all_to_all.28.refs_6_ = f32[32,2,8,128]{3,2,1,0:T(8,128)S(1)} all-to-all(f32[32,2,8,128]{3,2,1,0:T(8,128)S(1)} %get-tuple-element.77), channel_id=1, replica_groups=mesh['owner'=32,'sub'=4] {'owner'}, dimensions={0} | all-to-all | bytes 524288 | tf_op jit(solution)/shard_map/all_to_all | solution.py:481
  138.7 3.4 %apply.7 = (f32[96,128]{1,0:T(8,128)S(1)}, f32[560,128]{1,0:T(8,128)S(1)}) custom-call(s32[65]{0:T(128)S(1)} %get-tuple-element.59.meta.refs_0_, f32[70,7,8,128]{3,2,1,0:T(8,128)S(1)} %get-tuple-element.61.x.refs_1_, s32[560,128]{1,0:T(8,128)S(1)} %get-tuple-element.62.idx.refs_2_, f32[560,128]{1,0:T(8,128)S(1)} %get-tuple-element.75.refs_3_, ...), custom_call_target="tpu_custom_call" | custom-call | flops 10000000 | bytes 4000000 | tf_op jit(solution)/shard_map/apply/pallas_call | solution.py:493
  142.0 1.2 collective-permute-start.11
  143.3 0.6 collective-permute-start.10
  143.9 0.8 collective-permute-start.9
  144.7 0.0 copy-done.4
  144.7 2.9 %unpack.1 = f32[256,128]{1,0:T(8,128)} custom-call(s32[256]{0:T(256)S(1)} %copy-done.17, s32[65]{0:T(128)S(1)} %get-tuple-element.59.meta.refs_0_, f32[560,128]{1,0:T(8,128)S(1)} %get-tuple-element.79.imp, f32[256,128]{1,0:T(8,128)S(1)} %bitcast.6), custom_call_target="tpu_custom_call" | custom-call | flops 10000000 | bytes 4000000 | tf_op jit(solution)/shard_map/unpack/pallas_call | solution.py:512
  147.5 0.0 collective-permute-done.11.j3
  147.5 0.2 collective-permute-done.10.j2
  147.7 0.9 collective-permute-done.9.j1
  148.6 0.7 final.1
  (14 shorter events, 0.0 us)
Async XLA Ops:
  0.6 14.7 %copy-start.15 = (f32[6,2048]{1,0:T(8,128)S(1)}, f32[6,2048]{1,0:T(8,128)}, u32[]{:S(2)}) copy-start(f32[6,2048]{1,0:T(8,128)} %velocity.1) | copy-start | bytes 147460
  0.6 14.7 %copy-start.16 = (f32[4,2048]{1,0:T(4,128)S(1)}, f32[4,2048]{1,0:T(4,128)}, u32[]{:S(2)}) copy-start(f32[4,2048]{1,0:T(4,128)} %properties.1) | copy-start | bytes 98308
  0.7 14.7 %copy-start.17 = (s32[256]{0:T(256)S(1)}, s32[256]{0:T(256)}, u32[]{:S(2)}) copy-start(s32[256]{0:T(256)} %live.5) | copy-start | bytes 3076
  5.6 9.8 %copy-start = (f32[32,64,128]{2,1,0:T(8,128)S(1)}, f32[32,64,128]{2,1,0:T(8,128)}, u32[]{:S(2)}) copy-start(f32[32,64,128]{2,1,0:T(8,128)} %get-tuple-element.41.send) | copy-start | bytes 3145732
  5.6 9.8 %copy-start.1 = (f32[32,64,128]{2,1,0:T(8,128)S(1)}, f32[32,64,128]{2,1,0:T(8,128)}, u32[]{:S(2)}) copy-start(f32[32,64,128]{2,1,0:T(8,128)} %get-tuple-element.42.local) | copy-start | bytes 3145732
  5.6 26.9 %all-to-all-start = ((f32[32,64,128]{2,1,0:T(8,128)}), f32[32,64,128]{2,1,0:T(8,128)S(1)}, u32[]{:S(2)}, u32[]{:S(2)}) async-start(f32[32,64,128]{2,1,0:T(8,128)} %get-tuple-element.41.send), calls=%async_computation | async-start | bytes 2097152 | tf_op jit(solution)/shard_map/all_to_all | solution.py:457
  19.4 0.9 copy-start.2
  20.3 0.7 copy-start.5
  21.0 0.7 copy-start.7
  21.7 0.7 copy-start.9
  22.3 0.6 copy-start.11
  23.0 0.7 copy-start.13
  32.5 20.8 %copy-start.3 = (f32[32,7,8,128]{3,2,1,0:T(8,128)S(1)}, f32[32,7,8,128]{3,2,1,0:T(8,128)}, u32[]{:S(2)}) copy-start(f32[32,7,8,128]{3,2,1,0:T(8,128)} %copy-done.2) | copy-start | bytes 2752516
  32.5 1.0 copy-start.6
  33.6 19.8 %copy-start.8 = (s32[272,128]{1,0:T(8,128)S(1)}, s32[272,128]{1,0:T(8,128)}, u32[]{:S(2)}) copy-start(s32[272,128]{1,0:T(8,128)} %copy-done.7) | copy-start | bytes 417796
  33.6 19.8 %copy-start.10 = (f32[272,128]{1,0:T(8,128)S(1)}, f32[272,128]{1,0:T(8,128)}, u32[]{:S(2)}) copy-start(f32[272,128]{1,0:T(8,128)} %copy-done.9) | copy-start | bytes 417796
  33.6 19.8 %copy-start.12 = (f32[272,128]{1,0:T(8,128)S(1)}, f32[272,128]{1,0:T(8,128)}, u32[]{:S(2)}) copy-start(f32[272,128]{1,0:T(8,128)} %copy-done.11) | copy-start | bytes 417796
  33.6 19.8 %copy-start.14 = (f32[272,128]{1,0:T(8,128)S(1)}, f32[272,128]{1,0:T(8,128)}, u32[]{:S(2)}) copy-start(f32[272,128]{1,0:T(8,128)} %copy-done.13) | copy-start | bytes 417796
  57.7 4.4 %collective-permute-start.2 = (f32[96,128]{1,0:T(8,128)S(1)}, f32[96,128]{1,0:T(8,128)S(1)}, u32[]{:S(2)}, u32[]{:S(2)}) collective-permute-start(f32[96,128]{1,0:T(8,128)S(1)} %get-tuple-element.60.j0), channel_id=1, source_target_pairs={{0,3},{1,0},{2,1},{3,2},{4,7},{5,4},{6,5},{7,6},{8,11},{9,8},{10,9... | collective-permute-start | bytes 147464 | tf_op jit(solution)/shard_map/ppermute | solution.py:501
  61.0 4.5 %collective-permute-start.1 = (f32[96,128]{1,0:T(8,128)S(1)}, f32[96,128]{1,0:T(8,128)S(1)}, u32[]{:S(2)}, u32[]{:S(2)}) collective-permute-start(f32[96,128]{1,0:T(8,128)S(1)} %get-tuple-element.60.j0), channel_id=1, source_target_pairs={{0,2},{1,3},{2,0},{3,1},{4,6},{5,7},{6,4},{7,5},{8,10},{9,11},{10,... | collective-permute-start | bytes 147464 | tf_op jit(solution)/shard_map/ppermute | solution.py:501
  61.6 4.4 %collective-permute-start = (f32[96,128]{1,0:T(8,128)S(1)}, f32[96,128]{1,0:T(8,128)S(1)}, u32[]{:S(2)}, u32[]{:S(2)}) collective-permute-start(f32[96,128]{1,0:T(8,128)S(1)} %get-tuple-element.60.j0), channel_id=1, source_target_pairs={{0,1},{1,2},{2,3},{3,0},{4,5},{5,6},{6,7},{7,4},{8,9},{9,10},{10,1... | collective-permute-start | bytes 147464 | tf_op jit(solution)/shard_map/ppermute | solution.py:501
  86.8 3.0 %collective-permute-start.5 = (f32[96,128]{1,0:T(8,128)S(1)}, f32[96,128]{1,0:T(8,128)S(1)}, u32[]{:S(2)}, u32[]{:S(2)}) collective-permute-start(f32[96,128]{1,0:T(8,128)S(1)} %get-tuple-element.68.j0), channel_id=1, source_target_pairs={{0,3},{1,0},{2,1},{3,2},{4,7},{5,4},{6,5},{7,6},{8,11},{9,8},{10,9... | collective-permute-start | bytes 147464 | tf_op jit(solution)/shard_map/ppermute | solution.py:501
  88.0 4.4 %collective-permute-start.4 = (f32[96,128]{1,0:T(8,128)S(1)}, f32[96,128]{1,0:T(8,128)S(1)}, u32[]{:S(2)}, u32[]{:S(2)}) collective-permute-start(f32[96,128]{1,0:T(8,128)S(1)} %get-tuple-element.68.j0), channel_id=1, source_target_pairs={{0,2},{1,3},{2,0},{3,1},{4,6},{5,7},{6,4},{7,5},{8,10},{9,11},{10,... | collective-permute-start | bytes 147464 | tf_op jit(solution)/shard_map/ppermute | solution.py:501
  88.8 4.5 %collective-permute-start.3 = (f32[96,128]{1,0:T(8,128)S(1)}, f32[96,128]{1,0:T(8,128)S(1)}, u32[]{:S(2)}, u32[]{:S(2)}) collective-permute-start(f32[96,128]{1,0:T(8,128)S(1)} %get-tuple-element.68.j0), channel_id=1, source_target_pairs={{0,1},{1,2},{2,3},{3,0},{4,5},{5,6},{6,7},{7,4},{8,9},{9,10},{10,1... | collective-permute-start | bytes 147464 | tf_op jit(solution)/shard_map/ppermute | solution.py:501
  113.8 3.4 %collective-permute-start.8 = (f32[96,128]{1,0:T(8,128)S(1)}, f32[96,128]{1,0:T(8,128)S(1)}, u32[]{:S(2)}, u32[]{:S(2)}) collective-permute-start(f32[96,128]{1,0:T(8,128)S(1)} %get-tuple-element.73.j0), channel_id=1, source_target_pairs={{0,3},{1,0},{2,1},{3,2},{4,7},{5,4},{6,5},{7,6},{8,11},{9,8},{10,9... | collective-permute-start | bytes 147464 | tf_op jit(solution)/shard_map/ppermute | solution.py:501
  116.1 4.5 %collective-permute-start.7 = (f32[96,128]{1,0:T(8,128)S(1)}, f32[96,128]{1,0:T(8,128)S(1)}, u32[]{:S(2)}, u32[]{:S(2)}) collective-permute-start(f32[96,128]{1,0:T(8,128)S(1)} %get-tuple-element.73.j0), channel_id=1, source_target_pairs={{0,2},{1,3},{2,0},{3,1},{4,6},{5,7},{6,4},{7,5},{8,10},{9,11},{10,... | collective-permute-start | bytes 147464 | tf_op jit(solution)/shard_map/ppermute | solution.py:501
  116.7 4.7 %collective-permute-start.6 = (f32[96,128]{1,0:T(8,128)S(1)}, f32[96,128]{1,0:T(8,128)S(1)}, u32[]{:S(2)}, u32[]{:S(2)}) collective-permute-start(f32[96,128]{1,0:T(8,128)S(1)} %get-tuple-element.73.j0), channel_id=1, source_target_pairs={{0,1},{1,2},{2,3},{3,0},{4,5},{5,6},{6,7},{7,4},{8,9},{9,10},{10,1... | collective-permute-start | bytes 147464 | tf_op jit(solution)/shard_map/ppermute | solution.py:501
  124.3 20.4 %copy-start.4 = (f32[32768]{0:T(1024)S(1)}, f32[32768]{0:T(1024)}, u32[]{:S(2)}) copy-start(f32[32768]{0:T(1024)} %param.14) | copy-start | bytes 393220
  142.0 5.5 %collective-permute-start.11 = (f32[96,128]{1,0:T(8,128)S(1)}, f32[96,128]{1,0:T(8,128)S(1)}, u32[]{:S(2)}, u32[]{:S(2)}) collective-permute-start(f32[96,128]{1,0:T(8,128)S(1)} %get-tuple-element.78.j0), channel_id=1, source_target_pairs={{0,3},{1,0},{2,1},{3,2},{4,7},{5,4},{6,5},{7,6},{8,11},{9,8},{10,9... | collective-permute-start | bytes 147464 | tf_op jit(solution)/shard_map/ppermute | solution.py:501
  143.3 4.5 %collective-permute-start.10 = (f32[96,128]{1,0:T(8,128)S(1)}, f32[96,128]{1,0:T(8,128)S(1)}, u32[]{:S(2)}, u32[]{:S(2)}) collective-permute-start(f32[96,128]{1,0:T(8,128)S(1)} %get-tuple-element.78.j0), channel_id=1, source_target_pairs={{0,2},{1,3},{2,0},{3,1},{4,6},{5,7},{6,4},{7,5},{8,10},{9,11},{10,... | collective-permute-start | bytes 147464 | tf_op jit(solution)/shard_map/ppermute | solution.py:501
  143.9 4.7 %collective-permute-start.9 = (f32[96,128]{1,0:T(8,128)S(1)}, f32[96,128]{1,0:T(8,128)S(1)}, u32[]{:S(2)}, u32[]{:S(2)}) collective-permute-start(f32[96,128]{1,0:T(8,128)S(1)} %get-tuple-element.78.j0), channel_id=1, source_target_pairs={{0,1},{1,2},{2,3},{3,0},{4,5},{5,6},{6,7},{7,4},{8,9},{9,10},{10,1... | collective-permute-start | bytes 147464 | tf_op jit(solution)/shard_map/ppermute | solution.py:501

commit v4 on v3

--- a/solution.py
+++ b/solution.py
@@ -23,6 +23,7 @@
 STREAM = GROUPS * 8
 COUNT = 2 * PEERS
 PART = 8
+WAYS = 4
 VMEM = pl.BlockSpec(memory_space=pltpu.VMEM)
 SMEM = pl.BlockSpec(memory_space=pltpu.SMEM)
 
@@ -35,53 +36,43 @@
     return lax.broadcasted_iota(jnp.int32, (8, LANES), 0)
 
 
-def pack_kernel(live, geom, first, second, target, warm, send, local, *scratch):
+def pack_kernel(sent, live, geom, index, value, out, *scratch):
     start = pl.program_id(0) * PART
     lanes = lane_iota()
     subs = row_iota()
-    dead = jnp.where(subs == 4, -1.0, 0.0).astype(F32)
-
-    def one_partner(q, mixed, packed0, packed1):
+    fill = jnp.where((subs == 4) & sent, -1.0, 0.0).astype(F32)
+    mixes = (subs >= 3) & (subs < 6) if sent else subs >= 6
+
+    def one_partner(q, mixed, packed):
         rows = pl.ds(pl.multiple_of(q * BLK, BLK), BLK)
-        mixed[pl.ds(4, 8, stride=8), :] = (second[rows, :] & (HIGH * LANES - 1)).astype(F32)
-        mixed[pl.ds(5, 8, stride=8), :] = warm[rows, :]
-        mixed[pl.ds(6, 8, stride=8), :] = target[rows, :]
-        mixed[pl.ds(7, 8, stride=8), :] = (first[rows, :] & (HIGH * LANES - 1)).astype(F32)
+        mixed[pl.ds(4 if sent else 7, 8, stride=8), :] = (index[rows, :] & (HIGH * LANES - 1)).astype(F32)
+        mixed[pl.ds(5 if sent else 6, 8, stride=8), :] = value[rows, :]
         cols = [pl.ds(pl.multiple_of(q * BLK * LANES + b * LANES, LANES), LANES) for b in range(BLK)]
+        if sent:
+            for b in range(BLK):
+                mixed[pl.ds(8 * b + 3, 1), :] = geom[8:9, cols[b]]
+        offset = jnp.int32(0)
+        current = jnp.zeros((8, LANES), F32)
         for b in range(BLK):
-            mixed[pl.ds(8 * b + 3, 1), :] = geom[8:9, cols[b]]
-        offset = jnp.int32(0)
-        cur0 = jnp.zeros((8, LANES), F32)
-        cur1 = cur0
-        for b in range(BLK):
-            geo = geom[0:8, cols[b]]
-            mix = mixed[8 * b : 8 * b + 8, :]
             shift = offset & (LANES - 1)
             row = offset >> 7
-            rolled0 = pltpu.roll(jnp.where((subs >= 3) & (subs < 6), mix, geo), shift, 1)
-            rolled1 = pltpu.roll(jnp.where(subs >= 6, mix, geo), shift, 1)
-            keep = lanes < shift
-            cur0 = jnp.where(keep, cur0, rolled0)
-            cur1 = jnp.where(keep, cur1, rolled1)
-            packed0[row] = cur0
-            packed1[row] = cur1
+            both = jnp.where(mixes, mixed[8 * b : 8 * b + 8, :], geom[0:8, cols[b]])
+            rolled = pltpu.roll(both, shift, 1)
+            current = jnp.where(lanes < shift, current, rolled)
+            packed[row] = current
             offset = offset + live[(start + q) * BLK + b]
             spill = jnp.broadcast_to((offset >> 7) > row, (8, LANES))
-            cur0 = jnp.where(spill, rolled0, cur0)
-            cur1 = jnp.where(spill, rolled1, cur1)
-        packed0[offset >> 7] = cur0
-        packed1[offset >> 7] = cur1
+            current = jnp.where(spill, rolled, current)
+        packed[offset >> 7] = current
         for r in range(BLK):
-            alive = lanes + r * LANES < offset
-            send[q, 8 * r : 8 * r + 8, :] = jnp.where(alive, packed0[r], dead)
-            local[q, 8 * r : 8 * r + 8, :] = jnp.where(alive, packed1[r], 0.0)
-
-    def two_partners(pair, _):
-        one_partner(pair * 2, *scratch[0::2])
-        one_partner(pair * 2 + 1, *scratch[1::2])
-        return 0
-
-    lax.fori_loop(0, PART // 2, two_partners, 0)
+            out[q, 8 * r : 8 * r + 8, :] = jnp.where(lanes + r * LANES < offset, packed[r], fill)
+
+    def some_partners(step, _):
+        for k in range(WAYS):
+            one_partner(step * WAYS + k, *scratch[2 * k : 2 * k + 2])
+        return 0
+
+    lax.fori_loop(0, PART // WAYS, some_partners, 0)
 
 
 def gather_rows(tables, index, count):
@@ -198,7 +189,7 @@
         d1[rows, :] = local[q]
         return base + ((count + LANES - 1) >> 7)
 
-    total = lax.fori_loop(0, PEERS, one_partner, jnp.int32(0))
+    total = lax.fori_loop(0, PEERS, one_partner, jnp.int32(0), unroll=4)
     meta[PEERS] = total
     prepare(True, total, d0, d1, vel, prop, words, x_out, idx_out, imp_out, u_out, m_out)
 
@@ -208,13 +199,16 @@
         share[q, 1] = m_out[rows, :]
         return 0
 
-    lax.fori_loop(0, PEERS, one_share, 0)
+    lax.fori_loop(0, PEERS, one_share, 0, unroll=8)
 
 
 def second_kernel(
     received, share_first, vel, prop,
-    x_out, idx_out, imp_out, u_out, m_out, meta, share, d0, words, used,
+    x_out, idx_out, imp_out, u_out, m_out, meta, share, d0, words, used, sem,
 ):
+    copy = pltpu.make_async_copy(share_first, share.at[:, 0:2], sem)
+    copy.start()
+
     def count_rows(q, _):
         flags = received[q, pl.ds(4, 8, stride=8), :]
         used[q] = jnp.max(jnp.where(flags >= 0.0, row_iota() + 1, 0))
@@ -227,19 +221,18 @@
         d0[pl.ds(pl.multiple_of(base * 8, 8), 64), :] = received[q]
         return base + used[q]
 
-    total = lax.fori_loop(0, PEERS, one_partner, jnp.int32(0))
+    total = lax.fori_loop(0, PEERS, one_partner, jnp.int32(0), unroll=4)
     meta[PEERS] = total
     prepare(False, total, d0, None, vel, prop, words, x_out, idx_out, imp_out, u_out, m_out)
 
     def one_share(q, _):
         rows = pl.ds(meta[q], 8)
-        share[q, 0] = share_first[q, 0]
-        share[q, 1] = share_first[q, 1]
         share[q, 2] = u_out[rows, :]
         share[q, 3] = m_out[rows, :]
         return 0
 
-    lax.fori_loop(0, PEERS, one_share, 0)
+    lax.fori_loop(0, PEERS, one_share, 0, unroll=8)
+    copy.wait()
 
 
 def merge(side, shift, meta_in, ins, outs):
@@ -292,8 +285,8 @@
         other[pl.ds(meta[PEERS + p], 8), :] = received[p, 0]
         return 0
 
-    lax.fori_loop(0, PEERS, one_partner, 0)
-    lax.fori_loop(0, PEERS, second_partner, 0)
+    lax.fori_loop(0, PEERS, one_partner, 0, unroll=8)
+    lax.fori_loop(0, PEERS, second_partner, 0, unroll=8)
     iota_high = lax.broadcasted_iota(jnp.int32, (HIGH, LANES), 0)
     iota_low = lax.broadcasted_iota(jnp.int32, (LANES, LANES), 0)
 
@@ -371,7 +364,7 @@
         share[q, 1] = u_out[pl.ds(meta[PEERS + q], 8), :]
         return 0
 
-    lax.fori_loop(0, PEERS, one_share, 0)
+    lax.fori_loop(0, PEERS, one_share, 0, unroll=8)
 
 
 def final_kernel(vel, prop, j0, j1, j2, j3, out):
@@ -399,7 +392,7 @@
             offset = offset + count
         return 0
 
-    lax.fori_loop(0, PEERS, one_partner, 0, unroll=2)
+    lax.fori_loop(0, PEERS, one_partner, 0, unroll=4)
 
 
 def shape(*dims, dtype=F32):
@@ -421,21 +414,23 @@
     )
 
 
-def pack(live, geometry, first, second, target, warm):
+def pack(sent, live, geometry, index, value):
     rows = pl.BlockSpec((PART * BLK, LANES), lambda i: (i, 0))
-    out = pl.BlockSpec((PART, 64, LANES), lambda i: (i, 0, 0))
     return pl.pallas_call(
-        pack_kernel,
+        functools.partial(pack_kernel, sent),
         grid=(PEERS // PART,),
-        in_specs=[SMEM, pl.BlockSpec((9, PART * BLK * LANES), lambda i: (0, i))] + [rows] * 4,
-        out_specs=(out, out),
-        out_shape=(shape(PEERS, 64, LANES),) * 2,
-        scratch_shapes=[pltpu.VMEM((64, LANES), F32)] * 2 + [pltpu.VMEM((16, 8, LANES), F32)] * 4,
+        in_specs=[SMEM, pl.BlockSpec((9, PART * BLK * LANES), lambda i: (0, i)), rows, rows],
+        out_specs=pl.BlockSpec((PART, 64, LANES), lambda i: (i, 0, 0)),
+        out_shape=shape(PEERS, 64, LANES),
+        scratch_shapes=[pltpu.VMEM((64, LANES), F32), pltpu.VMEM((16, 8, LANES), F32)] * WAYS,
         compiler_params=pltpu.CompilerParams(
-            dimension_semantics=("arbitrary",), vmem_limit_bytes=60 << 20
+            dimension_semantics=("arbitrary",), vmem_limit_bytes=(60 if sent else 16) << 20
         ),
-        name="pack",
-    )(live, geometry, first, second, target, warm)
+        cost_estimate=pl.CostEstimate(
+            flops=10_000_000, bytes_accessed=4_000_000, transcendentals=0
+        ),
+        name="pack_sent" if sent else "pack_local",
+    )(live, geometry, index, value)
 
 
 def on_device(
@@ -451,9 +446,8 @@
             shape(groups, terms, 8, LANES), shape(length, LANES, dtype=jnp.int32), stream, stream, stream
         ]
 
-    send, local = pack(
-        live_pairs, geometry, table(first_body), table(second_body), table(target_speed), warm
-    )
+    send = pack(True, live_pairs, geometry, table(second_body), warm)
+    local = pack(False, live_pairs, geometry, table(first_body), table(target_speed))
     received = lax.all_to_all(send, "owner", split_axis=0, concat_axis=0, tiled=True)
     *side_a, meta_a, share, vel, prop = call(
         first_kernel,
@@ -468,10 +462,10 @@
     )(live_pairs, send, local, velocity, properties)
     *side_b, meta_b, share = call(
         second_kernel,
-        [VMEM] * 4,
+        [VMEM, pl.BlockSpec(memory_space=pltpu.HBM), VMEM, VMEM],
         streams(ROWS // 8, 6, STAGE)
         + [shape(PEERS + 1, dtype=jnp.int32), shape(PEERS, 4, 8, LANES)],
-        [pltpu.VMEM((STAGE * 8, LANES), F32), words, pltpu.SMEM((PEERS,), jnp.int32)],
+        [pltpu.VMEM((STAGE * 8, LANES), F32), words, pltpu.SMEM((PEERS,), jnp.int32), pltpu.SemaphoreType.DMA],
         name="second",
     )(received, share, vel, prop)
     n_sub = lax.axis_size("sub")

time: 150 us -> 148 us (0.987)
  Pallas kernels: 39.8 us -> 46.7 us
  local copies, waits for them, and re-layouts: 5.32 us -> 0.04 us
  starting transfers between devices: 22.3 us -> 18.4 us
  blocking collectives: 58.7 us -> 56.4 us
  waiting for transfers between devices: 22.3 us -> 24.2 us
    unnamed x36 -> x16, local copies, waits for them, and re-layouts: 5.32 us -> 0.04 us
    ppermute x12, starting transfers between devices: 12.5 us -> 8.75 us  [on_device(): lax.ppermute(own, 'sub', [(i, (i + d) % n_sub) for i in range(n_sub)])]
    pallas_call x2 -> x3, Pallas kernels: 9.38 us -> 12.1 us  [the longest x2 6.64 us: pack(): pl.pallas_call(functools.partial(pack_kernel, sent), grid=(PEERS // PART,...]
    all_to_all x4, blocking collectives: 58.7 us -> 56.4 us  [on_device(): lax.all_to_all(share, 'owner', split_axis=0, concat_axis=0, tiled=True)]
    pallas_call x3, Pallas kernels: 8.55 us -> 10.1 us  [on_device(): call(gather_kernel, [SMEM] + [VMEM] * 8, [shape(96, LANES), stream, shape...]
  transfers between devices with their start and end apart: 13 -> 13, of which waited for: 12 -> 11; matrix products, arithmetic and copies ran while one was open for 0% -> 0% of each run, Pallas kernels for 5% -> 7%
where the time goes in v4:
time: 148 us; the launch traced here: 147 us
  blocking collectives  56.4 us (38%)
  Pallas kernels  46.7 us (32%)
  waiting for transfers between devices  24.2 us (16%)
  starting transfers between devices  18.4 us (12%)
    all_to_all x4, blocking collectives, on_device(): lax.all_to_all(share, 'owner', split_axis=0, concat_axis=0, tiled=True)  56.4 us
    ppermute x12, waiting for transfers between devices, on_device(): lax.ppermute(own, 'sub', [(i, (i + d) % n_sub) for i in range(n_sub)])  14.4 us
    pallas_call x3, Pallas kernels, on_device(): call(functools.partial(apply_kernel, False), [SMEM] + [VMEM] * 6, [shape(...  11.5 us
    pallas_call x3, Pallas kernels, on_device(): call(gather_kernel, [SMEM] + [VMEM] * 8, [shape(96, LANES), stream, shape...  10.1 us
    all_to_all x1, waiting for transfers between devices, on_device(): lax.all_to_all(send, 'owner', split_axis=0, concat_axis=0, tiled=True)  9.8 us
    all_to_all x1, starting transfers between devices, on_device(): lax.all_to_all(send, 'owner', split_axis=0, concat_axis=0, tiled=True)  9.65 us
    ppermute x12, starting transfers between devices, on_device(): lax.ppermute(own, 'sub', [(i, (i + d) % n_sub) for i in range(n_sub)])  8.75 us
    pallas_call x2, Pallas kernels, pack(): pl.pallas_call(functools.partial(pack_kernel, sent), grid=(PEERS // PART,...  6.64 us
  transfers between devices with their start and end apart: 13, of which 11 were waited for; matrix products, arithmetic and copies ran while one was open for 0% of the time, Pallas kernels for 7%

profile of v4, /device:TPU:1, one launch (start us, length us, event | category | flops | bytes accessed | tf_op | source)
XLA Modules:
  0.0 146.6 jit_solution(13867827410923698011)
XLA Ops:
  0.6 0.0 copy-start.1
  0.6 0.0 copy-start.3
  0.7 0.0 copy-start.4
  0.7 0.0 copy-start.7
  0.7 4.5 %pack_sent.1.send = f32[32,64,128]{2,1,0:T(8,128)} custom-call(s32[256]{0:T(256)} %live.7, f32[9,32768]{1,0:T(8,128)} %geom.3, s32[256,128]{1,0:T(8,128)} %bitcast.9, f32[256,128]{1,0:T(8,128)} %bitcast.5), custom_call_target="tpu_custom_call" | custom-call | flops 10000000 | bytes 4000000 | tf_op jit(solution)/shard_map/pack_sent/pallas_call | solution.py:419
  5.2 9.7 %all-to-all-start = ((f32[32,64,128]{2,1,0:T(8,128)}), f32[32,64,128]{2,1,0:T(8,128)}, u32[]{:S(2)}, u32[]{:S(2)}) async-start(f32[32,64,128]{2,1,0:T(8,128)} %pack_sent.1.send), calls=%async_computation | async-start | bytes 2097152 | tf_op jit(solution)/shard_map/all_to_all | solution.py:451
  14.9 0.0 copy-start
  14.9 0.0 copy-start.5
  14.9 0.0 copy-start.6
  14.9 0.0 copy-done.1
  14.9 0.0 copy-done.3
  14.9 0.0 copy-done.4
  14.9 0.0 copy-done.7
  14.9 2.1 %pack_local.1.local = f32[32,64,128]{2,1,0:T(8,128)S(1)} custom-call(s32[256]{0:T(256)S(1)} %copy-done.7, f32[9,32768]{1,0:T(8,128)S(1)} %copy-done.1, s32[256,128]{1,0:T(8,128)S(1)} %bitcast.7, f32[256,128]{1,0:T(8,128)S(1)} %bitcast.8), custom_call_target="tpu_custom_call" | custom-call | flops 10000000 | bytes 4000000 | tf_op jit(solution)/shard_map/pack_local/pallas_call | solution.py:419
  17.1 0.0 copy-done
  17.1 0.0 copy-done.5
  17.1 0.0 copy-done.6
  17.1 5.2 %first.1 = (f32[32,7,8,128]{3,2,1,0:T(8,128)S(1)}, s32[272,128]{1,0:T(8,128)S(1)}, f32[272,128]{1,0:T(8,128)S(1)}, f32[272,128]{1,0:T(8,128)S(1)}, f32[272,128]{...) custom-call(s32[256]{0:T(256)S(1)} %copy-done.7, ...), custom_call_target="tpu_custom_call" | custom-call | flops 10000000 | bytes 4000000 | tf_op jit(solution)/shard_map/first/pallas_call | solution.py:452
  22.3 9.8 %all-to-all-done.received = f32[32,64,128]{2,1,0:T(8,128)} async-done(((f32[32,64,128]{2,1,0:T(8,128)}), f32[32,64,128]{2,1,0:T(8,128)}, u32[]{:S(2)}, u32[]{:S(2)}) %all-to-all-start) | async-done | bytes 1048608 | tf_op jit(solution)/shard_map/all_to_all | solution.py:451
  32.1 5.4 %second.1 = (f32[32,6,8,128]{3,2,1,0:T(8,128)S(1)}, s32[272,128]{1,0:T(8,128)S(1)}, f32[272,128]{1,0:T(8,128)S(1)}, f32[272,128]{1,0:T(8,128)S(1)}, f32[272,128]...) custom-call(f32[32,64,128]{2,1,0:T(8,128)} %all-to-all-done.received, ...), custom_call_target="tpu_custom_call" | custom-call | flops 10000000 | bytes 4000000 | tf_op jit(solution)/shard_map/second/pallas_call | solution.py:463
  37.5 15.6 %all_to_all.25.refs_12_ = f32[32,4,8,128]{3,2,1,0:T(8,128)S(1)} all-to-all(f32[32,4,8,128]{3,2,1,0:T(8,128)S(1)} %get-tuple-element.54), channel_id=1, replica_groups=mesh['owner'=32,'sub'=4] {'owner'}, dimensions={0} | all-to-all | bytes 1048576 | tf_op jit(solution)/shard_map/all_to_all | solution.py:475
  53.1 4.8 %apply.4 = (f32[96,128]{1,0:T(8,128)S(1)}, f32[560,128]{1,0:T(8,128)S(1)}, f32[560,128]{1,0:T(8,128)S(1)}, f32[70,7,8,128]{3,2,1,0:T(8,128)S(1)}, s32[560,128]{1,0:T(8,128)S(1)}, /*index=5*/s32[65]{0:T(128)S(1)}) custom-call(s32[33]{0:T(128)S(1)} %get-tuple-element.39.refs_0_, s32[33]{0:T(128)S(1)} %get-tuple-element.43.refs_1_, ...), custom_call_target="tpu_custom_call" | custom-call | flops 10000000 | bytes 4000000 | tf_op jit(solution)/shard_map/apply/pallas_call | solution.py:477
  57.8 1.2 collective-permute-start.2
  59.1 1.7 %collective-permute-start.1 = (f32[96,128]{1,0:T(8,128)S(1)}, f32[96,128]{1,0:T(8,128)S(1)}, u32[]{:S(2)}, u32[]{:S(2)}) collective-permute-start(f32[96,128]{1,0:T(8,128)S(1)} %get-tuple-element.56.j0), channel_id=1, source_target_pairs={{0,2},{1,3},{2,0},{3,1},{4,6},{5,7},{6,4},{7,5},{8,10},{9,11},{10,... | collective-permute-start | bytes 147464 | tf_op jit(solution)/shard_map/ppermute | solution.py:495
  60.7 0.8 collective-permute-start
  61.5 0.0 collective-permute-done.2.j3
  61.5 2.0 %collective-permute-done.1.j2 = f32[96,128]{1,0:T(8,128)S(1)} collective-permute-done((f32[96,128]{1,0:T(8,128)S(1)}, f32[96,128]{1,0:T(8,128)S(1)}, u32[]{:S(2)}, u32[]{:S(2)}) %collective-permute-start.1) | collective-permute-done | bytes 49184 | tf_op jit(solution)/shard_map/ppermute | solution.py:495
  63.5 1.4 collective-permute-done.j1
  64.9 3.4 %gather.3 = (f32[96,128]{1,0:T(8,128)S(1)}, f32[560,128]{1,0:T(8,128)S(1)}, f32[32,2,8,128]{3,2,1,0:T(8,128)S(1)}) custom-call(s32[65]{0:T(128)S(1)} %get-tuple-element.55.meta.refs_0_, f32[96,128]{1,0:T(8,128)S(1)} %get-tuple-element.41.vel, f32[64,128]{1,0:T(8,128)S(1)} %get-tuple-element.42.prop, f32[96,128]{1,0:T(8,128)S(1)} %get-tuple-element.56.j0, ...), custom_call_target="tpu_custom_call" | custom-call | flops 10000000 | bytes 4000000 | tf_op jit(solution)/shard_map/gather/pallas_call | solution.py:499
  68.3 14.0 %all_to_all.26.refs_6_ = f32[32,2,8,128]{3,2,1,0:T(8,128)S(1)} all-to-all(f32[32,2,8,128]{3,2,1,0:T(8,128)S(1)} %get-tuple-element.63), channel_id=1, replica_groups=mesh['owner'=32,'sub'=4] {'owner'}, dimensions={0} | all-to-all | bytes 524288 | tf_op jit(solution)/shard_map/all_to_all | solution.py:475
  82.3 3.8 %apply.5 = (f32[96,128]{1,0:T(8,128)S(1)}, f32[560,128]{1,0:T(8,128)S(1)}) custom-call(s32[65]{0:T(128)S(1)} %get-tuple-element.55.meta.refs_0_, f32[70,7,8,128]{3,2,1,0:T(8,128)S(1)} %get-tuple-element.57.x.refs_1_, s32[560,128]{1,0:T(8,128)S(1)} %get-tuple-element.58.idx.refs_2_, f32[560,128]{1,0:T(8,128)S(1)} %get-tuple-element.60.refs_3_, ...), custom_call_target="tpu_custom_call" | custom-call | flops 10000000 | bytes 4000000 | tf_op jit(solution)/shard_map/apply/pallas_call | solution.py:487
  86.1 0.1 collective-permute-start.5
  86.2 1.4 collective-permute-start.4
  87.6 0.2 collective-permute-start.3
  87.8 1.3 collective-permute-done.5.j3
  89.1 1.6 %collective-permute-done.4.j2 = f32[96,128]{1,0:T(8,128)S(1)} collective-permute-done((f32[96,128]{1,0:T(8,128)S(1)}, f32[96,128]{1,0:T(8,128)S(1)}, u32[]{:S(2)}, u32[]{:S(2)}) %collective-permute-start.4) | collective-permute-done | bytes 49184 | tf_op jit(solution)/shard_map/ppermute | solution.py:495
  90.7 2.1 %collective-permute-done.3.j1 = f32[96,128]{1,0:T(8,128)S(1)} collective-permute-done((f32[96,128]{1,0:T(8,128)S(1)}, f32[96,128]{1,0:T(8,128)S(1)}, u32[]{:S(2)}, u32[]{:S(2)}) %collective-permute-start.3) | collective-permute-done | bytes 49184 | tf_op jit(solution)/shard_map/ppermute | solution.py:495
  92.8 3.4 %gather.4 = (f32[96,128]{1,0:T(8,128)S(1)}, f32[560,128]{1,0:T(8,128)S(1)}, f32[32,2,8,128]{3,2,1,0:T(8,128)S(1)}) custom-call(s32[65]{0:T(128)S(1)} %get-tuple-element.55.meta.refs_0_, f32[96,128]{1,0:T(8,128)S(1)} %get-tuple-element.59.vel, f32[64,128]{1,0:T(8,128)S(1)} %get-tuple-element.42.prop, f32[96,128]{1,0:T(8,128)S(1)} %get-tuple-element.64.j0, ...), custom_call_target="tpu_custom_call" | custom-call | flops 10000000 | bytes 4000000 | tf_op jit(solution)/shard_map/gather/pallas_call | solution.py:499
  96.2 13.0 %all_to_all.27.refs_6_ = f32[32,2,8,128]{3,2,1,0:T(8,128)S(1)} all-to-all(f32[32,2,8,128]{3,2,1,0:T(8,128)S(1)} %get-tuple-element.68), channel_id=1, replica_groups=mesh['owner'=32,'sub'=4] {'owner'}, dimensions={0} | all-to-all | bytes 524288 | tf_op jit(solution)/shard_map/all_to_all | solution.py:475
  109.2 3.8 %apply.6 = (f32[96,128]{1,0:T(8,128)S(1)}, f32[560,128]{1,0:T(8,128)S(1)}) custom-call(s32[65]{0:T(128)S(1)} %get-tuple-element.55.meta.refs_0_, f32[70,7,8,128]{3,2,1,0:T(8,128)S(1)} %get-tuple-element.57.x.refs_1_, s32[560,128]{1,0:T(8,128)S(1)} %get-tuple-element.58.idx.refs_2_, f32[560,128]{1,0:T(8,128)S(1)} %get-tuple-element.66.refs_3_, ...), custom_call_target="tpu_custom_call" | custom-call | flops 10000000 | bytes 4000000 | tf_op jit(solution)/shard_map/apply/pallas_call | solution.py:487
  113.0 0.3 collective-permute-start.8
  113.3 1.4 collective-permute-start.7
  114.8 0.0 collective-permute-start.6
  114.8 1.3 collective-permute-done.8.j3
  116.0 1.7 %collective-permute-done.7.j2 = f32[96,128]{1,0:T(8,128)S(1)} collective-permute-done((f32[96,128]{1,0:T(8,128)S(1)}, f32[96,128]{1,0:T(8,128)S(1)}, u32[]{:S(2)}, u32[]{:S(2)}) %collective-permute-start.7) | collective-permute-done | bytes 49184 | tf_op jit(solution)/shard_map/ppermute | solution.py:495
  117.8 1.5 %collective-permute-done.6.j1 = f32[96,128]{1,0:T(8,128)S(1)} collective-permute-done((f32[96,128]{1,0:T(8,128)S(1)}, f32[96,128]{1,0:T(8,128)S(1)}, u32[]{:S(2)}, u32[]{:S(2)}) %collective-permute-start.6) | collective-permute-done | bytes 49184 | tf_op jit(solution)/shard_map/ppermute | solution.py:495
  119.3 3.4 %gather.5 = (f32[96,128]{1,0:T(8,128)S(1)}, f32[560,128]{1,0:T(8,128)S(1)}, f32[32,2,8,128]{3,2,1,0:T(8,128)S(1)}) custom-call(s32[65]{0:T(128)S(1)} %get-tuple-element.55.meta.refs_0_, f32[96,128]{1,0:T(8,128)S(1)} %get-tuple-element.65.vel, f32[64,128]{1,0:T(8,128)S(1)} %get-tuple-element.42.prop, f32[96,128]{1,0:T(8,128)S(1)} %get-tuple-element.69.j0, ...), custom_call_target="tpu_custom_call" | custom-call | flops 10000000 | bytes 4000000 | tf_op jit(solution)/shard_map/gather/pallas_call | solution.py:499
  122.7 0.0 copy-start.2
  122.7 13.8 %all_to_all.28.refs_6_ = f32[32,2,8,128]{3,2,1,0:T(8,128)S(1)} all-to-all(f32[32,2,8,128]{3,2,1,0:T(8,128)S(1)} %get-tuple-element.73), channel_id=1, replica_groups=mesh['owner'=32,'sub'=4] {'owner'}, dimensions={0} | all-to-all | bytes 524288 | tf_op jit(solution)/shard_map/all_to_all | solution.py:475
  136.5 3.8 %apply.7 = (f32[96,128]{1,0:T(8,128)S(1)}, f32[560,128]{1,0:T(8,128)S(1)}) custom-call(s32[65]{0:T(128)S(1)} %get-tuple-element.55.meta.refs_0_, f32[70,7,8,128]{3,2,1,0:T(8,128)S(1)} %get-tuple-element.57.x.refs_1_, s32[560,128]{1,0:T(8,128)S(1)} %get-tuple-element.58.idx.refs_2_, f32[560,128]{1,0:T(8,128)S(1)} %get-tuple-element.71.refs_3_, ...), custom_call_target="tpu_custom_call" | custom-call | flops 10000000 | bytes 4000000 | tf_op jit(solution)/shard_map/apply/pallas_call | solution.py:487
  140.4 0.1 collective-permute-start.11
  140.4 1.4 collective-permute-start.10
  141.8 0.3 collective-permute-start.9
  142.1 0.0 copy-done.2
  142.1 2.4 %unpack.1 = f32[256,128]{1,0:T(8,128)} custom-call(s32[256]{0:T(256)S(1)} %copy-done.7, s32[65]{0:T(128)S(1)} %get-tuple-element.55.meta.refs_0_, f32[560,128]{1,0:T(8,128)S(1)} %get-tuple-element.75.imp, f32[256,128]{1,0:T(8,128)S(1)} %bitcast.6), custom_call_target="tpu_custom_call" | custom-call | flops 10000000 | bytes 4000000 | tf_op jit(solution)/shard_map/unpack/pallas_call | solution.py:506
  144.5 0.0 collective-permute-done.11.j3
  144.5 0.5 collective-permute-done.10.j2
  145.0 1.0 collective-permute-done.9.j1
  146.0 0.7 final.1
Async XLA Ops:
  0.6 14.3 %copy-start.1 = (f32[9,32768]{1,0:T(8,128)S(1)}, f32[9,32768]{1,0:T(8,128)}, u32[]{:S(2)}) copy-start(f32[9,32768]{1,0:T(8,128)} %geom.3) | copy-start | bytes 3538948
  0.6 14.3 %copy-start.3 = (s32[32768]{0:T(1024)S(1)}, s32[32768]{0:T(1024)}, u32[]{:S(2)}) copy-start(s32[32768]{0:T(1024)} %param.10) | copy-start | bytes 393220
  0.7 14.3 %copy-start.4 = (f32[32768]{0:T(1024)S(1)}, f32[32768]{0:T(1024)}, u32[]{:S(2)}) copy-start(f32[32768]{0:T(1024)} %param.13) | copy-start | bytes 393220
  0.7 14.3 %copy-start.7 = (s32[256]{0:T(256)S(1)}, s32[256]{0:T(256)}, u32[]{:S(2)}) copy-start(s32[256]{0:T(256)} %live.7) | copy-start | bytes 3076
  5.2 26.9 %all-to-all-start = ((f32[32,64,128]{2,1,0:T(8,128)}), f32[32,64,128]{2,1,0:T(8,128)}, u32[]{:S(2)}, u32[]{:S(2)}) async-start(f32[32,64,128]{2,1,0:T(8,128)} %pack_sent.1.send), calls=%async_computation | async-start | bytes 2097152 | tf_op jit(solution)/shard_map/all_to_all | solution.py:451
  14.9 2.2 %copy-start = (f32[32,64,128]{2,1,0:T(8,128)S(1)}, f32[32,64,128]{2,1,0:T(8,128)}, u32[]{:S(2)}) copy-start(f32[32,64,128]{2,1,0:T(8,128)} %pack_sent.1.send) | copy-start | bytes 3145732
  14.9 2.2 %copy-start.5 = (f32[6,2048]{1,0:T(8,128)S(1)}, f32[6,2048]{1,0:T(8,128)}, u32[]{:S(2)}) copy-start(f32[6,2048]{1,0:T(8,128)} %velocity.1) | copy-start | bytes 147460
  14.9 2.2 %copy-start.6 = (f32[4,2048]{1,0:T(4,128)S(1)}, f32[4,2048]{1,0:T(4,128)}, u32[]{:S(2)}) copy-start(f32[4,2048]{1,0:T(4,128)} %properties.1) | copy-start | bytes 98308
  57.8 3.7 %collective-permute-start.2 = (f32[96,128]{1,0:T(8,128)S(1)}, f32[96,128]{1,0:T(8,128)S(1)}, u32[]{:S(2)}, u32[]{:S(2)}) collective-permute-start(f32[96,128]{1,0:T(8,128)S(1)} %get-tuple-element.56.j0), channel_id=1, source_target_pairs={{0,3},{1,0},{2,1},{3,2},{4,7},{5,4},{6,5},{7,6},{8,11},{9,8},{10,9... | collective-permute-start | bytes 147464 | tf_op jit(solution)/shard_map/ppermute | solution.py:495
  59.1 4.4 %collective-permute-start.1 = (f32[96,128]{1,0:T(8,128)S(1)}, f32[96,128]{1,0:T(8,128)S(1)}, u32[]{:S(2)}, u32[]{:S(2)}) collective-permute-start(f32[96,128]{1,0:T(8,128)S(1)} %get-tuple-element.56.j0), channel_id=1, source_target_pairs={{0,2},{1,3},{2,0},{3,1},{4,6},{5,7},{6,4},{7,5},{8,10},{9,11},{10,... | collective-permute-start | bytes 147464 | tf_op jit(solution)/shard_map/ppermute | solution.py:495
  60.7 4.2 %collective-permute-start = (f32[96,128]{1,0:T(8,128)S(1)}, f32[96,128]{1,0:T(8,128)S(1)}, u32[]{:S(2)}, u32[]{:S(2)}) collective-permute-start(f32[96,128]{1,0:T(8,128)S(1)} %get-tuple-element.56.j0), channel_id=1, source_target_pairs={{0,1},{1,2},{2,3},{3,0},{4,5},{5,6},{6,7},{7,4},{8,9},{9,10},{10,1... | collective-permute-start | bytes 147464 | tf_op jit(solution)/shard_map/ppermute | solution.py:495
  86.1 3.0 %collective-permute-start.5 = (f32[96,128]{1,0:T(8,128)S(1)}, f32[96,128]{1,0:T(8,128)S(1)}, u32[]{:S(2)}, u32[]{:S(2)}) collective-permute-start(f32[96,128]{1,0:T(8,128)S(1)} %get-tuple-element.64.j0), channel_id=1, source_target_pairs={{0,3},{1,0},{2,1},{3,2},{4,7},{5,4},{6,5},{7,6},{8,11},{9,8},{10,9... | collective-permute-start | bytes 147464 | tf_op jit(solution)/shard_map/ppermute | solution.py:495
  86.2 4.5 %collective-permute-start.4 = (f32[96,128]{1,0:T(8,128)S(1)}, f32[96,128]{1,0:T(8,128)S(1)}, u32[]{:S(2)}, u32[]{:S(2)}) collective-permute-start(f32[96,128]{1,0:T(8,128)S(1)} %get-tuple-element.64.j0), channel_id=1, source_target_pairs={{0,2},{1,3},{2,0},{3,1},{4,6},{5,7},{6,4},{7,5},{8,10},{9,11},{10,... | collective-permute-start | bytes 147464 | tf_op jit(solution)/shard_map/ppermute | solution.py:495
  87.6 5.3 %collective-permute-start.3 = (f32[96,128]{1,0:T(8,128)S(1)}, f32[96,128]{1,0:T(8,128)S(1)}, u32[]{:S(2)}, u32[]{:S(2)}) collective-permute-start(f32[96,128]{1,0:T(8,128)S(1)} %get-tuple-element.64.j0), channel_id=1, source_target_pairs={{0,1},{1,2},{2,3},{3,0},{4,5},{5,6},{6,7},{7,4},{8,9},{9,10},{10,1... | collective-permute-start | bytes 147464 | tf_op jit(solution)/shard_map/ppermute | solution.py:495
  113.0 3.0 %collective-permute-start.8 = (f32[96,128]{1,0:T(8,128)S(1)}, f32[96,128]{1,0:T(8,128)S(1)}, u32[]{:S(2)}, u32[]{:S(2)}) collective-permute-start(f32[96,128]{1,0:T(8,128)S(1)} %get-tuple-element.69.j0), channel_id=1, source_target_pairs={{0,3},{1,0},{2,1},{3,2},{4,7},{5,4},{6,5},{7,6},{8,11},{9,8},{10,9... | collective-permute-start | bytes 147464 | tf_op jit(solution)/shard_map/ppermute | solution.py:495
  113.3 4.4 %collective-permute-start.7 = (f32[96,128]{1,0:T(8,128)S(1)}, f32[96,128]{1,0:T(8,128)S(1)}, u32[]{:S(2)}, u32[]{:S(2)}) collective-permute-start(f32[96,128]{1,0:T(8,128)S(1)} %get-tuple-element.69.j0), channel_id=1, source_target_pairs={{0,2},{1,3},{2,0},{3,1},{4,6},{5,7},{6,4},{7,5},{8,10},{9,11},{10,... | collective-permute-start | bytes 147464 | tf_op jit(solution)/shard_map/ppermute | solution.py:495
  114.8 4.5 %collective-permute-start.6 = (f32[96,128]{1,0:T(8,128)S(1)}, f32[96,128]{1,0:T(8,128)S(1)}, u32[]{:S(2)}, u32[]{:S(2)}) collective-permute-start(f32[96,128]{1,0:T(8,128)S(1)} %get-tuple-element.69.j0), channel_id=1, source_target_pairs={{0,1},{1,2},{2,3},{3,0},{4,5},{5,6},{6,7},{7,4},{8,9},{9,10},{10,1... | collective-permute-start | bytes 147464 | tf_op jit(solution)/shard_map/ppermute | solution.py:495
  122.7 19.4 %copy-start.2 = (f32[32768]{0:T(1024)S(1)}, f32[32768]{0:T(1024)}, u32[]{:S(2)}) copy-start(f32[32768]{0:T(1024)} %param.14) | copy-start | bytes 393220
  140.4 4.1 %collective-permute-start.11 = (f32[96,128]{1,0:T(8,128)S(1)}, f32[96,128]{1,0:T(8,128)S(1)}, u32[]{:S(2)}, u32[]{:S(2)}) collective-permute-start(f32[96,128]{1,0:T(8,128)S(1)} %get-tuple-element.74.j0), channel_id=1, source_target_pairs={{0,3},{1,0},{2,1},{3,2},{4,7},{5,4},{6,5},{7,6},{8,11},{9,8},{10,9... | collective-permute-start | bytes 147464 | tf_op jit(solution)/shard_map/ppermute | solution.py:495
  140.4 4.5 %collective-permute-start.10 = (f32[96,128]{1,0:T(8,128)S(1)}, f32[96,128]{1,0:T(8,128)S(1)}, u32[]{:S(2)}, u32[]{:S(2)}) collective-permute-start(f32[96,128]{1,0:T(8,128)S(1)} %get-tuple-element.74.j0), channel_id=1, source_target_pairs={{0,2},{1,3},{2,0},{3,1},{4,6},{5,7},{6,4},{7,5},{8,10},{9,11},{10,... | collective-permute-start | bytes 147464 | tf_op jit(solution)/shard_map/ppermute | solution.py:495
  141.8 4.2 %collective-permute-start.9 = (f32[96,128]{1,0:T(8,128)S(1)}, f32[96,128]{1,0:T(8,128)S(1)}, u32[]{:S(2)}, u32[]{:S(2)}) collective-permute-start(f32[96,128]{1,0:T(8,128)S(1)} %get-tuple-element.74.j0), channel_id=1, source_target_pairs={{0,1},{1,2},{2,3},{3,0},{4,5},{5,6},{6,7},{7,4},{8,9},{9,10},{10,1... | collective-permute-start | bytes 147464 | tf_op jit(solution)/shard_map/ppermute | solution.py:495

commit v5 on v4

--- a/solution.py
+++ b/solution.py
@@ -18,11 +18,11 @@
 ROWS = PEERS * BLK
 STAGE = ROWS + 2 * BLK
 HALF = float(1 << 20)
-CHUNK = 6
+CHUNK = 5
 GROUPS = 2 * ROWS // 8 + CHUNK
 STREAM = GROUPS * 8
 COUNT = 2 * PEERS
-PART = 8
+PART = 16
 WAYS = 4
 VMEM = pl.BlockSpec(memory_space=pltpu.VMEM)
 SMEM = pl.BlockSpec(memory_space=pltpu.SMEM)
@@ -203,9 +203,15 @@
 
 
 def second_kernel(
-    received, share_first, vel, prop,
-    x_out, idx_out, imp_out, u_out, m_out, meta, share, d0, words, used, sem,
+    arrived, share_first, vel, prop,
+    x_out, idx_out, imp_out, u_out, m_out, meta, share, received, d0, words, used, sem, sems,
 ):
+    piece = PEERS // 4
+    pieces = []
+    for k in range(4):
+        part = pl.ds(k * piece, piece)
+        pieces.append(pltpu.make_async_copy(arrived.at[part], received.at[part], sems.at[k]))
+        pieces[k].start()
     copy = pltpu.make_async_copy(share_first, share.at[:, 0:2], sem)
     copy.start()
 
@@ -214,7 +220,9 @@
         used[q] = jnp.max(jnp.where(flags >= 0.0, row_iota() + 1, 0))
         return 0
 
-    lax.fori_loop(0, PEERS, count_rows, 0, unroll=8)
+    for k in range(4):
+        pieces[k].wait()
+        lax.fori_loop(k * piece, (k + 1) * piece, count_rows, 0, unroll=8)
 
     def one_partner(q, base):
         meta[q] = base
@@ -462,10 +470,13 @@
     )(live_pairs, send, local, velocity, properties)
     *side_b, meta_b, share = call(
         second_kernel,
-        [VMEM, pl.BlockSpec(memory_space=pltpu.HBM), VMEM, VMEM],
+        [pl.BlockSpec(memory_space=pltpu.HBM)] * 2 + [VMEM] * 2,
         streams(ROWS // 8, 6, STAGE)
         + [shape(PEERS + 1, dtype=jnp.int32), shape(PEERS, 4, 8, LANES)],
-        [pltpu.VMEM((STAGE * 8, LANES), F32), words, pltpu.SMEM((PEERS,), jnp.int32), pltpu.SemaphoreType.DMA],
+        [
+            pltpu.VMEM((PEERS, 64, LANES), F32), pltpu.VMEM((STAGE * 8, LANES), F32), words,
+            pltpu.SMEM((PEERS,), jnp.int32), pltpu.SemaphoreType.DMA, pltpu.SemaphoreType.DMA((4,)),
+        ],
         name="second",
     )(received, share, vel, prop)
     n_sub = lax.axis_size("sub")

time: 148 us -> 148 us (level)
  blocking collectives: 56.4 us -> 53.1 us
  waiting for transfers between devices: 24.2 us -> 27.1 us
  starting transfers between devices: 18.4 us -> 20 us
    all_to_all x4, blocking collectives: 56.4 us -> 53.1 us  [on_device(): lax.all_to_all(share, 'owner', split_axis=0, concat_axis=0, tiled=True)]
    ppermute x12, waiting for transfers between devices: 14.4 us -> 16.7 us  [on_device(): lax.ppermute(own, 'sub', [(i, (i + d) % n_sub) for i in range(n_sub)])]
    ppermute x12, starting transfers between devices: 8.75 us -> 10.3 us  [on_device(): lax.ppermute(own, 'sub', [(i, (i + d) % n_sub) for i in range(n_sub)])]
  transfers between devices with their start and end apart: 13 -> 13, of which waited for: 11 -> 11; matrix products, arithmetic and copies ran while one was open for 0% -> 0% of each run, Pallas kernels for 7% -> 6%
where the time goes in v5:
time: 148 us; the launch traced here: 147 us
  blocking collectives  53.1 us (36%)
  Pallas kernels  46 us (31%)
  waiting for transfers between devices  27.1 us (18%)
  starting transfers between devices  20 us (14%)
    all_to_all x4, blocking collectives, on_device(): lax.all_to_all(share, 'owner', split_axis=0, concat_axis=0, tiled=True)  53.1 us
    ppermute x12, waiting for transfers between devices, on_device(): lax.ppermute(own, 'sub', [(i, (i + d) % n_sub) for i in range(n_sub)])  16.7 us
    pallas_call x3, Pallas kernels, on_device(): call(functools.partial(apply_kernel, False), [SMEM] + [VMEM] * 6, [shape(...  12.3 us
    all_to_all x1, waiting for transfers between devices, on_device(): lax.all_to_all(send, 'owner', split_axis=0, concat_axis=0, tiled=True)  10.4 us
    ppermute x12, starting transfers between devices, on_device(): lax.ppermute(own, 'sub', [(i, (i + d) % n_sub) for i in range(n_sub)])  10.3 us
    all_to_all x1, starting transfers between devices, on_device(): lax.all_to_all(send, 'owner', split_axis=0, concat_axis=0, tiled=True)  9.65 us
    pallas_call x3, Pallas kernels, on_device(): call(gather_kernel, [SMEM] + [VMEM] * 8, [shape(96, LANES), stream, shape...  9.47 us
    pallas_call x2, Pallas kernels, pack(): pl.pallas_call(functools.partial(pack_kernel, sent), grid=(PEERS // PART,...  5.78 us
  transfers between devices with their start and end apart: 13, of which 11 were waited for; matrix products, arithmetic and copies ran while one was open for 0% of the time, Pallas kernels for 6%

profile of v5, /device:TPU:1, one launch (start us, length us, event | category | flops | bytes accessed | tf_op | source)
XLA Modules:
  0.0 147.2 jit_solution(6999657616604433642)
XLA Ops:
  0.6 0.0 copy-start.1
  0.6 0.0 copy-start.3
  0.7 0.0 copy-start.4
  0.7 0.0 copy-start.7
  0.7 3.8 %pack_sent.1.send = f32[32,64,128]{2,1,0:T(8,128)} custom-call(s32[256]{0:T(256)} %live.7, f32[9,32768]{1,0:T(8,128)} %geom.3, s32[256,128]{1,0:T(8,128)} %bitcast.9, f32[256,128]{1,0:T(8,128)} %bitcast.5), custom_call_target="tpu_custom_call" | custom-call | flops 10000000 | bytes 4000000 | tf_op jit(solution)/shard_map/pack_sent/pallas_call | solution.py:427
  4.4 9.7 %all-to-all-start = ((f32[32,64,128]{2,1,0:T(8,128)}), f32[32,64,128]{2,1,0:T(8,128)}, u32[]{:S(2)}, u32[]{:S(2)}) async-start(f32[32,64,128]{2,1,0:T(8,128)} %pack_sent.1.send), calls=%async_computation | async-start | bytes 2097152 | tf_op jit(solution)/shard_map/all_to_all | solution.py:459
  14.1 0.0 copy-start
  14.1 0.0 copy-start.5
  14.1 0.0 copy-start.6
  14.1 0.0 copy-done.1
  14.1 0.0 copy-done.3
  14.2 0.0 copy-done.4
  14.2 0.0 copy-done.7
  14.2 2.0 %pack_local.1.local = f32[32,64,128]{2,1,0:T(8,128)S(1)} custom-call(s32[256]{0:T(256)S(1)} %copy-done.7, f32[9,32768]{1,0:T(8,128)S(1)} %copy-done.1, s32[256,128]{1,0:T(8,128)S(1)} %bitcast.7, f32[256,128]{1,0:T(8,128)S(1)} %bitcast.8), custom_call_target="tpu_custom_call" | custom-call | flops 10000000 | bytes 4000000 | tf_op jit(solution)/shard_map/pack_local/pallas_call | solution.py:427
  16.2 0.0 copy-done
  16.2 0.0 copy-done.5
  16.2 0.0 copy-done.6
  16.2 4.7 %first.1 = (f32[32,7,8,128]{3,2,1,0:T(8,128)S(1)}, s32[272,128]{1,0:T(8,128)S(1)}, f32[272,128]{1,0:T(8,128)S(1)}, f32[272,128]{1,0:T(8,128)S(1)}, f32[272,128]{...) custom-call(s32[256]{0:T(256)S(1)} %copy-done.7, ...), custom_call_target="tpu_custom_call" | custom-call | flops 10000000 | bytes 4000000 | tf_op jit(solution)/shard_map/first/pallas_call | solution.py:460
  20.9 10.4 %all-to-all-done.arrived = f32[32,64,128]{2,1,0:T(8,128)} async-done(((f32[32,64,128]{2,1,0:T(8,128)}), f32[32,64,128]{2,1,0:T(8,128)}, u32[]{:S(2)}, u32[]{:S(2)}) %all-to-all-start) | async-done | bytes 1048608 | tf_op jit(solution)/shard_map/all_to_all | solution.py:459
  31.3 5.6 %second.1 = (f32[32,6,8,128]{3,2,1,0:T(8,128)S(1)}, s32[272,128]{1,0:T(8,128)S(1)}, f32[272,128]{1,0:T(8,128)S(1)}, f32[272,128]{1,0:T(8,128)S(1)}, f32[272,128]...) custom-call(f32[32,64,128]{2,1,0:T(8,128)} %all-to-all-done.arrived, ...), custom_call_target="tpu_custom_call" | custom-call | flops 10000000 | bytes 4000000 | tf_op jit(solution)/shard_map/second/pallas_call | solution.py:471
  37.0 15.1 %all_to_all.25.refs_12_ = f32[32,4,8,128]{3,2,1,0:T(8,128)S(1)} all-to-all(f32[32,4,8,128]{3,2,1,0:T(8,128)S(1)} %get-tuple-element.54), channel_id=1, replica_groups=mesh['owner'=32,'sub'=4] {'owner'}, dimensions={0} | all-to-all | bytes 1048576 | tf_op jit(solution)/shard_map/all_to_all | solution.py:486
  52.0 5.0 %apply.4 = (f32[96,128]{1,0:T(8,128)S(1)}, f32[552,128]{1,0:T(8,128)S(1)}, f32[552,128]{1,0:T(8,128)S(1)}, f32[69,7,8,128]{3,2,1,0:T(8,128)S(1)}, s32[552,128]{1,0:T(8,128)S(1)}, /*index=5*/s32[65]{0:T(128)S(1)}) custom-call(s32[33]{0:T(128)S(1)} %get-tuple-element.39.refs_0_, s32[33]{0:T(128)S(1)} %get-tuple-element.43.refs_1_, ...), custom_call_target="tpu_custom_call" | custom-call | flops 10000000 | bytes 4000000 | tf_op jit(solution)/shard_map/apply/pallas_call | solution.py:488
  57.1 2.3 %collective-permute-start.2 = (f32[96,128]{1,0:T(8,128)S(1)}, f32[96,128]{1,0:T(8,128)S(1)}, u32[]{:S(2)}, u32[]{:S(2)}) collective-permute-start(f32[96,128]{1,0:T(8,128)S(1)} %get-tuple-element.56.j0), channel_id=1, source_target_pairs={{0,3},{1,0},{2,1},{3,2},{4,7},{5,4},{6,5},{7,6},{8,11},{9,8},{10,9... | collective-permute-start | bytes 147464 | tf_op jit(solution)/shard_map/ppermute | solution.py:506
  59.4 0.6 collective-permute-start.1
  60.0 0.8 collective-permute-start
  60.8 0.0 collective-permute-done.2.j3
  60.8 3.1 %collective-permute-done.1.j2 = f32[96,128]{1,0:T(8,128)S(1)} collective-permute-done((f32[96,128]{1,0:T(8,128)S(1)}, f32[96,128]{1,0:T(8,128)S(1)}, u32[]{:S(2)}, u32[]{:S(2)}) %collective-permute-start.1) | collective-permute-done | bytes 49184 | tf_op jit(solution)/shard_map/ppermute | solution.py:506
  63.8 1.1 collective-permute-done.j1
  64.9 3.2 %gather.3 = (f32[96,128]{1,0:T(8,128)S(1)}, f32[552,128]{1,0:T(8,128)S(1)}, f32[32,2,8,128]{3,2,1,0:T(8,128)S(1)}) custom-call(s32[65]{0:T(128)S(1)} %get-tuple-element.55.meta.refs_0_, f32[96,128]{1,0:T(8,128)S(1)} %get-tuple-element.41.vel, f32[64,128]{1,0:T(8,128)S(1)} %get-tuple-element.42.prop, f32[96,128]{1,0:T(8,128)S(1)} %get-tuple-element.56.j0, ...), custom_call_target="tpu_custom_call" | custom-call | flops 10000000 | bytes 4000000 | tf_op jit(solution)/shard_map/gather/pallas_call | solution.py:510
  68.1 12.9 %all_to_all.26.refs_6_ = f32[32,2,8,128]{3,2,1,0:T(8,128)S(1)} all-to-all(f32[32,2,8,128]{3,2,1,0:T(8,128)S(1)} %get-tuple-element.63), channel_id=1, replica_groups=mesh['owner'=32,'sub'=4] {'owner'}, dimensions={0} | all-to-all | bytes 524288 | tf_op jit(solution)/shard_map/all_to_all | solution.py:486
  80.9 4.1 %apply.5 = (f32[96,128]{1,0:T(8,128)S(1)}, f32[552,128]{1,0:T(8,128)S(1)}) custom-call(s32[65]{0:T(128)S(1)} %get-tuple-element.55.meta.refs_0_, f32[69,7,8,128]{3,2,1,0:T(8,128)S(1)} %get-tuple-element.57.x.refs_1_, s32[552,128]{1,0:T(8,128)S(1)} %get-tuple-element.58.idx.refs_2_, f32[552,128]{1,0:T(8,128)S(1)} %get-tuple-element.60.refs_3_, ...), custom_call_target="tpu_custom_call" | custom-call | flops 10000000 | bytes 4000000 | tf_op jit(solution)/shard_map/apply/pallas_call | solution.py:498
  85.1 1.1 collective-permute-start.5
  86.2 0.6 collective-permute-start.4
  86.8 0.8 collective-permute-start.3
  87.6 1.3 collective-permute-done.5.j3
  88.9 1.8 %collective-permute-done.4.j2 = f32[96,128]{1,0:T(8,128)S(1)} collective-permute-done((f32[96,128]{1,0:T(8,128)S(1)}, f32[96,128]{1,0:T(8,128)S(1)}, u32[]{:S(2)}, u32[]{:S(2)}) %collective-permute-start.4) | collective-permute-done | bytes 49184 | tf_op jit(solution)/shard_map/ppermute | solution.py:506
  90.7 1.6 %collective-permute-done.3.j1 = f32[96,128]{1,0:T(8,128)S(1)} collective-permute-done((f32[96,128]{1,0:T(8,128)S(1)}, f32[96,128]{1,0:T(8,128)S(1)}, u32[]{:S(2)}, u32[]{:S(2)}) %collective-permute-start.3) | collective-permute-done | bytes 49184 | tf_op jit(solution)/shard_map/ppermute | solution.py:506
  92.3 3.2 %gather.4 = (f32[96,128]{1,0:T(8,128)S(1)}, f32[552,128]{1,0:T(8,128)S(1)}, f32[32,2,8,128]{3,2,1,0:T(8,128)S(1)}) custom-call(s32[65]{0:T(128)S(1)} %get-tuple-element.55.meta.refs_0_, f32[96,128]{1,0:T(8,128)S(1)} %get-tuple-element.59.vel, f32[64,128]{1,0:T(8,128)S(1)} %get-tuple-element.42.prop, f32[96,128]{1,0:T(8,128)S(1)} %get-tuple-element.64.j0, ...), custom_call_target="tpu_custom_call" | custom-call | flops 10000000 | bytes 4000000 | tf_op jit(solution)/shard_map/gather/pallas_call | solution.py:510
  95.5 12.5 %all_to_all.27.refs_6_ = f32[32,2,8,128]{3,2,1,0:T(8,128)S(1)} all-to-all(f32[32,2,8,128]{3,2,1,0:T(8,128)S(1)} %get-tuple-element.68), channel_id=1, replica_groups=mesh['owner'=32,'sub'=4] {'owner'}, dimensions={0} | all-to-all | bytes 524288 | tf_op jit(solution)/shard_map/all_to_all | solution.py:486
  108.0 4.1 %apply.6 = (f32[96,128]{1,0:T(8,128)S(1)}, f32[552,128]{1,0:T(8,128)S(1)}) custom-call(s32[65]{0:T(128)S(1)} %get-tuple-element.55.meta.refs_0_, f32[69,7,8,128]{3,2,1,0:T(8,128)S(1)} %get-tuple-element.57.x.refs_1_, s32[552,128]{1,0:T(8,128)S(1)} %get-tuple-element.58.idx.refs_2_, f32[552,128]{1,0:T(8,128)S(1)} %get-tuple-element.66.refs_3_, ...), custom_call_target="tpu_custom_call" | custom-call | flops 10000000 | bytes 4000000 | tf_op jit(solution)/shard_map/apply/pallas_call | solution.py:498
  112.1 1.1 collective-permute-start.8
  113.2 0.4 collective-permute-start.7
  113.6 0.5 collective-permute-start.6
  114.2 1.7 %collective-permute-done.8.j3 = f32[96,128]{1,0:T(8,128)S(1)} collective-permute-done((f32[96,128]{1,0:T(8,128)S(1)}, f32[96,128]{1,0:T(8,128)S(1)}, u32[]{:S(2)}, u32[]{:S(2)}) %collective-permute-start.8) | collective-permute-done | bytes 49184 | tf_op jit(solution)/shard_map/ppermute | solution.py:506
  115.9 1.8 %collective-permute-done.7.j2 = f32[96,128]{1,0:T(8,128)S(1)} collective-permute-done((f32[96,128]{1,0:T(8,128)S(1)}, f32[96,128]{1,0:T(8,128)S(1)}, u32[]{:S(2)}, u32[]{:S(2)}) %collective-permute-start.7) | collective-permute-done | bytes 49184 | tf_op jit(solution)/shard_map/ppermute | solution.py:506
  117.7 1.6 %collective-permute-done.6.j1 = f32[96,128]{1,0:T(8,128)S(1)} collective-permute-done((f32[96,128]{1,0:T(8,128)S(1)}, f32[96,128]{1,0:T(8,128)S(1)}, u32[]{:S(2)}, u32[]{:S(2)}) %collective-permute-start.6) | collective-permute-done | bytes 49184 | tf_op jit(solution)/shard_map/ppermute | solution.py:506
  119.3 3.2 %gather.5 = (f32[96,128]{1,0:T(8,128)S(1)}, f32[552,128]{1,0:T(8,128)S(1)}, f32[32,2,8,128]{3,2,1,0:T(8,128)S(1)}) custom-call(s32[65]{0:T(128)S(1)} %get-tuple-element.55.meta.refs_0_, f32[96,128]{1,0:T(8,128)S(1)} %get-tuple-element.65.vel, f32[64,128]{1,0:T(8,128)S(1)} %get-tuple-element.42.prop, f32[96,128]{1,0:T(8,128)S(1)} %get-tuple-element.69.j0, ...), custom_call_target="tpu_custom_call" | custom-call | flops 10000000 | bytes 4000000 | tf_op jit(solution)/shard_map/gather/pallas_call | solution.py:510
  122.4 0.0 copy-start.2
  122.5 12.7 %all_to_all.28.refs_6_ = f32[32,2,8,128]{3,2,1,0:T(8,128)S(1)} all-to-all(f32[32,2,8,128]{3,2,1,0:T(8,128)S(1)} %get-tuple-element.73), channel_id=1, replica_groups=mesh['owner'=32,'sub'=4] {'owner'}, dimensions={0} | all-to-all | bytes 524288 | tf_op jit(solution)/shard_map/all_to_all | solution.py:486
  135.2 4.1 %apply.7 = (f32[96,128]{1,0:T(8,128)S(1)}, f32[552,128]{1,0:T(8,128)S(1)}) custom-call(s32[65]{0:T(128)S(1)} %get-tuple-element.55.meta.refs_0_, f32[69,7,8,128]{3,2,1,0:T(8,128)S(1)} %get-tuple-element.57.x.refs_1_, s32[552,128]{1,0:T(8,128)S(1)} %get-tuple-element.58.idx.refs_2_, f32[552,128]{1,0:T(8,128)S(1)} %get-tuple-element.71.refs_3_, ...), custom_call_target="tpu_custom_call" | custom-call | flops 10000000 | bytes 4000000 | tf_op jit(solution)/shard_map/apply/pallas_call | solution.py:498
  139.3 1.1 collective-permute-start.11
  140.4 0.4 collective-permute-start.10
  140.8 0.5 collective-permute-start.9
  141.3 0.0 copy-done.2
  141.3 2.4 %unpack.1 = f32[256,128]{1,0:T(8,128)} custom-call(s32[256]{0:T(256)S(1)} %copy-done.7, s32[65]{0:T(128)S(1)} %get-tuple-element.55.meta.refs_0_, f32[552,128]{1,0:T(8,128)S(1)} %get-tuple-element.75.imp, f32[256,128]{1,0:T(8,128)S(1)} %bitcast.6), custom_call_target="tpu_custom_call" | custom-call | flops 10000000 | bytes 4000000 | tf_op jit(solution)/shard_map/unpack/pallas_call | solution.py:517
  143.8 0.0 collective-permute-done.11.j3
  143.8 1.1 collective-permute-done.10.j2
  144.9 1.6 %collective-permute-done.9.j1 = f32[96,128]{1,0:T(8,128)S(1)} collective-permute-done((f32[96,128]{1,0:T(8,128)S(1)}, f32[96,128]{1,0:T(8,128)S(1)}, u32[]{:S(2)}, u32[]{:S(2)}) %collective-permute-start.9) | collective-permute-done | bytes 49184 | tf_op jit(solution)/shard_map/ppermute | solution.py:506
  146.5 0.7 final.1
Async XLA Ops:
  0.6 13.5 %copy-start.1 = (f32[9,32768]{1,0:T(8,128)S(1)}, f32[9,32768]{1,0:T(8,128)}, u32[]{:S(2)}) copy-start(f32[9,32768]{1,0:T(8,128)} %geom.3) | copy-start | bytes 3538948
  0.6 13.5 %copy-start.3 = (s32[32768]{0:T(1024)S(1)}, s32[32768]{0:T(1024)}, u32[]{:S(2)}) copy-start(s32[32768]{0:T(1024)} %param.10) | copy-start | bytes 393220
  0.7 13.5 %copy-start.4 = (f32[32768]{0:T(1024)S(1)}, f32[32768]{0:T(1024)}, u32[]{:S(2)}) copy-start(f32[32768]{0:T(1024)} %param.13) | copy-start | bytes 393220
  0.7 13.5 %copy-start.7 = (s32[256]{0:T(256)S(1)}, s32[256]{0:T(256)}, u32[]{:S(2)}) copy-start(s32[256]{0:T(256)} %live.7) | copy-start | bytes 3076
  4.4 26.9 %all-to-all-start = ((f32[32,64,128]{2,1,0:T(8,128)}), f32[32,64,128]{2,1,0:T(8,128)}, u32[]{:S(2)}, u32[]{:S(2)}) async-start(f32[32,64,128]{2,1,0:T(8,128)} %pack_sent.1.send), calls=%async_computation | async-start | bytes 2097152 | tf_op jit(solution)/shard_map/all_to_all | solution.py:459
  14.1 2.1 %copy-start = (f32[32,64,128]{2,1,0:T(8,128)S(1)}, f32[32,64,128]{2,1,0:T(8,128)}, u32[]{:S(2)}) copy-start(f32[32,64,128]{2,1,0:T(8,128)} %pack_sent.1.send) | copy-start | bytes 3145732
  14.1 2.1 %copy-start.5 = (f32[6,2048]{1,0:T(8,128)S(1)}, f32[6,2048]{1,0:T(8,128)}, u32[]{:S(2)}) copy-start(f32[6,2048]{1,0:T(8,128)} %velocity.1) | copy-start | bytes 147460
  14.1 2.1 %copy-start.6 = (f32[4,2048]{1,0:T(4,128)S(1)}, f32[4,2048]{1,0:T(4,128)}, u32[]{:S(2)}) copy-start(f32[4,2048]{1,0:T(4,128)} %properties.1) | copy-start | bytes 98308
  57.1 3.7 %collective-permute-start.2 = (f32[96,128]{1,0:T(8,128)S(1)}, f32[96,128]{1,0:T(8,128)S(1)}, u32[]{:S(2)}, u32[]{:S(2)}) collective-permute-start(f32[96,128]{1,0:T(8,128)S(1)} %get-tuple-element.56.j0), channel_id=1, source_target_pairs={{0,3},{1,0},{2,1},{3,2},{4,7},{5,4},{6,5},{7,6},{8,11},{9,8},{10,9... | collective-permute-start | bytes 147464 | tf_op jit(solution)/shard_map/ppermute | solution.py:506
  59.4 4.5 %collective-permute-start.1 = (f32[96,128]{1,0:T(8,128)S(1)}, f32[96,128]{1,0:T(8,128)S(1)}, u32[]{:S(2)}, u32[]{:S(2)}) collective-permute-start(f32[96,128]{1,0:T(8,128)S(1)} %get-tuple-element.56.j0), channel_id=1, source_target_pairs={{0,2},{1,3},{2,0},{3,1},{4,6},{5,7},{6,4},{7,5},{8,10},{9,11},{10,... | collective-permute-start | bytes 147464 | tf_op jit(solution)/shard_map/ppermute | solution.py:506
  60.0 4.9 %collective-permute-start = (f32[96,128]{1,0:T(8,128)S(1)}, f32[96,128]{1,0:T(8,128)S(1)}, u32[]{:S(2)}, u32[]{:S(2)}) collective-permute-start(f32[96,128]{1,0:T(8,128)S(1)} %get-tuple-element.56.j0), channel_id=1, source_target_pairs={{0,1},{1,2},{2,3},{3,0},{4,5},{5,6},{6,7},{7,4},{8,9},{9,10},{10,1... | collective-permute-start | bytes 147464 | tf_op jit(solution)/shard_map/ppermute | solution.py:506
  85.1 3.8 %collective-permute-start.5 = (f32[96,128]{1,0:T(8,128)S(1)}, f32[96,128]{1,0:T(8,128)S(1)}, u32[]{:S(2)}, u32[]{:S(2)}) collective-permute-start(f32[96,128]{1,0:T(8,128)S(1)} %get-tuple-element.64.j0), channel_id=1, source_target_pairs={{0,3},{1,0},{2,1},{3,2},{4,7},{5,4},{6,5},{7,6},{8,11},{9,8},{10,9... | collective-permute-start | bytes 147464 | tf_op jit(solution)/shard_map/ppermute | solution.py:506
  86.2 4.5 %collective-permute-start.4 = (f32[96,128]{1,0:T(8,128)S(1)}, f32[96,128]{1,0:T(8,128)S(1)}, u32[]{:S(2)}, u32[]{:S(2)}) collective-permute-start(f32[96,128]{1,0:T(8,128)S(1)} %get-tuple-element.64.j0), channel_id=1, source_target_pairs={{0,2},{1,3},{2,0},{3,1},{4,6},{5,7},{6,4},{7,5},{8,10},{9,11},{10,... | collective-permute-start | bytes 147464 | tf_op jit(solution)/shard_map/ppermute | solution.py:506
  86.8 5.5 %collective-permute-start.3 = (f32[96,128]{1,0:T(8,128)S(1)}, f32[96,128]{1,0:T(8,128)S(1)}, u32[]{:S(2)}, u32[]{:S(2)}) collective-permute-start(f32[96,128]{1,0:T(8,128)S(1)} %get-tuple-element.64.j0), channel_id=1, source_target_pairs={{0,1},{1,2},{2,3},{3,0},{4,5},{5,6},{6,7},{7,4},{8,9},{9,10},{10,1... | collective-permute-start | bytes 147464 | tf_op jit(solution)/shard_map/ppermute | solution.py:506
  112.1 3.8 %collective-permute-start.8 = (f32[96,128]{1,0:T(8,128)S(1)}, f32[96,128]{1,0:T(8,128)S(1)}, u32[]{:S(2)}, u32[]{:S(2)}) collective-permute-start(f32[96,128]{1,0:T(8,128)S(1)} %get-tuple-element.69.j0), channel_id=1, source_target_pairs={{0,3},{1,0},{2,1},{3,2},{4,7},{5,4},{6,5},{7,6},{8,11},{9,8},{10,9... | collective-permute-start | bytes 147464 | tf_op jit(solution)/shard_map/ppermute | solution.py:506
  113.2 4.5 %collective-permute-start.7 = (f32[96,128]{1,0:T(8,128)S(1)}, f32[96,128]{1,0:T(8,128)S(1)}, u32[]{:S(2)}, u32[]{:S(2)}) collective-permute-start(f32[96,128]{1,0:T(8,128)S(1)} %get-tuple-element.69.j0), channel_id=1, source_target_pairs={{0,2},{1,3},{2,0},{3,1},{4,6},{5,7},{6,4},{7,5},{8,10},{9,11},{10,... | collective-permute-start | bytes 147464 | tf_op jit(solution)/shard_map/ppermute | solution.py:506
  113.6 5.6 %collective-permute-start.6 = (f32[96,128]{1,0:T(8,128)S(1)}, f32[96,128]{1,0:T(8,128)S(1)}, u32[]{:S(2)}, u32[]{:S(2)}) collective-permute-start(f32[96,128]{1,0:T(8,128)S(1)} %get-tuple-element.69.j0), channel_id=1, source_target_pairs={{0,1},{1,2},{2,3},{3,0},{4,5},{5,6},{6,7},{7,4},{8,9},{9,10},{10,1... | collective-permute-start | bytes 147464 | tf_op jit(solution)/shard_map/ppermute | solution.py:506
  122.4 18.9 %copy-start.2 = (f32[32768]{0:T(1024)S(1)}, f32[32768]{0:T(1024)}, u32[]{:S(2)}) copy-start(f32[32768]{0:T(1024)} %param.14) | copy-start | bytes 393220
  139.3 4.5 %collective-permute-start.11 = (f32[96,128]{1,0:T(8,128)S(1)}, f32[96,128]{1,0:T(8,128)S(1)}, u32[]{:S(2)}, u32[]{:S(2)}) collective-permute-start(f32[96,128]{1,0:T(8,128)S(1)} %get-tuple-element.74.j0), channel_id=1, source_target_pairs={{0,3},{1,0},{2,1},{3,2},{4,7},{5,4},{6,5},{7,6},{8,11},{9,8},{10,9... | collective-permute-start | bytes 147464 | tf_op jit(solution)/shard_map/ppermute | solution.py:506
  140.4 4.5 %collective-permute-start.10 = (f32[96,128]{1,0:T(8,128)S(1)}, f32[96,128]{1,0:T(8,128)S(1)}, u32[]{:S(2)}, u32[]{:S(2)}) collective-permute-start(f32[96,128]{1,0:T(8,128)S(1)} %get-tuple-element.74.j0), channel_id=1, source_target_pairs={{0,2},{1,3},{2,0},{3,1},{4,6},{5,7},{6,4},{7,5},{8,10},{9,11},{10,... | collective-permute-start | bytes 147464 | tf_op jit(solution)/shard_map/ppermute | solution.py:506
  140.8 5.7 %collective-permute-start.9 = (f32[96,128]{1,0:T(8,128)S(1)}, f32[96,128]{1,0:T(8,128)S(1)}, u32[]{:S(2)}, u32[]{:S(2)}) collective-permute-start(f32[96,128]{1,0:T(8,128)S(1)} %get-tuple-element.74.j0), channel_id=1, source_target_pairs={{0,1},{1,2},{2,3},{3,0},{4,5},{5,6},{6,7},{7,4},{8,9},{9,10},{10,1... | collective-permute-start | bytes 147464 | tf_op jit(solution)/shard_map/ppermute | solution.py:506

commit v6 on v5

--- a/solution.py
+++ b/solution.py
@@ -348,15 +348,15 @@
     j_out[...] = total[0:96] + total[96:192]
 
 
-def moved(vel, prop, j0, j1, j2, j3, c):
+def moved(vel, prop, j0, j1, j3, j2, c):
     rows = slice(c * HIGH, (c + 1) * HIGH)
     k = max(c - 2, 0)
-    gain = (j0[rows, :] + j2[rows, :]) + (j1[rows, :] + j3[rows, :])
+    gain = (j0[rows, :] + j1[rows, :]) + (j2[rows, :] + j3[rows, :])
     return vel[rows, :] + prop[k * HIGH : (k + 1) * HIGH, :] * gain
 
 
-def gather_kernel(meta, vel, prop, j0, j1, j2, j3, x, idx, vel_out, u_out, share, words):
-    rows = [moved(vel, prop, j0, j1, j2, j3, c) for c in range(6)]
+def gather_kernel(meta, vel, prop, j0, j1, j3, j2, x, idx, vel_out, u_out, share, words):
+    rows = [moved(vel, prop, j0, j1, j3, j2, c) for c in range(6)]
     for c in range(6):
         vel_out[c * HIGH : (c + 1) * HIGH, :] = rows[c]
     unit = fixed_words(rows, words)
@@ -375,9 +375,9 @@
     lax.fori_loop(0, PEERS, one_share, 0, unroll=8)
 
 
-def final_kernel(vel, prop, j0, j1, j2, j3, out):
+def final_kernel(vel, prop, j0, j1, j3, j2, out):
     for c in range(6):
-        rows = moved(vel, prop, j0, j1, j2, j3, c)
+        rows = moved(vel, prop, j0, j1, j3, j2, c)
         for h in range(HIGH):
             out[c : c + 1, h * LANES : (h + 1) * LANES] = rows[h : h + 1]
 
@@ -503,8 +503,7 @@
                 name="apply",
             )(meta, x, idx, imp, u, weight, told)
         gains = [own] + [
-            lax.ppermute(own, "sub", [(i, (i + d) % n_sub) for i in range(n_sub)])
-            for d in (1, 2, 3)
+            lax.ppermute(own, "sub", [(i, i ^ d) for i in range(n_sub)]) for d in (1, 3, 2)
         ]
         if iteration < ITERS - 1:
             vel, u, share = call(

time: 148 us -> 146 us (0.986)
  waiting for transfers between devices: 27.1 us -> 20.8 us
  blocking collectives: 53.1 us -> 57 us
  starting transfers between devices: 20 us -> 21.5 us
    ppermute x12, waiting for transfers between devices: 16.7 us -> 9.93 us  [on_device(): lax.ppermute(own, 'sub', [(i, i ^ d) for i in range(n_sub)])]
    all_to_all x4, blocking collectives: 53.1 us -> 57 us  [on_device(): lax.all_to_all(share, 'owner', split_axis=0, concat_axis=0, tiled=True)]
    ppermute x12, starting transfers between devices: 10.3 us -> 11.9 us  [on_device(): lax.ppermute(own, 'sub', [(i, i ^ d) for i in range(n_sub)])]
  transfers between devices with their start and end apart: 13 -> 13, of which waited for: 11 -> 9; matrix products, arithmetic and copies ran while one was open for 0% -> 0% of each run, Pallas kernels for 6% -> 6%
where the time goes in v6:
time: 146 us
  blocking collectives  57 us (39%)
  Pallas kernels  45.5 us (31%)
  starting transfers between devices  21.5 us (15%)
  waiting for transfers between devices  20.8 us (14%)
    all_to_all x4, blocking collectives, on_device(): lax.all_to_all(share, 'owner', split_axis=0, concat_axis=0, tiled=True)  57 us
    pallas_call x3, Pallas kernels, on_device(): call(functools.partial(apply_kernel, False), [SMEM] + [VMEM] * 6, [shape(...  12.3 us
    ppermute x12, starting transfers between devices, on_device(): lax.ppermute(own, 'sub', [(i, i ^ d) for i in range(n_sub)])  11.9 us
    all_to_all x1, waiting for transfers between devices, on_device(): lax.all_to_all(send, 'owner', split_axis=0, concat_axis=0, tiled=True)  10.9 us
    ppermute x12, waiting for transfers between devices, on_device(): lax.ppermute(own, 'sub', [(i, i ^ d) for i in range(n_sub)])  9.93 us
    all_to_all x1, starting transfers between devices, on_device(): lax.all_to_all(send, 'owner', split_axis=0, concat_axis=0, tiled=True)  9.65 us
    pallas_call x3, Pallas kernels, on_device(): call(gather_kernel, [SMEM] + [VMEM] * 8, [shape(96, LANES), stream, shape...  9.47 us
    pallas_call x2, Pallas kernels, pack(): pl.pallas_call(functools.partial(pack_kernel, sent), grid=(PEERS // PART,...  5.78 us
  transfers between devices with their start and end apart: 13, of which 9 were waited for; matrix products, arithmetic and copies ran while one was open for 0% of the time, Pallas kernels for 6%

profile of v6, /device:TPU:1, one launch (start us, length us, event | category | flops | bytes accessed | tf_op | source)
XLA Modules:
  0.0 145.7 jit_solution(7311976743637442599)
XLA Ops:
  0.6 0.0 copy-start.1
  0.6 0.0 copy-start.3
  0.7 0.0 copy-start.4
  0.7 0.0 copy-start.7
  0.7 3.8 %pack_sent.1.send = f32[32,64,128]{2,1,0:T(8,128)} custom-call(s32[256]{0:T(256)} %live.7, f32[9,32768]{1,0:T(8,128)} %geom.3, s32[256,128]{1,0:T(8,128)} %bitcast.9, f32[256,128]{1,0:T(8,128)} %bitcast.5), custom_call_target="tpu_custom_call" | custom-call | flops 10000000 | bytes 4000000 | tf_op jit(solution)/shard_map/pack_sent/pallas_call | solution.py:427
  4.4 9.7 %all-to-all-start = ((f32[32,64,128]{2,1,0:T(8,128)}), f32[32,64,128]{2,1,0:T(8,128)}, u32[]{:S(2)}, u32[]{:S(2)}) async-start(f32[32,64,128]{2,1,0:T(8,128)} %pack_sent.1.send), calls=%async_computation | async-start | bytes 2097152 | tf_op jit(solution)/shard_map/all_to_all | solution.py:459
  14.1 0.0 copy-start
  14.1 0.0 copy-start.5
  14.1 0.0 copy-start.6
  14.1 0.0 copy-done.1
  14.1 0.0 copy-done.3
  14.2 0.0 copy-done.4
  14.2 0.0 copy-done.7
  14.2 2.0 %pack_local.1.local = f32[32,64,128]{2,1,0:T(8,128)S(1)} custom-call(s32[256]{0:T(256)S(1)} %copy-done.7, f32[9,32768]{1,0:T(8,128)S(1)} %copy-done.1, s32[256,128]{1,0:T(8,128)S(1)} %bitcast.7, f32[256,128]{1,0:T(8,128)S(1)} %bitcast.8), custom_call_target="tpu_custom_call" | custom-call | flops 10000000 | bytes 4000000 | tf_op jit(solution)/shard_map/pack_local/pallas_call | solution.py:427
  16.2 0.0 copy-done
  16.2 0.0 copy-done.5
  16.2 0.0 copy-done.6
  16.2 4.2 %first.1 = (f32[32,7,8,128]{3,2,1,0:T(8,128)S(1)}, s32[272,128]{1,0:T(8,128)S(1)}, f32[272,128]{1,0:T(8,128)S(1)}, f32[272,128]{1,0:T(8,128)S(1)}, f32[272,128]{...) custom-call(s32[256]{0:T(256)S(1)} %copy-done.7, ...), custom_call_target="tpu_custom_call" | custom-call | flops 10000000 | bytes 4000000 | tf_op jit(solution)/shard_map/first/pallas_call | solution.py:460
  20.4 10.9 %all-to-all-done.arrived = f32[32,64,128]{2,1,0:T(8,128)} async-done(((f32[32,64,128]{2,1,0:T(8,128)}), f32[32,64,128]{2,1,0:T(8,128)}, u32[]{:S(2)}, u32[]{:S(2)}) %all-to-all-start) | async-done | bytes 1048608 | tf_op jit(solution)/shard_map/all_to_all | solution.py:459
  31.3 5.6 %second.1 = (f32[32,6,8,128]{3,2,1,0:T(8,128)S(1)}, s32[272,128]{1,0:T(8,128)S(1)}, f32[272,128]{1,0:T(8,128)S(1)}, f32[272,128]{1,0:T(8,128)S(1)}, f32[272,128]...) custom-call(f32[32,64,128]{2,1,0:T(8,128)} %all-to-all-done.arrived, ...), custom_call_target="tpu_custom_call" | custom-call | flops 10000000 | bytes 4000000 | tf_op jit(solution)/shard_map/second/pallas_call | solution.py:471
  37.0 15.1 %all_to_all.25.refs_12_ = f32[32,4,8,128]{3,2,1,0:T(8,128)S(1)} all-to-all(f32[32,4,8,128]{3,2,1,0:T(8,128)S(1)} %get-tuple-element.54), channel_id=1, replica_groups=mesh['owner'=32,'sub'=4] {'owner'}, dimensions={0} | all-to-all | bytes 1048576 | tf_op jit(solution)/shard_map/all_to_all | solution.py:486
  52.0 5.0 %apply.4 = (f32[96,128]{1,0:T(8,128)S(1)}, f32[552,128]{1,0:T(8,128)S(1)}, f32[552,128]{1,0:T(8,128)S(1)}, f32[69,7,8,128]{3,2,1,0:T(8,128)S(1)}, s32[552,128]{1,0:T(8,128)S(1)}, /*index=5*/s32[65]{0:T(128)S(1)}) custom-call(s32[33]{0:T(128)S(1)} %get-tuple-element.39.refs_0_, s32[33]{0:T(128)S(1)} %get-tuple-element.43.refs_1_, ...), custom_call_target="tpu_custom_call" | custom-call | flops 10000000 | bytes 4000000 | tf_op jit(solution)/shard_map/apply/pallas_call | solution.py:488
  57.1 2.3 %collective-permute-start.2 = (f32[96,128]{1,0:T(8,128)S(1)}, f32[96,128]{1,0:T(8,128)S(1)}, u32[]{:S(2)}, u32[]{:S(2)}) collective-permute-start(f32[96,128]{1,0:T(8,128)S(1)} %get-tuple-element.56.j0), channel_id=1, source_target_pairs={{0,2},{1,3},{2,0},{3,1},{4,6},{5,7},{6,4},{7,5},{8,10},{9,11},{10,... | collective-permute-start | bytes 147464 | tf_op jit(solution)/shard_map/ppermute | solution.py:506
  59.4 1.4 collective-permute-start.1
  60.8 0.0 collective-permute-start
  60.8 0.8 collective-permute-done.2.j2
  61.6 2.0 %collective-permute-done.1.j3 = f32[96,128]{1,0:T(8,128)S(1)} collective-permute-done((f32[96,128]{1,0:T(8,128)S(1)}, f32[96,128]{1,0:T(8,128)S(1)}, u32[]{:S(2)}, u32[]{:S(2)}) %collective-permute-start.1) | collective-permute-done | bytes 49184 | tf_op jit(solution)/shard_map/ppermute | solution.py:506
  63.6 0.2 collective-permute-done.j1
  63.7 3.2 %gather.3 = (f32[96,128]{1,0:T(8,128)S(1)}, f32[552,128]{1,0:T(8,128)S(1)}, f32[32,2,8,128]{3,2,1,0:T(8,128)S(1)}) custom-call(s32[65]{0:T(128)S(1)} %get-tuple-element.55.meta.refs_0_, f32[96,128]{1,0:T(8,128)S(1)} %get-tuple-element.41.vel, f32[64,128]{1,0:T(8,128)S(1)} %get-tuple-element.42.prop, f32[96,128]{1,0:T(8,128)S(1)} %get-tuple-element.56.j0, ...), custom_call_target="tpu_custom_call" | custom-call | flops 10000000 | bytes 4000000 | tf_op jit(solution)/shard_map/gather/pallas_call | solution.py:509
  66.9 14.1 %all_to_all.26.refs_6_ = f32[32,2,8,128]{3,2,1,0:T(8,128)S(1)} all-to-all(f32[32,2,8,128]{3,2,1,0:T(8,128)S(1)} %get-tuple-element.63), channel_id=1, replica_groups=mesh['owner'=32,'sub'=4] {'owner'}, dimensions={0} | all-to-all | bytes 524288 | tf_op jit(solution)/shard_map/all_to_all | solution.py:486
  81.0 4.1 %apply.5 = (f32[96,128]{1,0:T(8,128)S(1)}, f32[552,128]{1,0:T(8,128)S(1)}) custom-call(s32[65]{0:T(128)S(1)} %get-tuple-element.55.meta.refs_0_, f32[69,7,8,128]{3,2,1,0:T(8,128)S(1)} %get-tuple-element.57.x.refs_1_, s32[552,128]{1,0:T(8,128)S(1)} %get-tuple-element.58.idx.refs_2_, f32[552,128]{1,0:T(8,128)S(1)} %get-tuple-element.60.refs_3_, ...), custom_call_target="tpu_custom_call" | custom-call | flops 10000000 | bytes 4000000 | tf_op jit(solution)/shard_map/apply/pallas_call | solution.py:498
  85.1 1.3 collective-permute-start.5
  86.3 0.6 collective-permute-start.4
  86.9 0.9 collective-permute-start.3
  87.8 1.8 %collective-permute-done.5.j2 = f32[96,128]{1,0:T(8,128)S(1)} collective-permute-done((f32[96,128]{1,0:T(8,128)S(1)}, f32[96,128]{1,0:T(8,128)S(1)}, u32[]{:S(2)}, u32[]{:S(2)}) %collective-permute-start.5) | collective-permute-done | bytes 49184 | tf_op jit(solution)/shard_map/ppermute | solution.py:506
  89.6 1.2 collective-permute-done.4.j3
  90.8 0.0 collective-permute-done.3.j1
  90.8 3.2 %gather.4 = (f32[96,128]{1,0:T(8,128)S(1)}, f32[552,128]{1,0:T(8,128)S(1)}, f32[32,2,8,128]{3,2,1,0:T(8,128)S(1)}) custom-call(s32[65]{0:T(128)S(1)} %get-tuple-element.55.meta.refs_0_, f32[96,128]{1,0:T(8,128)S(1)} %get-tuple-element.59.vel, f32[64,128]{1,0:T(8,128)S(1)} %get-tuple-element.42.prop, f32[96,128]{1,0:T(8,128)S(1)} %get-tuple-element.64.j0, ...), custom_call_target="tpu_custom_call" | custom-call | flops 10000000 | bytes 4000000 | tf_op jit(solution)/shard_map/gather/pallas_call | solution.py:509
  94.0 13.8 %all_to_all.27.refs_6_ = f32[32,2,8,128]{3,2,1,0:T(8,128)S(1)} all-to-all(f32[32,2,8,128]{3,2,1,0:T(8,128)S(1)} %get-tuple-element.68), channel_id=1, replica_groups=mesh['owner'=32,'sub'=4] {'owner'}, dimensions={0} | all-to-all | bytes 524288 | tf_op jit(solution)/shard_map/all_to_all | solution.py:486
  107.8 4.1 %apply.6 = (f32[96,128]{1,0:T(8,128)S(1)}, f32[552,128]{1,0:T(8,128)S(1)}) custom-call(s32[65]{0:T(128)S(1)} %get-tuple-element.55.meta.refs_0_, f32[69,7,8,128]{3,2,1,0:T(8,128)S(1)} %get-tuple-element.57.x.refs_1_, s32[552,128]{1,0:T(8,128)S(1)} %get-tuple-element.58.idx.refs_2_, f32[552,128]{1,0:T(8,128)S(1)} %get-tuple-element.66.refs_3_, ...), custom_call_target="tpu_custom_call" | custom-call | flops 10000000 | bytes 4000000 | tf_op jit(solution)/shard_map/apply/pallas_call | solution.py:498
  111.9 1.2 collective-permute-start.8
  113.1 1.5 %collective-permute-start.7 = (f32[96,128]{1,0:T(8,128)S(1)}, f32[96,128]{1,0:T(8,128)S(1)}, u32[]{:S(2)}, u32[]{:S(2)}) collective-permute-start(f32[96,128]{1,0:T(8,128)S(1)} %get-tuple-element.69.j0), channel_id=1, source_target_pairs={{0,3},{1,2},{2,1},{3,0},{4,7},{5,6},{6,5},{7,4},{8,11},{9,10},{10,... | collective-permute-start | bytes 147464 | tf_op jit(solution)/shard_map/ppermute | solution.py:506
  114.5 0.1 collective-permute-start.6
  114.6 1.8 %collective-permute-done.8.j2 = f32[96,128]{1,0:T(8,128)S(1)} collective-permute-done((f32[96,128]{1,0:T(8,128)S(1)}, f32[96,128]{1,0:T(8,128)S(1)}, u32[]{:S(2)}, u32[]{:S(2)}) %collective-permute-start.8) | collective-permute-done | bytes 49184 | tf_op jit(solution)/shard_map/ppermute | solution.py:506
  116.4 1.2 collective-permute-done.7.j3
  117.6 0.0 collective-permute-done.6.j1
  117.6 3.2 %gather.5 = (f32[96,128]{1,0:T(8,128)S(1)}, f32[552,128]{1,0:T(8,128)S(1)}, f32[32,2,8,128]{3,2,1,0:T(8,128)S(1)}) custom-call(s32[65]{0:T(128)S(1)} %get-tuple-element.55.meta.refs_0_, f32[96,128]{1,0:T(8,128)S(1)} %get-tuple-element.65.vel, f32[64,128]{1,0:T(8,128)S(1)} %get-tuple-element.42.prop, f32[96,128]{1,0:T(8,128)S(1)} %get-tuple-element.69.j0, ...), custom_call_target="tpu_custom_call" | custom-call | flops 10000000 | bytes 4000000 | tf_op jit(solution)/shard_map/gather/pallas_call | solution.py:509
  120.8 0.0 copy-start.2
  120.8 14.0 %all_to_all.28.refs_6_ = f32[32,2,8,128]{3,2,1,0:T(8,128)S(1)} all-to-all(f32[32,2,8,128]{3,2,1,0:T(8,128)S(1)} %get-tuple-element.73), channel_id=1, replica_groups=mesh['owner'=32,'sub'=4] {'owner'}, dimensions={0} | all-to-all | bytes 524288 | tf_op jit(solution)/shard_map/all_to_all | solution.py:486
  134.8 4.1 %apply.7 = (f32[96,128]{1,0:T(8,128)S(1)}, f32[552,128]{1,0:T(8,128)S(1)}) custom-call(s32[65]{0:T(128)S(1)} %get-tuple-element.55.meta.refs_0_, f32[69,7,8,128]{3,2,1,0:T(8,128)S(1)} %get-tuple-element.57.x.refs_1_, s32[552,128]{1,0:T(8,128)S(1)} %get-tuple-element.58.idx.refs_2_, f32[552,128]{1,0:T(8,128)S(1)} %get-tuple-element.71.refs_3_, ...), custom_call_target="tpu_custom_call" | custom-call | flops 10000000 | bytes 4000000 | tf_op jit(solution)/shard_map/apply/pallas_call | solution.py:498
  138.9 1.0 collective-permute-start.11
  140.0 1.5 %collective-permute-start.10 = (f32[96,128]{1,0:T(8,128)S(1)}, f32[96,128]{1,0:T(8,128)S(1)}, u32[]{:S(2)}, u32[]{:S(2)}) collective-permute-start(f32[96,128]{1,0:T(8,128)S(1)} %get-tuple-element.74.j0), channel_id=1, source_target_pairs={{0,3},{1,2},{2,1},{3,0},{4,7},{5,6},{6,5},{7,4},{8,11},{9,10},{10,... | collective-permute-start | bytes 147464 | tf_op jit(solution)/shard_map/ppermute | solution.py:506
  141.5 0.2 collective-permute-start.9
  141.7 0.0 copy-done.2
  141.7 2.4 %unpack.1 = f32[256,128]{1,0:T(8,128)} custom-call(s32[256]{0:T(256)S(1)} %copy-done.7, s32[65]{0:T(128)S(1)} %get-tuple-element.55.meta.refs_0_, f32[552,128]{1,0:T(8,128)S(1)} %get-tuple-element.75.imp, f32[256,128]{1,0:T(8,128)S(1)} %bitcast.6), custom_call_target="tpu_custom_call" | custom-call | flops 10000000 | bytes 4000000 | tf_op jit(solution)/shard_map/unpack/pallas_call | solution.py:516
  144.1 0.0 collective-permute-done.11.j2
  144.1 1.0 collective-permute-done.10.j3
  145.0 0.0 collective-permute-done.9.j1
  145.1 0.7 final.1
Async XLA Ops:
  0.6 13.5 %copy-start.1 = (f32[9,32768]{1,0:T(8,128)S(1)}, f32[9,32768]{1,0:T(8,128)}, u32[]{:S(2)}) copy-start(f32[9,32768]{1,0:T(8,128)} %geom.3) | copy-start | bytes 3538948
  0.6 13.5 %copy-start.3 = (s32[32768]{0:T(1024)S(1)}, s32[32768]{0:T(1024)}, u32[]{:S(2)}) copy-start(s32[32768]{0:T(1024)} %param.10) | copy-start | bytes 393220
  0.7 13.5 %copy-start.4 = (f32[32768]{0:T(1024)S(1)}, f32[32768]{0:T(1024)}, u32[]{:S(2)}) copy-start(f32[32768]{0:T(1024)} %param.13) | copy-start | bytes 393220
  0.7 13.5 %copy-start.7 = (s32[256]{0:T(256)S(1)}, s32[256]{0:T(256)}, u32[]{:S(2)}) copy-start(s32[256]{0:T(256)} %live.7) | copy-start | bytes 3076
  4.4 26.9 %all-to-all-start = ((f32[32,64,128]{2,1,0:T(8,128)}), f32[32,64,128]{2,1,0:T(8,128)}, u32[]{:S(2)}, u32[]{:S(2)}) async-start(f32[32,64,128]{2,1,0:T(8,128)} %pack_sent.1.send), calls=%async_computation | async-start | bytes 2097152 | tf_op jit(solution)/shard_map/all_to_all | solution.py:459
  14.1 2.1 %copy-start = (f32[32,64,128]{2,1,0:T(8,128)S(1)}, f32[32,64,128]{2,1,0:T(8,128)}, u32[]{:S(2)}) copy-start(f32[32,64,128]{2,1,0:T(8,128)} %pack_sent.1.send) | copy-start | bytes 3145732
  14.1 2.1 %copy-start.5 = (f32[6,2048]{1,0:T(8,128)S(1)}, f32[6,2048]{1,0:T(8,128)}, u32[]{:S(2)}) copy-start(f32[6,2048]{1,0:T(8,128)} %velocity.1) | copy-start | bytes 147460
  14.1 2.1 %copy-start.6 = (f32[4,2048]{1,0:T(4,128)S(1)}, f32[4,2048]{1,0:T(4,128)}, u32[]{:S(2)}) copy-start(f32[4,2048]{1,0:T(4,128)} %properties.1) | copy-start | bytes 98308
  57.1 4.5 %collective-permute-start.2 = (f32[96,128]{1,0:T(8,128)S(1)}, f32[96,128]{1,0:T(8,128)S(1)}, u32[]{:S(2)}, u32[]{:S(2)}) collective-permute-start(f32[96,128]{1,0:T(8,128)S(1)} %get-tuple-element.56.j0), channel_id=1, source_target_pairs={{0,2},{1,3},{2,0},{3,1},{4,6},{5,7},{6,4},{7,5},{8,10},{9,11},{10,... | collective-permute-start | bytes 147464 | tf_op jit(solution)/shard_map/ppermute | solution.py:506
  59.4 4.2 %collective-permute-start.1 = (f32[96,128]{1,0:T(8,128)S(1)}, f32[96,128]{1,0:T(8,128)S(1)}, u32[]{:S(2)}, u32[]{:S(2)}) collective-permute-start(f32[96,128]{1,0:T(8,128)S(1)} %get-tuple-element.56.j0), channel_id=1, source_target_pairs={{0,3},{1,2},{2,1},{3,0},{4,7},{5,6},{6,5},{7,4},{8,11},{9,10},{10,... | collective-permute-start | bytes 147464 | tf_op jit(solution)/shard_map/ppermute | solution.py:506
  60.8 2.9 %collective-permute-start = (f32[96,128]{1,0:T(8,128)S(1)}, f32[96,128]{1,0:T(8,128)S(1)}, u32[]{:S(2)}, u32[]{:S(2)}) collective-permute-start(f32[96,128]{1,0:T(8,128)S(1)} %get-tuple-element.56.j0), channel_id=1, source_target_pairs={{0,1},{1,0},{2,3},{3,2},{4,5},{5,4},{6,7},{7,6},{8,9},{9,8},{10,11... | collective-permute-start | bytes 147464 | tf_op jit(solution)/shard_map/ppermute | solution.py:506
  85.1 4.5 %collective-permute-start.5 = (f32[96,128]{1,0:T(8,128)S(1)}, f32[96,128]{1,0:T(8,128)S(1)}, u32[]{:S(2)}, u32[]{:S(2)}) collective-permute-start(f32[96,128]{1,0:T(8,128)S(1)} %get-tuple-element.64.j0), channel_id=1, source_target_pairs={{0,2},{1,3},{2,0},{3,1},{4,6},{5,7},{6,4},{7,5},{8,10},{9,11},{10,... | collective-permute-start | bytes 147464 | tf_op jit(solution)/shard_map/ppermute | solution.py:506
  86.3 4.5 %collective-permute-start.4 = (f32[96,128]{1,0:T(8,128)S(1)}, f32[96,128]{1,0:T(8,128)S(1)}, u32[]{:S(2)}, u32[]{:S(2)}) collective-permute-start(f32[96,128]{1,0:T(8,128)S(1)} %get-tuple-element.64.j0), channel_id=1, source_target_pairs={{0,3},{1,2},{2,1},{3,0},{4,7},{5,6},{6,5},{7,4},{8,11},{9,10},{10,... | collective-permute-start | bytes 147464 | tf_op jit(solution)/shard_map/ppermute | solution.py:506
  86.9 3.9 %collective-permute-start.3 = (f32[96,128]{1,0:T(8,128)S(1)}, f32[96,128]{1,0:T(8,128)S(1)}, u32[]{:S(2)}, u32[]{:S(2)}) collective-permute-start(f32[96,128]{1,0:T(8,128)S(1)} %get-tuple-element.64.j0), channel_id=1, source_target_pairs={{0,1},{1,0},{2,3},{3,2},{4,5},{5,4},{6,7},{7,6},{8,9},{9,8},{10,11... | collective-permute-start | bytes 147464 | tf_op jit(solution)/shard_map/ppermute | solution.py:506
  111.9 4.5 %collective-permute-start.8 = (f32[96,128]{1,0:T(8,128)S(1)}, f32[96,128]{1,0:T(8,128)S(1)}, u32[]{:S(2)}, u32[]{:S(2)}) collective-permute-start(f32[96,128]{1,0:T(8,128)S(1)} %get-tuple-element.69.j0), channel_id=1, source_target_pairs={{0,2},{1,3},{2,0},{3,1},{4,6},{5,7},{6,4},{7,5},{8,10},{9,11},{10,... | collective-permute-start | bytes 147464 | tf_op jit(solution)/shard_map/ppermute | solution.py:506
  113.1 4.6 %collective-permute-start.7 = (f32[96,128]{1,0:T(8,128)S(1)}, f32[96,128]{1,0:T(8,128)S(1)}, u32[]{:S(2)}, u32[]{:S(2)}) collective-permute-start(f32[96,128]{1,0:T(8,128)S(1)} %get-tuple-element.69.j0), channel_id=1, source_target_pairs={{0,3},{1,2},{2,1},{3,0},{4,7},{5,6},{6,5},{7,4},{8,11},{9,10},{10,... | collective-permute-start | bytes 147464 | tf_op jit(solution)/shard_map/ppermute | solution.py:506
  114.5 3.1 %collective-permute-start.6 = (f32[96,128]{1,0:T(8,128)S(1)}, f32[96,128]{1,0:T(8,128)S(1)}, u32[]{:S(2)}, u32[]{:S(2)}) collective-permute-start(f32[96,128]{1,0:T(8,128)S(1)} %get-tuple-element.69.j0), channel_id=1, source_target_pairs={{0,1},{1,0},{2,3},{3,2},{4,5},{5,4},{6,7},{7,6},{8,9},{9,8},{10,11... | collective-permute-start | bytes 147464 | tf_op jit(solution)/shard_map/ppermute | solution.py:506
  120.8 20.9 %copy-start.2 = (f32[32768]{0:T(1024)S(1)}, f32[32768]{0:T(1024)}, u32[]{:S(2)}) copy-start(f32[32768]{0:T(1024)} %param.14) | copy-start | bytes 393220
  138.9 5.1 %collective-permute-start.11 = (f32[96,128]{1,0:T(8,128)S(1)}, f32[96,128]{1,0:T(8,128)S(1)}, u32[]{:S(2)}, u32[]{:S(2)}) collective-permute-start(f32[96,128]{1,0:T(8,128)S(1)} %get-tuple-element.74.j0), channel_id=1, source_target_pairs={{0,2},{1,3},{2,0},{3,1},{4,6},{5,7},{6,4},{7,5},{8,10},{9,11},{10,... | collective-permute-start | bytes 147464 | tf_op jit(solution)/shard_map/ppermute | solution.py:506
  140.0 5.1 %collective-permute-start.10 = (f32[96,128]{1,0:T(8,128)S(1)}, f32[96,128]{1,0:T(8,128)S(1)}, u32[]{:S(2)}, u32[]{:S(2)}) collective-permute-start(f32[96,128]{1,0:T(8,128)S(1)} %get-tuple-element.74.j0), channel_id=1, source_target_pairs={{0,3},{1,2},{2,1},{3,0},{4,7},{5,6},{6,5},{7,4},{8,11},{9,10},{10,... | collective-permute-start | bytes 147464 | tf_op jit(solution)/shard_map/ppermute | solution.py:506
  141.5 3.6 %collective-permute-start.9 = (f32[96,128]{1,0:T(8,128)S(1)}, f32[96,128]{1,0:T(8,128)S(1)}, u32[]{:S(2)}, u32[]{:S(2)}) collective-permute-start(f32[96,128]{1,0:T(8,128)S(1)} %get-tuple-element.74.j0), channel_id=1, source_target_pairs={{0,1},{1,0},{2,3},{3,2},{4,5},{5,4},{6,7},{7,6},{8,9},{9,8},{10,11... | collective-permute-start | bytes 147464 | tf_op jit(solution)/shard_map/ppermute | solution.py:506

commit v7 on v6

--- a/solution.py
+++ b/solution.py
@@ -123,8 +123,7 @@
         u_out[rows[k], :] = u - x[g, 6] if offset else u
 
 
-def prepare(first, total, d0, d1, vel, prop, words, x_out, idx_out, imp_out, u_out, m_out):
-    unit = fixed_words([vel[c * HIGH : (c + 1) * HIGH, :] for c in range(6)], words)
+def prepare(first, total, unit, d0, d1, prop, words, x_out, idx_out, imp_out, u_out, m_out):
 
     def load(g):
         base = g * 64
@@ -191,7 +190,8 @@
 
     total = lax.fori_loop(0, PEERS, one_partner, jnp.int32(0), unroll=4)
     meta[PEERS] = total
-    prepare(True, total, d0, d1, vel, prop, words, x_out, idx_out, imp_out, u_out, m_out)
+    unit = fixed_words([vel[c * HIGH : (c + 1) * HIGH, :] for c in range(6)], words)
+    prepare(True, total, unit, d0, d1, prop, words, x_out, idx_out, imp_out, u_out, m_out)
 
     def one_share(q, _):
         rows = pl.ds(meta[q], 8)
@@ -212,6 +212,7 @@
         part = pl.ds(k * piece, piece)
         pieces.append(pltpu.make_async_copy(arrived.at[part], received.at[part], sems.at[k]))
         pieces[k].start()
+    unit = fixed_words([vel[c * HIGH : (c + 1) * HIGH, :] for c in range(6)], words)
     copy = pltpu.make_async_copy(share_first, share.at[:, 0:2], sem)
     copy.start()
 
@@ -231,7 +232,7 @@
 
     total = lax.fori_loop(0, PEERS, one_partner, jnp.int32(0), unroll=4)
     meta[PEERS] = total
-    prepare(False, total, d0, None, vel, prop, words, x_out, idx_out, imp_out, u_out, m_out)
+    prepare(False, total, unit, d0, None, prop, words, x_out, idx_out, imp_out, u_out, m_out)
 
     def one_share(q, _):
         rows = pl.ds(meta[q], 8)

time: 146 us -> 146 us (level)
  no operation moved by 1% of the time
where the time goes in v7:
time: 146 us; the launch traced here: 145 us
  blocking collectives  57.4 us (39%)
  Pallas kernels  45.4 us (31%)
  starting transfers between devices  21.5 us (15%)
  waiting for transfers between devices  20.1 us (14%)
    all_to_all x4, blocking collectives, on_device(): lax.all_to_all(share, 'owner', split_axis=0, concat_axis=0, tiled=True)  57.4 us
    pallas_call x3, Pallas kernels, on_device(): call(functools.partial(apply_kernel, False), [SMEM] + [VMEM] * 6, [shape(...  12.3 us
    ppermute x12, starting transfers between devices, on_device(): lax.ppermute(own, 'sub', [(i, i ^ d) for i in range(n_sub)])  11.8 us
    all_to_all x1, waiting for transfers between devices, on_device(): lax.all_to_all(send, 'owner', split_axis=0, concat_axis=0, tiled=True)  10.4 us
    ppermute x12, waiting for transfers between devices, on_device(): lax.ppermute(own, 'sub', [(i, i ^ d) for i in range(n_sub)])  9.69 us
    all_to_all x1, starting transfers between devices, on_device(): lax.all_to_all(send, 'owner', split_axis=0, concat_axis=0, tiled=True)  9.65 us
    pallas_call x3, Pallas kernels, on_device(): call(gather_kernel, [SMEM] + [VMEM] * 8, [shape(96, LANES), stream, shape...  9.47 us
    pallas_call x2, Pallas kernels, pack(): pl.pallas_call(functools.partial(pack_kernel, sent), grid=(PEERS // PART,...  5.78 us
  transfers between devices with their start and end apart: 13, of which 9 were waited for; matrix products, arithmetic and copies ran while one was open for 0% of the time, Pallas kernels for 6%

profile of v7, /device:TPU:1, one launch (start us, length us, event | category | flops | bytes accessed | tf_op | source)
XLA Modules:
  0.0 145.2 jit_solution(10687908128124875316)
XLA Ops:
  0.6 0.0 copy-start.1
  0.6 0.0 copy-start.3
  0.7 0.0 copy-start.4
  0.7 0.0 copy-start.7
  0.7 3.8 %pack_sent.1.send = f32[32,64,128]{2,1,0:T(8,128)} custom-call(s32[256]{0:T(256)} %live.7, f32[9,32768]{1,0:T(8,128)} %geom.3, s32[256,128]{1,0:T(8,128)} %bitcast.9, f32[256,128]{1,0:T(8,128)} %bitcast.5), custom_call_target="tpu_custom_call" | custom-call | flops 10000000 | bytes 4000000 | tf_op jit(solution)/shard_map/pack_sent/pallas_call | solution.py:428
  4.4 9.7 %all-to-all-start = ((f32[32,64,128]{2,1,0:T(8,128)}), f32[32,64,128]{2,1,0:T(8,128)}, u32[]{:S(2)}, u32[]{:S(2)}) async-start(f32[32,64,128]{2,1,0:T(8,128)} %pack_sent.1.send), calls=%async_computation | async-start | bytes 2097152 | tf_op jit(solution)/shard_map/all_to_all | solution.py:460
  14.1 0.0 copy-start
  14.1 0.0 copy-start.5
  14.1 0.0 copy-start.6
  14.1 0.0 copy-done.1
  14.1 0.0 copy-done.3
  14.2 0.0 copy-done.4
  14.2 0.0 copy-done.7
  14.2 2.0 %pack_local.1.local = f32[32,64,128]{2,1,0:T(8,128)S(1)} custom-call(s32[256]{0:T(256)S(1)} %copy-done.7, f32[9,32768]{1,0:T(8,128)S(1)} %copy-done.1, s32[256,128]{1,0:T(8,128)S(1)} %bitcast.7, f32[256,128]{1,0:T(8,128)S(1)} %bitcast.8), custom_call_target="tpu_custom_call" | custom-call | flops 10000000 | bytes 4000000 | tf_op jit(solution)/shard_map/pack_local/pallas_call | solution.py:428
  16.2 0.0 copy-done
  16.2 0.0 copy-done.5
  16.2 0.0 copy-done.6
  16.2 4.7 %first.1 = (f32[32,7,8,128]{3,2,1,0:T(8,128)S(1)}, s32[272,128]{1,0:T(8,128)S(1)}, f32[272,128]{1,0:T(8,128)S(1)}, f32[272,128]{1,0:T(8,128)S(1)}, f32[272,128]{...) custom-call(s32[256]{0:T(256)S(1)} %copy-done.7, ...), custom_call_target="tpu_custom_call" | custom-call | flops 10000000 | bytes 4000000 | tf_op jit(solution)/shard_map/first/pallas_call | solution.py:461
  20.9 10.4 %all-to-all-done.arrived = f32[32,64,128]{2,1,0:T(8,128)} async-done(((f32[32,64,128]{2,1,0:T(8,128)}), f32[32,64,128]{2,1,0:T(8,128)}, u32[]{:S(2)}, u32[]{:S(2)}) %all-to-all-start) | async-done | bytes 1048608 | tf_op jit(solution)/shard_map/all_to_all | solution.py:460
  31.3 5.0 %second.1 = (f32[32,6,8,128]{3,2,1,0:T(8,128)S(1)}, s32[272,128]{1,0:T(8,128)S(1)}, f32[272,128]{1,0:T(8,128)S(1)}, f32[272,128]{1,0:T(8,128)S(1)}, f32[272,128]...) custom-call(f32[32,64,128]{2,1,0:T(8,128)} %all-to-all-done.arrived, ...), custom_call_target="tpu_custom_call" | custom-call | flops 10000000 | bytes 4000000 | tf_op jit(solution)/shard_map/second/pallas_call | solution.py:472
  36.4 15.1 %all_to_all.25.refs_12_ = f32[32,4,8,128]{3,2,1,0:T(8,128)S(1)} all-to-all(f32[32,4,8,128]{3,2,1,0:T(8,128)S(1)} %get-tuple-element.54), channel_id=1, replica_groups=mesh['owner'=32,'sub'=4] {'owner'}, dimensions={0} | all-to-all | bytes 1048576 | tf_op jit(solution)/shard_map/all_to_all | solution.py:487
  51.4 5.0 %apply.4 = (f32[96,128]{1,0:T(8,128)S(1)}, f32[552,128]{1,0:T(8,128)S(1)}, f32[552,128]{1,0:T(8,128)S(1)}, f32[69,7,8,128]{3,2,1,0:T(8,128)S(1)}, s32[552,128]{1,0:T(8,128)S(1)}, /*index=5*/s32[65]{0:T(128)S(1)}) custom-call(s32[33]{0:T(128)S(1)} %get-tuple-element.39.refs_0_, s32[33]{0:T(128)S(1)} %get-tuple-element.43.refs_1_, ...), custom_call_target="tpu_custom_call" | custom-call | flops 10000000 | bytes 4000000 | tf_op jit(solution)/shard_map/apply/pallas_call | solution.py:489
  56.5 2.1 %collective-permute-start.2 = (f32[96,128]{1,0:T(8,128)S(1)}, f32[96,128]{1,0:T(8,128)S(1)}, u32[]{:S(2)}, u32[]{:S(2)}) collective-permute-start(f32[96,128]{1,0:T(8,128)S(1)} %get-tuple-element.56.j0), channel_id=1, source_target_pairs={{0,2},{1,3},{2,0},{3,1},{4,6},{5,7},{6,4},{7,5},{8,10},{9,11},{10,... | collective-permute-start | bytes 147464 | tf_op jit(solution)/shard_map/ppermute | solution.py:507
  58.6 0.9 collective-permute-start.1
  59.5 0.3 collective-permute-start
  59.8 1.9 %collective-permute-done.2.j2 = f32[96,128]{1,0:T(8,128)S(1)} collective-permute-done((f32[96,128]{1,0:T(8,128)S(1)}, f32[96,128]{1,0:T(8,128)S(1)}, u32[]{:S(2)}, u32[]{:S(2)}) %collective-permute-start.2) | collective-permute-done | bytes 49184 | tf_op jit(solution)/shard_map/ppermute | solution.py:507
  61.6 1.1 collective-permute-done.1.j3
  62.8 0.0 collective-permute-done.j1
  62.8 3.2 %gather.3 = (f32[96,128]{1,0:T(8,128)S(1)}, f32[552,128]{1,0:T(8,128)S(1)}, f32[32,2,8,128]{3,2,1,0:T(8,128)S(1)}) custom-call(s32[65]{0:T(128)S(1)} %get-tuple-element.55.meta.refs_0_, f32[96,128]{1,0:T(8,128)S(1)} %get-tuple-element.41.vel, f32[64,128]{1,0:T(8,128)S(1)} %get-tuple-element.42.prop, f32[96,128]{1,0:T(8,128)S(1)} %get-tuple-element.56.j0, ...), custom_call_target="tpu_custom_call" | custom-call | flops 10000000 | bytes 4000000 | tf_op jit(solution)/shard_map/gather/pallas_call | solution.py:510
  65.9 14.5 %all_to_all.26.refs_6_ = f32[32,2,8,128]{3,2,1,0:T(8,128)S(1)} all-to-all(f32[32,2,8,128]{3,2,1,0:T(8,128)S(1)} %get-tuple-element.63), channel_id=1, replica_groups=mesh['owner'=32,'sub'=4] {'owner'}, dimensions={0} | all-to-all | bytes 524288 | tf_op jit(solution)/shard_map/all_to_all | solution.py:487
  80.4 4.1 %apply.5 = (f32[96,128]{1,0:T(8,128)S(1)}, f32[552,128]{1,0:T(8,128)S(1)}) custom-call(s32[65]{0:T(128)S(1)} %get-tuple-element.55.meta.refs_0_, f32[69,7,8,128]{3,2,1,0:T(8,128)S(1)} %get-tuple-element.57.x.refs_1_, s32[552,128]{1,0:T(8,128)S(1)} %get-tuple-element.58.idx.refs_2_, f32[552,128]{1,0:T(8,128)S(1)} %get-tuple-element.60.refs_3_, ...), custom_call_target="tpu_custom_call" | custom-call | flops 10000000 | bytes 4000000 | tf_op jit(solution)/shard_map/apply/pallas_call | solution.py:499
  84.5 0.9 collective-permute-start.5
  85.4 1.4 collective-permute-start.4
  86.9 0.5 collective-permute-start.3
  87.4 2.5 %collective-permute-done.5.j2 = f32[96,128]{1,0:T(8,128)S(1)} collective-permute-done((f32[96,128]{1,0:T(8,128)S(1)}, f32[96,128]{1,0:T(8,128)S(1)}, u32[]{:S(2)}, u32[]{:S(2)}) %collective-permute-start.5) | collective-permute-done | bytes 49184 | tf_op jit(solution)/shard_map/ppermute | solution.py:507
  89.9 0.6 collective-permute-done.4.j3
  90.4 0.0 collective-permute-done.3.j1
  90.4 3.2 %gather.4 = (f32[96,128]{1,0:T(8,128)S(1)}, f32[552,128]{1,0:T(8,128)S(1)}, f32[32,2,8,128]{3,2,1,0:T(8,128)S(1)}) custom-call(s32[65]{0:T(128)S(1)} %get-tuple-element.55.meta.refs_0_, f32[96,128]{1,0:T(8,128)S(1)} %get-tuple-element.59.vel, f32[64,128]{1,0:T(8,128)S(1)} %get-tuple-element.42.prop, f32[96,128]{1,0:T(8,128)S(1)} %get-tuple-element.64.j0, ...), custom_call_target="tpu_custom_call" | custom-call | flops 10000000 | bytes 4000000 | tf_op jit(solution)/shard_map/gather/pallas_call | solution.py:510
  93.6 13.4 %all_to_all.27.refs_6_ = f32[32,2,8,128]{3,2,1,0:T(8,128)S(1)} all-to-all(f32[32,2,8,128]{3,2,1,0:T(8,128)S(1)} %get-tuple-element.68), channel_id=1, replica_groups=mesh['owner'=32,'sub'=4] {'owner'}, dimensions={0} | all-to-all | bytes 524288 | tf_op jit(solution)/shard_map/all_to_all | solution.py:487
  107.0 4.1 %apply.6 = (f32[96,128]{1,0:T(8,128)S(1)}, f32[552,128]{1,0:T(8,128)S(1)}) custom-call(s32[65]{0:T(128)S(1)} %get-tuple-element.55.meta.refs_0_, f32[69,7,8,128]{3,2,1,0:T(8,128)S(1)} %get-tuple-element.57.x.refs_1_, s32[552,128]{1,0:T(8,128)S(1)} %get-tuple-element.58.idx.refs_2_, f32[552,128]{1,0:T(8,128)S(1)} %get-tuple-element.66.refs_3_, ...), custom_call_target="tpu_custom_call" | custom-call | flops 10000000 | bytes 4000000 | tf_op jit(solution)/shard_map/apply/pallas_call | solution.py:499
  111.2 2.0 %collective-permute-start.8 = (f32[96,128]{1,0:T(8,128)S(1)}, f32[96,128]{1,0:T(8,128)S(1)}, u32[]{:S(2)}, u32[]{:S(2)}) collective-permute-start(f32[96,128]{1,0:T(8,128)S(1)} %get-tuple-element.69.j0), channel_id=1, source_target_pairs={{0,2},{1,3},{2,0},{3,1},{4,6},{5,7},{6,4},{7,5},{8,10},{9,11},{10,... | collective-permute-start | bytes 147464 | tf_op jit(solution)/shard_map/ppermute | solution.py:507
  113.1 0.4 collective-permute-start.7
  113.5 0.5 collective-permute-start.6
  114.0 2.5 %collective-permute-done.8.j2 = f32[96,128]{1,0:T(8,128)S(1)} collective-permute-done((f32[96,128]{1,0:T(8,128)S(1)}, f32[96,128]{1,0:T(8,128)S(1)}, u32[]{:S(2)}, u32[]{:S(2)}) %collective-permute-start.8) | collective-permute-done | bytes 49184 | tf_op jit(solution)/shard_map/ppermute | solution.py:507
  116.5 0.8 collective-permute-done.7.j3
  117.3 0.0 collective-permute-done.6.j1
  117.3 3.2 %gather.5 = (f32[96,128]{1,0:T(8,128)S(1)}, f32[552,128]{1,0:T(8,128)S(1)}, f32[32,2,8,128]{3,2,1,0:T(8,128)S(1)}) custom-call(s32[65]{0:T(128)S(1)} %get-tuple-element.55.meta.refs_0_, f32[96,128]{1,0:T(8,128)S(1)} %get-tuple-element.65.vel, f32[64,128]{1,0:T(8,128)S(1)} %get-tuple-element.42.prop, f32[96,128]{1,0:T(8,128)S(1)} %get-tuple-element.69.j0, ...), custom_call_target="tpu_custom_call" | custom-call | flops 10000000 | bytes 4000000 | tf_op jit(solution)/shard_map/gather/pallas_call | solution.py:510
  120.5 0.0 copy-start.2
  120.5 14.4 %all_to_all.28.refs_6_ = f32[32,2,8,128]{3,2,1,0:T(8,128)S(1)} all-to-all(f32[32,2,8,128]{3,2,1,0:T(8,128)S(1)} %get-tuple-element.73), channel_id=1, replica_groups=mesh['owner'=32,'sub'=4] {'owner'}, dimensions={0} | all-to-all | bytes 524288 | tf_op jit(solution)/shard_map/all_to_all | solution.py:487
  134.9 4.1 %apply.7 = (f32[96,128]{1,0:T(8,128)S(1)}, f32[552,128]{1,0:T(8,128)S(1)}) custom-call(s32[65]{0:T(128)S(1)} %get-tuple-element.55.meta.refs_0_, f32[69,7,8,128]{3,2,1,0:T(8,128)S(1)} %get-tuple-element.57.x.refs_1_, s32[552,128]{1,0:T(8,128)S(1)} %get-tuple-element.58.idx.refs_2_, f32[552,128]{1,0:T(8,128)S(1)} %get-tuple-element.71.refs_3_, ...), custom_call_target="tpu_custom_call" | custom-call | flops 10000000 | bytes 4000000 | tf_op jit(solution)/shard_map/apply/pallas_call | solution.py:499
  139.0 1.1 collective-permute-start.11
  140.1 1.3 collective-permute-start.10
  141.4 0.5 collective-permute-start.9
  141.8 0.0 copy-done.2
  141.8 2.4 %unpack.1 = f32[256,128]{1,0:T(8,128)} custom-call(s32[256]{0:T(256)S(1)} %copy-done.7, s32[65]{0:T(128)S(1)} %get-tuple-element.55.meta.refs_0_, f32[552,128]{1,0:T(8,128)S(1)} %get-tuple-element.75.imp, f32[256,128]{1,0:T(8,128)S(1)} %bitcast.6), custom_call_target="tpu_custom_call" | custom-call | flops 10000000 | bytes 4000000 | tf_op jit(solution)/shard_map/unpack/pallas_call | solution.py:517
  144.2 0.1 collective-permute-done.11.j2
  144.3 0.2 collective-permute-done.10.j3
  144.6 0.0 collective-permute-done.9.j1
  144.6 0.7 final.1
Async XLA Ops:
  0.6 13.5 %copy-start.1 = (f32[9,32768]{1,0:T(8,128)S(1)}, f32[9,32768]{1,0:T(8,128)}, u32[]{:S(2)}) copy-start(f32[9,32768]{1,0:T(8,128)} %geom.3) | copy-start | bytes 3538948
  0.6 13.5 %copy-start.3 = (s32[32768]{0:T(1024)S(1)}, s32[32768]{0:T(1024)}, u32[]{:S(2)}) copy-start(s32[32768]{0:T(1024)} %param.10) | copy-start | bytes 393220
  0.7 13.5 %copy-start.4 = (f32[32768]{0:T(1024)S(1)}, f32[32768]{0:T(1024)}, u32[]{:S(2)}) copy-start(f32[32768]{0:T(1024)} %param.13) | copy-start | bytes 393220
  0.7 13.5 %copy-start.7 = (s32[256]{0:T(256)S(1)}, s32[256]{0:T(256)}, u32[]{:S(2)}) copy-start(s32[256]{0:T(256)} %live.7) | copy-start | bytes 3076
  4.4 26.9 %all-to-all-start = ((f32[32,64,128]{2,1,0:T(8,128)}), f32[32,64,128]{2,1,0:T(8,128)}, u32[]{:S(2)}, u32[]{:S(2)}) async-start(f32[32,64,128]{2,1,0:T(8,128)} %pack_sent.1.send), calls=%async_computation | async-start | bytes 2097152 | tf_op jit(solution)/shard_map/all_to_all | solution.py:460
  14.1 2.1 %copy-start = (f32[32,64,128]{2,1,0:T(8,128)S(1)}, f32[32,64,128]{2,1,0:T(8,128)}, u32[]{:S(2)}) copy-start(f32[32,64,128]{2,1,0:T(8,128)} %pack_sent.1.send) | copy-start | bytes 3145732
  14.1 2.1 %copy-start.5 = (f32[6,2048]{1,0:T(8,128)S(1)}, f32[6,2048]{1,0:T(8,128)}, u32[]{:S(2)}) copy-start(f32[6,2048]{1,0:T(8,128)} %velocity.1) | copy-start | bytes 147460
  14.1 2.1 %copy-start.6 = (f32[4,2048]{1,0:T(4,128)S(1)}, f32[4,2048]{1,0:T(4,128)}, u32[]{:S(2)}) copy-start(f32[4,2048]{1,0:T(4,128)} %properties.1) | copy-start | bytes 98308
  56.5 5.2 %collective-permute-start.2 = (f32[96,128]{1,0:T(8,128)S(1)}, f32[96,128]{1,0:T(8,128)S(1)}, u32[]{:S(2)}, u32[]{:S(2)}) collective-permute-start(f32[96,128]{1,0:T(8,128)S(1)} %get-tuple-element.56.j0), channel_id=1, source_target_pairs={{0,2},{1,3},{2,0},{3,1},{4,6},{5,7},{6,4},{7,5},{8,10},{9,11},{10,... | collective-permute-start | bytes 147464 | tf_op jit(solution)/shard_map/ppermute | solution.py:507
  58.6 4.2 %collective-permute-start.1 = (f32[96,128]{1,0:T(8,128)S(1)}, f32[96,128]{1,0:T(8,128)S(1)}, u32[]{:S(2)}, u32[]{:S(2)}) collective-permute-start(f32[96,128]{1,0:T(8,128)S(1)} %get-tuple-element.56.j0), channel_id=1, source_target_pairs={{0,3},{1,2},{2,1},{3,0},{4,7},{5,6},{6,5},{7,4},{8,11},{9,10},{10,... | collective-permute-start | bytes 147464 | tf_op jit(solution)/shard_map/ppermute | solution.py:507
  59.5 3.3 %collective-permute-start = (f32[96,128]{1,0:T(8,128)S(1)}, f32[96,128]{1,0:T(8,128)S(1)}, u32[]{:S(2)}, u32[]{:S(2)}) collective-permute-start(f32[96,128]{1,0:T(8,128)S(1)} %get-tuple-element.56.j0), channel_id=1, source_target_pairs={{0,1},{1,0},{2,3},{3,2},{4,5},{5,4},{6,7},{7,6},{8,9},{9,8},{10,11... | collective-permute-start | bytes 147464 | tf_op jit(solution)/shard_map/ppermute | solution.py:507
  84.5 5.3 %collective-permute-start.5 = (f32[96,128]{1,0:T(8,128)S(1)}, f32[96,128]{1,0:T(8,128)S(1)}, u32[]{:S(2)}, u32[]{:S(2)}) collective-permute-start(f32[96,128]{1,0:T(8,128)S(1)} %get-tuple-element.64.j0), channel_id=1, source_target_pairs={{0,2},{1,3},{2,0},{3,1},{4,6},{5,7},{6,4},{7,5},{8,10},{9,11},{10,... | collective-permute-start | bytes 147464 | tf_op jit(solution)/shard_map/ppermute | solution.py:507
  85.4 5.0 %collective-permute-start.4 = (f32[96,128]{1,0:T(8,128)S(1)}, f32[96,128]{1,0:T(8,128)S(1)}, u32[]{:S(2)}, u32[]{:S(2)}) collective-permute-start(f32[96,128]{1,0:T(8,128)S(1)} %get-tuple-element.64.j0), channel_id=1, source_target_pairs={{0,3},{1,2},{2,1},{3,0},{4,7},{5,6},{6,5},{7,4},{8,11},{9,10},{10,... | collective-permute-start | bytes 147464 | tf_op jit(solution)/shard_map/ppermute | solution.py:507
  86.9 3.6 %collective-permute-start.3 = (f32[96,128]{1,0:T(8,128)S(1)}, f32[96,128]{1,0:T(8,128)S(1)}, u32[]{:S(2)}, u32[]{:S(2)}) collective-permute-start(f32[96,128]{1,0:T(8,128)S(1)} %get-tuple-element.64.j0), channel_id=1, source_target_pairs={{0,1},{1,0},{2,3},{3,2},{4,5},{5,4},{6,7},{7,6},{8,9},{9,8},{10,11... | collective-permute-start | bytes 147464 | tf_op jit(solution)/shard_map/ppermute | solution.py:507
  111.2 5.3 %collective-permute-start.8 = (f32[96,128]{1,0:T(8,128)S(1)}, f32[96,128]{1,0:T(8,128)S(1)}, u32[]{:S(2)}, u32[]{:S(2)}) collective-permute-start(f32[96,128]{1,0:T(8,128)S(1)} %get-tuple-element.69.j0), channel_id=1, source_target_pairs={{0,2},{1,3},{2,0},{3,1},{4,6},{5,7},{6,4},{7,5},{8,10},{9,11},{10,... | collective-permute-start | bytes 147464 | tf_op jit(solution)/shard_map/ppermute | solution.py:507
  113.1 4.2 %collective-permute-start.7 = (f32[96,128]{1,0:T(8,128)S(1)}, f32[96,128]{1,0:T(8,128)S(1)}, u32[]{:S(2)}, u32[]{:S(2)}) collective-permute-start(f32[96,128]{1,0:T(8,128)S(1)} %get-tuple-element.69.j0), channel_id=1, source_target_pairs={{0,3},{1,2},{2,1},{3,0},{4,7},{5,6},{6,5},{7,4},{8,11},{9,10},{10,... | collective-permute-start | bytes 147464 | tf_op jit(solution)/shard_map/ppermute | solution.py:507
  113.5 3.8 %collective-permute-start.6 = (f32[96,128]{1,0:T(8,128)S(1)}, f32[96,128]{1,0:T(8,128)S(1)}, u32[]{:S(2)}, u32[]{:S(2)}) collective-permute-start(f32[96,128]{1,0:T(8,128)S(1)} %get-tuple-element.69.j0), channel_id=1, source_target_pairs={{0,1},{1,0},{2,3},{3,2},{4,5},{5,4},{6,7},{7,6},{8,9},{9,8},{10,11... | collective-permute-start | bytes 147464 | tf_op jit(solution)/shard_map/ppermute | solution.py:507
  120.5 21.4 %copy-start.2 = (f32[32768]{0:T(1024)S(1)}, f32[32768]{0:T(1024)}, u32[]{:S(2)}) copy-start(f32[32768]{0:T(1024)} %param.14) | copy-start | bytes 393220
  139.0 5.3 %collective-permute-start.11 = (f32[96,128]{1,0:T(8,128)S(1)}, f32[96,128]{1,0:T(8,128)S(1)}, u32[]{:S(2)}, u32[]{:S(2)}) collective-permute-start(f32[96,128]{1,0:T(8,128)S(1)} %get-tuple-element.74.j0), channel_id=1, source_target_pairs={{0,2},{1,3},{2,0},{3,1},{4,6},{5,7},{6,4},{7,5},{8,10},{9,11},{10,... | collective-permute-start | bytes 147464 | tf_op jit(solution)/shard_map/ppermute | solution.py:507
  140.1 4.5 %collective-permute-start.10 = (f32[96,128]{1,0:T(8,128)S(1)}, f32[96,128]{1,0:T(8,128)S(1)}, u32[]{:S(2)}, u32[]{:S(2)}) collective-permute-start(f32[96,128]{1,0:T(8,128)S(1)} %get-tuple-element.74.j0), channel_id=1, source_target_pairs={{0,3},{1,2},{2,1},{3,0},{4,7},{5,6},{6,5},{7,4},{8,11},{9,10},{10,... | collective-permute-start | bytes 147464 | tf_op jit(solution)/shard_map/ppermute | solution.py:507
  141.4 3.2 %collective-permute-start.9 = (f32[96,128]{1,0:T(8,128)S(1)}, f32[96,128]{1,0:T(8,128)S(1)}, u32[]{:S(2)}, u32[]{:S(2)}) collective-permute-start(f32[96,128]{1,0:T(8,128)S(1)} %get-tuple-element.74.j0), channel_id=1, source_target_pairs={{0,1},{1,0},{2,3},{3,2},{4,5},{5,4},{6,7},{7,6},{8,9},{9,8},{10,11... | collective-permute-start | bytes 147464 | tf_op jit(solution)/shard_map/ppermute | solution.py:507
